TPU v7x, 32 devices: a whole 2x2x4 slice. The times are simulated.
32 devices in a mesh: dp: 8 (over z, y), expert: 4 (over x, core).
Axes of the slice: x: 2, y: 2, z: 4, core: 2. Of those that a mesh axis runs over, the one named last changes fastest.
Arguments:
- tokens: bfloat16 [4, 1024, 1536], P('expert', 'dp'), may hold values from -6 to 6
- cotangent: bfloat16 [4, 1024, 1536], P('expert', 'dp'), may hold values from -6 to 6
- lengths: int32 [4, 2], P('expert'), may hold values from 341 to 683, as said below
- deal: int32 [4], replicated, may hold values from 0 to 3, each once
- routes: int32 [4, 1024, 8], P('expert', 'dp'), may hold values from 0 to 39, all different within a row; in each aligned block of 128 rows (0 to 127, 128 to 255, ..., all dimensions but the last counted through in order) at most 40 rows name the same one
- gates: float32 [4, 1024, 8], P('expert', 'dp'), may hold values from 0.15 to 0.5
- q_weight: float32 [1536, 1536], P(('dp', 'expert')), may hold values from -0.625 to 0.625
- k_weight: float32 [1536, 512], P(('dp', 'expert')), may hold values from -0.625 to 0.625
- v_weight: float32 [1536, 512], P(('dp', 'expert')), may hold values from -0.15625 to 0.15625
- o_weight: float32 [1536, 1536], P(('dp', 'expert')), may hold values from -1.5 to 1.5
- gain_attn: float32 [1536], P(('dp', 'expert')), may hold values from 0.5 to 1.5
- gain_moe: float32 [1536], P(('dp', 'expert')), may hold values from 0.5 to 1.5
- in_weight: float32 [1536, 40, 1024], P('dp', 'expert'), may hold values from -0.15625 to 0.15625
- down_weight: float32 [512, 40, 1536], P('dp', 'expert'), may hold values from -1 to 1
Outputs:
- output: float32 [4, 1024, 1536], P('expert', 'dp')
- input_grad: float32 [4, 1024, 1536], P('expert', 'dp')
- q_weight_grad: float32 [1536, 1536], P(('dp', 'expert'))
- k_weight_grad: float32 [1536, 512], P(('dp', 'expert'))
- v_weight_grad: float32 [1536, 512], P(('dp', 'expert'))
- o_weight_grad: float32 [1536, 1536], P(('dp', 'expert'))
- gain_attn_grad: float32 [1536], P(('dp', 'expert'))
- gain_moe_grad: float32 [1536], P(('dp', 'expert'))
- in_weight_grad: float32 [1536, 40, 1024], P('dp', 'expert')
- down_weight_grad: float32 [512, 40, 1536], P('dp', 'expert')
Inputs may be any that keep to these rules, and one draw needn't show every extreme that they name: In each group the lengths of sequences 2i and 2i + 1 sum to 1024; in some group a sequence has the largest length. `routes`: each token names 8 different experts; in the rows of one device no expert is named by more than 40 rows.
All inputs are finite; a program needn't handle non-finite values.
Results may differ from a plain program's by a relative error of at most 0.018.
The roundings to bfloat16 on the way count: a program that leaves them out, or rounds other values in their place, can miss the bound.
Values may be sent and summed in bfloat16 or wider, within the bound.
No kernel may reach another device: no remote copies, remote signals or barrier semaphores. Data moves between devices by JAX's collectives and lax.ppermute only.
A program may use at most 256 MiB of HBM per device.

v0:
```python
import functools

import jax
import jax.numpy as jnp
from jax import lax
from jax.experimental import pallas as pl
from jax.experimental.pallas import tpu as pltpu
from jax.sharding import PartitionSpec as P


H = 24
KVH = 8
HD = 64
E = 40
FF = 512
TOPK = 8
CAP = 40


EPSILON = 1e-06
RESIDUAL = 0.22
SCORE_SCALE = 0.015625
THETA = 10000.0
NEGATIVE = -1e30
ROWS_DIMS = (((0,), (0,)), ((), ()))
COLS_DIMS = (((1,), (1,)), ((), ()))


def rms_scale(values, gain):
    return values * lax.rsqrt(jnp.mean(values * values, axis=-1, keepdims=True) + EPSILON) * gain


def rotate(values, cosine, sine_table):
    half_width = values.shape[-1] // 2
    turned = jnp.concatenate([-values[..., half_width:], values[..., :half_width]], axis=-1)
    return values * cosine + turned * sine_table


def turn_back(grads_in, cosine, sine_table):
    half_width = grads_in.shape[-1] // 2
    scaled = grads_in * sine_table
    return grads_in * cosine + jnp.concatenate(
        [scaled[..., half_width:], -scaled[..., :half_width]], axis=-1
    )


def silu_product(gate_in, up_in):
    return jax.nn.silu(gate_in) * up_in


def locate(where_at, seq_ends):
    return jnp.sum((where_at[:, None] >= seq_ends[None, :]).astype(jnp.int32), axis=-1)


def cut_block(source, begin_at, block_rows, heads):
    piece = lax.dynamic_slice_in_dim(source, begin_at, block_rows, 0)
    return piece.reshape(block_rows, heads, source.shape[1] // heads)


def group_chooser(wanted, carried, pieces, start):
    piece_rows = pieces[0].shape[0]
    inside = (wanted >= start) & (wanted < start + piece_rows)
    offset_at = jnp.clip(wanted, 0, piece_rows - 1)
    return tuple(
        (
            jnp.where(inside, lax.dynamic_slice_in_dim(member_piece, offset_at, 1, 0), member_carry)
            for member_piece, member_carry in zip(pieces, carried)
        )
    )


def per_device_wide(
    tokens,
    cotangent,
    lengths,
    deal,
    routes,
    gates,
    q_weight,
    k_weight,
    v_weight,
    o_weight,
    gain_attn,
    gain_moe,
    in_weight,
    down_weight,
):
    tok_rows = tokens.shape[1]
    model_width = tokens.shape[2]
    group_rows = tok_rows * lax.axis_size("dp")
    block_rows = min(512, group_rows)
    heads_per = H // KVH
    owner_index = lax.axis_index("expert")
    group_ids = jnp.arange(deal.shape[0], dtype=jnp.int32)
    wanted_in = jnp.sum(jnp.where(group_ids == owner_index, deal, 0))
    wanted_out = jnp.sum(jnp.where(deal == owner_index, group_ids, 0))
    dealt_tokens, dealt_cotangent = group_chooser(
        wanted_in,
        (jnp.zeros_like(tokens), jnp.zeros_like(cotangent)),
        (
            lax.all_gather(tokens, "expert", axis=0, tiled=True),
            lax.all_gather(cotangent, "expert", axis=0, tiled=True),
        ),
        jnp.int32(0),
    )
    inputs = dealt_tokens[0].astype(jnp.float32)
    q_full, k_full, v_full, o_full, gain_one, gain_two = (
        lax.all_gather(q_weight.astype(jnp.bfloat16), ("dp", "expert"), axis=0, tiled=True),
        lax.all_gather(k_weight.astype(jnp.bfloat16), ("dp", "expert"), axis=0, tiled=True),
        lax.all_gather(v_weight.astype(jnp.bfloat16), ("dp", "expert"), axis=0, tiled=True),
        lax.all_gather(o_weight.astype(jnp.bfloat16), ("dp", "expert"), axis=0, tiled=True),
        lax.all_gather(gain_attn.astype(jnp.bfloat16), ("dp", "expert"), axis=0, tiled=True),
        lax.all_gather(gain_moe.astype(jnp.bfloat16), ("dp", "expert"), axis=0, tiled=True),
    )
    gain_one = gain_one.astype(jnp.float32)
    gain_two = gain_two.astype(jnp.float32)
    seq_lengths = lengths[0]
    seq_ends = jnp.cumsum(seq_lengths)
    seq_starts = seq_ends - seq_lengths
    first_place = lax.axis_index("dp") * tok_rows
    places = first_place + jnp.arange(tok_rows, dtype=jnp.int32)
    member = (places[:, None] >= seq_starts[None, :]) & (places[:, None] < seq_ends[None, :])
    offsets = jnp.sum(jnp.where(member, places[:, None] - seq_starts[None, :], 0), axis=-1)
    frequency = THETA ** (-jnp.arange(HD // 2, dtype=jnp.float32) * 2.0 / HD)
    angles = offsets.astype(jnp.float32)[:, None] * frequency[None, :]
    angles = jnp.concatenate([angles, angles], axis=-1)[:, None, :]
    cosine = jnp.cos(angles)
    sine_table = jnp.sin(angles)
    query_seq = locate(places, seq_ends)
    seq_floor = jnp.sum(jnp.where(member[0], seq_starts, 0))
    low_block = seq_floor // block_rows
    high_block = (first_place + tok_rows - 1) // block_rows + 1
    normed = rms_scale(inputs, gain_one).astype(jnp.bfloat16)
    query_pre = jnp.dot(normed, q_full, preferred_element_type=jnp.float32).reshape(tok_rows, H, HD)
    key_pre = jnp.dot(normed, k_full, preferred_element_type=jnp.float32).reshape(tok_rows, KVH, HD)
    value_rows = jnp.dot(normed, v_full, preferred_element_type=jnp.float32).astype(jnp.bfloat16)
    queries = (
        rotate(query_pre, cosine, sine_table)
        .astype(jnp.bfloat16)
        .reshape(tok_rows, KVH, heads_per, HD)
    )
    key_rows = rotate(key_pre, cosine, sine_table).astype(jnp.bfloat16).reshape(tok_rows, KVH * HD)
    all_keys, all_values = (
        lax.all_gather(key_rows, "dp", axis=0, tiled=True),
        lax.all_gather(value_rows, "dp", axis=0, tiled=True),
    )

    def scores_for(block_id, key_block):
        begin_at = block_id * block_rows
        key_places = begin_at + jnp.arange(block_rows, dtype=jnp.int32)
        allowed = (query_seq[:, None] == locate(key_places, seq_ends)[None, :]) & (
            key_places[None, :] <= places[:, None]
        )
        raw_scores = SCORE_SCALE * jnp.einsum(
            "tkgd,skd->kgts", queries, key_block, preferred_element_type=jnp.float32
        )
        return (raw_scores, allowed)

    def stats_step(block_id, carried):
        run_top, run_total = carried
        key_block = cut_block(all_keys, block_id * block_rows, block_rows, KVH)
        raw_scores, allowed = scores_for(block_id, key_block)
        new_top = jnp.maximum(run_top, jnp.max(jnp.where(allowed, raw_scores, NEGATIVE), axis=-1))
        weights_now = jnp.where(allowed, jnp.exp(raw_scores - new_top[..., None]), 0.0)
        run_total = run_total * jnp.exp(run_top - new_top) + jnp.sum(weights_now, axis=-1)
        return (new_top, run_total)

    top_init = jnp.full((KVH, heads_per, tok_rows), NEGATIVE, jnp.float32)
    total_init = jnp.zeros((KVH, heads_per, tok_rows), jnp.float32)
    run_top, run_total = lax.fori_loop(low_block, high_block, stats_step, (top_init, total_init))
    log_total = run_top + jnp.log(run_total)

    def attn_probs(block_id, key_block):
        raw_scores, allowed = scores_for(block_id, key_block)
        return jnp.where(allowed, jnp.exp(raw_scores - log_total[..., None]), 0.0)

    def value_step(block_id, running):
        key_block = cut_block(all_keys, block_id * block_rows, block_rows, KVH)
        value_block = cut_block(all_values, block_id * block_rows, block_rows, KVH)
        chances = attn_probs(block_id, key_block).astype(jnp.bfloat16)
        return running + jnp.einsum(
            "kgts,skd->tkgd", chances, value_block, preferred_element_type=jnp.float32
        )

    mixed_init = jnp.zeros((tok_rows, KVH, heads_per, HD), jnp.float32)
    mixed_rows = lax.fori_loop(low_block, high_block, value_step, mixed_init).reshape(
        tok_rows, H * HD
    )
    mixed_low = mixed_rows.astype(jnp.bfloat16)
    branch = lax.dot_general(mixed_low, o_full, COLS_DIMS, preferred_element_type=jnp.float32)
    middle = inputs + RESIDUAL * branch
    sent_rows = rms_scale(middle, gain_two).astype(jnp.bfloat16)
    route_ids = routes[0].reshape(tok_rows * TOPK)
    matches = (route_ids[:, None] == jnp.arange(E, dtype=jnp.int32)[None, :]).astype(jnp.int32)
    slot_rank = jnp.sum(matches * jnp.cumsum(matches, axis=0), axis=-1) - 1
    slot_index = route_ids * CAP + slot_rank
    copies = jnp.repeat(sent_rows, TOPK, axis=0)
    outgoing = (
        jnp.zeros((E * CAP, model_width), jnp.bfloat16)
        .at[slot_index]
        .set(copies)
        .reshape(E, CAP, model_width)
    )
    arrived = lax.all_to_all(outgoing, "expert", split_axis=0, concat_axis=1, tiled=True)
    w_in, w_down = (
        lax.all_gather(in_weight.astype(jnp.bfloat16), "dp", axis=0, tiled=True),
        lax.all_gather(down_weight.astype(jnp.bfloat16), "dp", axis=0, tiled=True),
    )
    gate_up = jnp.einsum("erd,def->erf", arrived, w_in, preferred_element_type=jnp.float32)
    gate_part = gate_up[..., :FF]
    up_part = gate_up[..., FF:]
    hidden = silu_product(gate_part, up_part).astype(jnp.bfloat16)
    produced = jnp.einsum(
        "erf,fed->erd", hidden, w_down, preferred_element_type=jnp.float32
    ).astype(jnp.bfloat16)
    returned = lax.all_to_all(produced, "expert", split_axis=1, concat_axis=0, tiled=True).reshape(
        E * CAP, model_width
    )
    route_gates = gates[0].reshape(tok_rows * TOPK)
    picked = returned[slot_index].astype(jnp.float32) * route_gates[:, None]
    expert_sum = jnp.sum(picked.reshape(tok_rows, TOPK, model_width), axis=1)
    output = middle + RESIDUAL * expert_sum
    upstream = dealt_cotangent[0].astype(jnp.float32)
    spread = (RESIDUAL * route_gates[:, None] * jnp.repeat(upstream, TOPK, axis=0)).astype(
        jnp.bfloat16
    )
    back_out = (
        jnp.zeros((E * CAP, model_width), jnp.bfloat16)
        .at[slot_index]
        .set(spread)
        .reshape(E, CAP, model_width)
    )
    back_in = lax.all_to_all(back_out, "expert", split_axis=0, concat_axis=1, tiled=True)
    hidden_grad = jnp.einsum("erd,fed->erf", back_in, w_down, preferred_element_type=jnp.float32)
    down_term = jnp.einsum("erf,erd->fed", hidden, back_in, preferred_element_type=jnp.float32)
    ignored, silu_pull = jax.vjp(silu_product, gate_part, up_part)
    gate_grad, up_grad = silu_pull(hidden_grad)
    gate_up_grad = jnp.concatenate([gate_grad, up_grad], axis=-1).astype(jnp.bfloat16)
    in_term = jnp.einsum("erd,erf->def", arrived, gate_up_grad, preferred_element_type=jnp.float32)
    arrived_grad = jnp.einsum(
        "erf,def->erd", gate_up_grad, w_in, preferred_element_type=jnp.float32
    ).astype(jnp.bfloat16)
    sent_back = lax.all_to_all(
        arrived_grad, "expert", split_axis=1, concat_axis=0, tiled=True
    ).reshape(E * CAP, model_width)
    sent_grad = jnp.sum(
        sent_back[slot_index].astype(jnp.float32).reshape(tok_rows, TOPK, model_width), axis=1
    )
    in_grad, down_grad = (
        lax.psum_scatter(
            in_term.astype(jnp.bfloat16), "dp", scatter_dimension=0, tiled=True
        ).astype(jnp.float32),
        lax.psum_scatter(
            down_term.astype(jnp.bfloat16), "dp", scatter_dimension=0, tiled=True
        ).astype(jnp.float32),
    )
    ignored, second_pull = jax.vjp(rms_scale, middle, gain_two)
    middle_part, gain_two_term = second_pull(sent_grad)
    middle_grad = upstream + middle_part
    branch_grad = (RESIDUAL * middle_grad).astype(jnp.bfloat16)
    o_term = lax.dot_general(branch_grad, mixed_low, ROWS_DIMS, preferred_element_type=jnp.float32)
    grad_heads = jnp.dot(branch_grad, o_full, preferred_element_type=jnp.float32).astype(
        jnp.bfloat16
    )
    grad_heads = grad_heads.reshape(tok_rows, KVH, heads_per, HD)

    def delta_step(block_id, running):
        key_block = cut_block(all_keys, block_id * block_rows, block_rows, KVH)
        value_block = cut_block(all_values, block_id * block_rows, block_rows, KVH)
        chances = attn_probs(block_id, key_block)
        prob_grad = jnp.einsum(
            "tkgd,skd->kgts", grad_heads, value_block, preferred_element_type=jnp.float32
        )
        return running + jnp.sum(chances * prob_grad, axis=-1)

    row_delta = lax.fori_loop(
        low_block, high_block, delta_step, jnp.zeros((KVH, heads_per, tok_rows), jnp.float32)
    )

    def grad_step(block_id, carried):
        query_grad, key_buffer, value_buffer = carried
        begin_at = block_id * block_rows
        key_block = cut_block(all_keys, begin_at, block_rows, KVH)
        value_block = cut_block(all_values, begin_at, block_rows, KVH)
        chances = attn_probs(block_id, key_block)
        prob_grad = jnp.einsum(
            "tkgd,skd->kgts", grad_heads, value_block, preferred_element_type=jnp.float32
        )
        score_grad = (chances * (prob_grad - row_delta[..., None])).astype(jnp.bfloat16)
        query_grad = query_grad + SCORE_SCALE * jnp.einsum(
            "kgts,skd->tkgd", score_grad, key_block, preferred_element_type=jnp.float32
        )
        key_part = SCORE_SCALE * jnp.einsum(
            "kgts,tkgd->skd", score_grad, queries, preferred_element_type=jnp.float32
        )
        value_part = jnp.einsum(
            "kgts,tkgd->skd",
            chances.astype(jnp.bfloat16),
            grad_heads,
            preferred_element_type=jnp.float32,
        )
        key_buffer = lax.dynamic_update_slice_in_dim(
            key_buffer, key_part.reshape(block_rows, KVH * HD), begin_at, 0
        )
        value_buffer = lax.dynamic_update_slice_in_dim(
            value_buffer, value_part.reshape(block_rows, KVH * HD), begin_at, 0
        )
        return (query_grad, key_buffer, value_buffer)

    grad_init = (
        jnp.zeros((tok_rows, KVH, heads_per, HD), jnp.float32),
        jnp.zeros((group_rows, KVH * HD), jnp.float32),
        jnp.zeros((group_rows, KVH * HD), jnp.float32),
    )
    query_grad, key_buffer, value_buffer = lax.fori_loop(
        low_block, high_block, grad_step, grad_init
    )
    key_grad, value_grad = (
        lax.psum_scatter(
            key_buffer.astype(jnp.bfloat16), "dp", scatter_dimension=0, tiled=True
        ).astype(jnp.float32),
        lax.psum_scatter(
            value_buffer.astype(jnp.bfloat16), "dp", scatter_dimension=0, tiled=True
        ).astype(jnp.float32),
    )
    query_low = (
        turn_back(query_grad.reshape(tok_rows, H, HD), cosine, sine_table)
        .reshape(tok_rows, H * HD)
        .astype(jnp.bfloat16)
    )
    key_low = (
        turn_back(key_grad.reshape(tok_rows, KVH, HD), cosine, sine_table)
        .reshape(tok_rows, KVH * HD)
        .astype(jnp.bfloat16)
    )
    value_low = value_grad.astype(jnp.bfloat16)
    q_term = lax.dot_general(normed, query_low, ROWS_DIMS, preferred_element_type=jnp.float32)
    k_term = lax.dot_general(normed, key_low, ROWS_DIMS, preferred_element_type=jnp.float32)
    v_term = lax.dot_general(normed, value_low, ROWS_DIMS, preferred_element_type=jnp.float32)
    normed_grad = lax.dot_general(query_low, q_full, COLS_DIMS, preferred_element_type=jnp.float32)
    normed_grad = normed_grad + lax.dot_general(
        key_low, k_full, COLS_DIMS, preferred_element_type=jnp.float32
    )
    normed_grad = normed_grad + lax.dot_general(
        value_low, v_full, COLS_DIMS, preferred_element_type=jnp.float32
    )
    ignored, first_pull = jax.vjp(rms_scale, inputs, gain_one)
    input_part, gain_one_term = first_pull(normed_grad)
    input_grad = middle_grad + input_part
    q_grad, k_grad, v_grad, o_grad, gain_attn_grad, gain_moe_grad = (
        lax.psum_scatter(q_term, ("dp", "expert"), scatter_dimension=0, tiled=True),
        lax.psum_scatter(k_term, ("dp", "expert"), scatter_dimension=0, tiled=True),
        lax.psum_scatter(v_term, ("dp", "expert"), scatter_dimension=0, tiled=True),
        lax.psum_scatter(o_term, ("dp", "expert"), scatter_dimension=0, tiled=True),
        lax.psum_scatter(gain_one_term, ("dp", "expert"), scatter_dimension=0, tiled=True),
        lax.psum_scatter(gain_two_term, ("dp", "expert"), scatter_dimension=0, tiled=True),
    )
    given_output, given_input_grad = group_chooser(
        wanted_out,
        (
            jnp.zeros((1, tok_rows, model_width), jnp.float32),
            jnp.zeros((1, tok_rows, model_width), jnp.float32),
        ),
        (
            lax.all_gather(output[None].astype(jnp.bfloat16), "expert", axis=0, tiled=True).astype(
                jnp.float32
            ),
            lax.all_gather(
                input_grad[None].astype(jnp.bfloat16), "expert", axis=0, tiled=True
            ).astype(jnp.float32),
        ),
        jnp.int32(0),
    )
    return (
        given_output,
        given_input_grad,
        q_grad,
        k_grad,
        v_grad,
        o_grad,
        gain_attn_grad,
        gain_moe_grad,
        in_grad,
        down_grad,
    )


SWAP_Y = [(i, i ^ 1) for i in range(8)]
SWAP_CORE = [(j, j ^ 1) for j in range(4)]
SWAP_X = [(j, j ^ 2) for j in range(4)]


def along_z(moves):
    return [(2 * s + y, 2 * d + y) for s, d in moves for y in range(2)]


Z_NEAR = along_z([(0, 1), (1, 0), (2, 3), (3, 2)])
Z_MIDDLE = along_z([(1, 2), (2, 1)])
Z_OUT = along_z([(1, 0), (2, 3)])
Z_IN = along_z([(0, 1), (3, 2)])
SLOT_Z = ((0, 1, 2, 3), (1, 0, 3, 2), (2, 2, 1, 1), (3, 3, 0, 0))


def over_dp(piece, moves):
    return lax.ppermute(piece, "dp", moves)


def over_expert(piece, moves):
    return lax.ppermute(piece, "expert", moves)


def added(first, *others):
    total = first.astype(jnp.float32)
    for other in others:
        total = total + other.astype(jnp.float32)
    return total.astype(jnp.bfloat16)


def halves(array):
    half = array.shape[0] // 2
    return array[:half], array[half:]


def joined(*arrays):
    return jnp.concatenate(arrays, axis=0)


def one_round(outs, ins, cover=None):
    if cover is None:
        return lax.optimization_barrier(outs), None
    return lax.optimization_barrier((outs, cover(lambda x: after(x, *ins))))


def swap_y(value):
    return over_dp(value, SWAP_Y)


def swap_x(value):
    return over_expert(value, SWAP_X)


def swap_core(value):
    return over_expert(value, SWAP_CORE)


def dp_gather(piece, covers=(None, None, None, None)):
    (near, middle, y0), work1 = one_round(
        (over_dp(piece, Z_NEAR), over_dp(piece, Z_MIDDLE), swap_y(piece)), (piece,), covers[0]
    )
    (far, out1, y1), work2 = one_round(
        (over_dp(near, Z_MIDDLE), over_dp(middle, Z_OUT), swap_y(near)), (near, middle), covers[1]
    )
    third = middle + out1
    (out2, y2), work3 = one_round((over_dp(far, Z_OUT), swap_y(third)), (far, third), covers[2])
    fourth = far + out2
    y3, work4 = one_round(swap_y(fourth), (fourth,), covers[3])
    return joined(piece, y0, near, y1, third, y2, fourth, y3), (work1, work2, work3, work4)


class DpScatter:
    def __init__(self, total):
        blocks = jnp.split(total, 8, axis=0)
        self.own, self.sent = blocks[0::2], blocks[1::2]
        self.round = 0

    def step(self, tie=lambda v: v):
        self.round += 1
        if self.round == 1:
            self.z = swap_y(tie(self.sent[3]))
        elif self.round == 2:
            self.fourth = added(self.own[3], self.z)
            self.z = over_dp(tie(self.fourth), Z_IN), swap_y(self.sent[2])
        elif self.round == 3:
            fourth = added(self.fourth, self.z[0])
            self.third = added(self.own[2], self.z[1])
            self.z = (
                over_dp(tie(fourth), Z_MIDDLE),
                over_dp(self.third, Z_IN),
                swap_y(self.sent[1]),
            )
        else:
            third = added(self.third, self.z[1])
            near = added(self.own[1], self.z[2], self.z[0])
            self.z = (
                over_dp(tie(near), Z_NEAR),
                over_dp(third, Z_MIDDLE),
                swap_y(self.sent[0]),
            )
        return self.z

    def keep(self, values):
        self.z = values

    def total(self):
        total = self.own[0].astype(jnp.float32)
        for value in self.z:
            total = total + value.astype(jnp.float32)
        return total


def gather_beside_sum(piece, project, mix):
    (near, middle), projected = one_round(
        (over_dp(piece, Z_NEAR), over_dp(piece, Z_MIDDLE)), (piece,), project
    )
    (far, out1, y0), (mixed, part) = one_round(
        (over_dp(near, Z_MIDDLE), over_dp(middle, Z_OUT), swap_y(piece)),
        (near, middle),
        lambda tie: mix(tie, projected),
    )
    third = middle + out1
    pair0 = joined(piece, y0)
    total = DpScatter(part)
    (out2, y1, x0, sums), _ = one_round(
        (over_dp(far, Z_OUT), swap_y(near), swap_x(pair0), total.step()), (far, pair0)
    )
    total.keep(sums)
    fourth = far + out2
    pair1 = joined(near, y1)
    (y2, x1, sums), _ = one_round((swap_y(third), swap_x(pair1), total.step()), (third, pair1))
    total.keep(sums)
    pair2 = joined(third, y2)
    (y3, x2, sums), _ = one_round((swap_y(fourth), swap_x(pair2), total.step()), (fourth, pair2))
    total.keep(sums)
    pair3 = joined(fourth, y3)
    (x3, sums), _ = one_round((swap_x(pair3), total.step()), (pair3,))
    total.keep(sums)
    here = joined(pair0, x0, pair1, x1, pair2, x2, pair3, x3)
    return joined(here, swap_core(here)), total.total(), (projected, mixed)


def gather_slots(piece, covers):
    y, x, core = swap_y, swap_x, swap_core
    t0, l0 = halves(piece)
    outs = over_dp(piece, Z_NEAR), over_dp(piece, Z_MIDDLE), y(t0), x(l0)
    (near, middle, yt0, xl0), _ = one_round(outs, (piece,))
    t1, l1 = halves(near)
    top0, low0 = joined(t0, yt0), joined(l0, xl0)
    outs = over_dp(near, Z_MIDDLE), over_dp(middle, Z_OUT), x(top0), y(low0), y(t1), x(l1)
    (far, out1, xt0, yl0, yt1, xl1), work2 = one_round(outs, (top0, low0), covers[0])
    third = middle + out1
    t2, l2 = halves(third)
    top1, low1, here0 = joined(t1, yt1), joined(l1, xl1), joined(top0, xt0, low0, yl0)
    outs = over_dp(far, Z_OUT), x(top1), y(low1), y(t2), x(l2), core(here0)
    (out2, xt1, yl1, yt2, xl2, core0), work3 = one_round(outs, (top1, low1), covers[1])
    fourth = far + out2
    t3, l3 = halves(fourth)
    slot0 = joined(here0, core0)
    top2, low2, here1 = joined(t2, yt2), joined(l2, xl2), joined(top1, xt1, low1, yl1)
    outs = x(top2), y(low2), y(t3), x(l3), core(here1)
    (xt2, yl2, yt3, xl3, core1), work4 = one_round(
        outs, (top2, low2), lambda tie: covers[2](tie, slot0)
    )
    slot1 = joined(here1, core1)
    top3, low3, here2 = joined(t3, yt3), joined(l3, xl3), joined(top2, xt2, low2, yl2)
    outs = x(top3), y(low3), core(here2)
    (xt3, yl3, core2), work5 = one_round(outs, (top3, low3), lambda tie: covers[2](tie, slot1))
    slot2 = joined(here2, core2)
    here3 = joined(top3, xt3, low3, yl3)
    core3, work6 = one_round(core(here3), (here3,), lambda tie: covers[2](tie, slot2))
    slot3 = joined(here3, core3)
    return [slot0, slot1, slot2, slot3], [work4, work5, work6], (work2, work3)


def scatter_slots(totals, covers):
    y, x, core = swap_y, swap_x, swap_core

    def big(here):
        top, low = halves(here)
        (ta, tb), (la, lb) = halves(top), halves(low)
        return (ta, la), (x(tb), y(lb))

    def small(top, low):
        (ta, tb), (la, lb) = halves(top), halves(low)
        return (ta, la), (y(tb), x(lb))

    works = []

    def run(outs, ins, cover):
        outs, work = one_round(outs, ins, cover and (lambda tie: cover(tie, works)))
        works.append(work)
        return outs

    (m0, o0), (m1, o1), (m2, o2), (m3, o3) = [halves(t) for t in totals]
    c3 = run(core(o3), (o3,), covers[0])
    h3 = added(m3, c3)
    k3, b3 = big(h3)
    (b3, c2) = run((b3, core(o2)), (h3,), covers[1])
    p3 = [added(k, v) for k, v in zip(k3, b3)]
    h2 = added(m2, c2)
    k2, b2 = big(h2)
    s3, a3 = small(*p3)
    (a3, b2, c1, c0) = run((a3, b2, core(o1), core(o0)), (h2, *p3), covers[2])
    fourth = joined(*[added(k, v) for k, v in zip(s3, a3)])
    p2 = [added(k, v) for k, v in zip(k2, b2)]
    h1, h0 = added(m1, c1), added(m0, c0)
    k1, b1 = big(h1)
    s2, a2 = small(*p2)
    (z3, a2, b1) = run(
        (over_dp(fourth, Z_IN), a2, b1), (fourth, h1, *p2), covers[3]
    )
    fourth = added(fourth, z3)
    third = joined(*[added(k, v) for k, v in zip(s2, a2)])
    p1 = [added(k, v) for k, v in zip(k1, b1)]
    k0, b0 = big(h0)
    s1, a1 = small(*p1)
    (z3, z2, a1, b0) = run(
        (over_dp(fourth, Z_MIDDLE), over_dp(third, Z_IN), a1, b0), (fourth, third, *p1), covers[4]
    )
    third = added(third, z2)
    near = added(joined(*[added(k, v) for k, v in zip(s1, a1)]), z3)
    p0 = [added(k, v) for k, v in zip(k0, b0)]
    s0, a0 = small(*p0)
    (z1, z2, a0) = run(
        (over_dp(near, Z_NEAR), over_dp(third, Z_MIDDLE), a0), (near, third, *p0), covers[5]
    )
    own = joined(*[added(k, v) for k, v in zip(s0, a0)])
    total = own.astype(jnp.float32) + z1.astype(jnp.float32) + z2.astype(jnp.float32)
    return total, works


def far_order(ex_index, dealt_of):
    r = jnp.arange(64, dtype=jnp.int32)
    slot, core, half, outer, inner = r // 16, r // 8 % 2, r // 4 % 2, r // 2 % 2, r % 2
    flip_y = jnp.where(half == 0, inner, outer)
    flip_x = jnp.where(half == 0, outer, inner)

    def place(flip):
        return ((flip % 2 * 4 + slot) * 4 + flip // 2 * 2 + flip_y) * 2 + half

    flip = 2 * flip_x + core
    return place(flip), place(jnp.take(dealt_of, ex_index ^ flip) ^ ex_index)


def take_kernel(index_ref, *refs, at_once):
    count = len(refs) // (at_once + 1)
    for p in range(count):
        target = refs[count * at_once + p]
        rows = target.shape[0] // at_once
        for k in range(at_once):
            target[k * rows : (k + 1) * rows, :] = refs[p * at_once + k][...]


def take_blocks(index, array, parts, block):
    at_once = 8
    steps = index.shape[1] // at_once

    def source(row, column, k):
        return lambda i, idx: (idx[row, at_once * i + k], column)

    return pl.pallas_call(
        functools.partial(take_kernel, at_once=at_once),
        out_shape=[
            jax.ShapeDtypeStruct((index.shape[1] * block, width), array.dtype)
            for row, column, width in parts
        ],
        grid_spec=pltpu.PrefetchScalarGridSpec(
            num_scalar_prefetch=1,
            grid=(steps,),
            in_specs=[
                pl.BlockSpec((block, width), source(row, column, k))
                for row, column, width in parts
                for k in range(at_once)
            ],
            out_specs=[
                pl.BlockSpec((at_once * block, width), lambda i, idx: (i, 0))
                for row, column, width in parts
            ],
        ),
        name="take_blocks",
    )(index, *([array] * (at_once * len(parts))))


def attend_masks(row_ids, col_ids, begin, rows):
    seq_rows = row_ids[pl.ds(begin, rows), 0:1]
    place_rows = row_ids[pl.ds(begin, rows), 1:2]
    return (seq_rows == col_ids[0:1, :]) & (col_ids[1:2, :] <= place_rows)


def attend_kernel(q_ref, k_ref, v_ref, row_ids, col_ids, o_ref, top_ref, total_ref, *, heads, rows):
    for kv in range(k_ref.shape[1] // HD):
        keys = k_ref[:, kv * HD : (kv + 1) * HD]
        vals = v_ref[:, kv * HD : (kv + 1) * HD]

        def step(i, carry):
            begin = pl.multiple_of(i * rows, rows)
            allowed = attend_masks(row_ids, col_ids, begin, rows)
            outs, tops, totals = [], [], []
            for h in range(heads):
                at = (kv * heads + h) * HD
                scores = SCORE_SCALE * lax.dot_general(
                    q_ref[pl.ds(begin, rows), at : at + HD],
                    keys,
                    COLS_DIMS,
                    preferred_element_type=jnp.float32,
                )
                scores = jnp.where(allowed, scores, NEGATIVE)
                top = jnp.max(scores, axis=-1, keepdims=True)
                weights = jnp.exp(scores - top)
                total = jnp.sum(weights, axis=-1, keepdims=True)
                chances = (weights / total).astype(jnp.bfloat16)
                outs.append(jnp.dot(chances, vals, preferred_element_type=jnp.float32))
                tops.append(top)
                totals.append(total)
            begin_at = kv * heads
            o_ref[pl.ds(begin, rows), begin_at * HD : (begin_at + heads) * HD] = jnp.concatenate(
                outs, axis=1
            ).astype(jnp.bfloat16)
            top_ref[pl.ds(begin, rows), begin_at : begin_at + heads] = jnp.concatenate(tops, axis=1)
            total_ref[pl.ds(begin, rows), begin_at : begin_at + heads] = jnp.concatenate(
                totals, axis=1
            )
            return carry

        lax.fori_loop(0, q_ref.shape[0] // rows, step, 0)


def attend(queries, keys, vals, row_ids, col_ids):
    rows = queries.shape[0]
    heads = queries.shape[1] // HD
    return pl.pallas_call(
        functools.partial(attend_kernel, heads=H // KVH, rows=min(256, rows)),
        out_shape=[
            jax.ShapeDtypeStruct(queries.shape, jnp.bfloat16),
            jax.ShapeDtypeStruct((rows, heads), jnp.float32),
            jax.ShapeDtypeStruct((rows, heads), jnp.float32),
        ],
        name="attend",
    )(queries, keys, vals, row_ids, col_ids)


def attend_back_kernel(
    q_ref, k_ref, v_ref, g_ref, top_ref, total_ref, row_ids, col_ids, dq_ref, dk_ref, dv_ref, *, heads, rows
):
    dk_ref[...] = jnp.zeros_like(dk_ref)
    dv_ref[...] = jnp.zeros_like(dv_ref)
    for kv in range(k_ref.shape[1] // HD):
        cols = slice(kv * HD, (kv + 1) * HD)
        keys = k_ref[:, cols]
        vals = v_ref[:, cols]

        def step(i, carry):
            begin = pl.multiple_of(i * rows, rows)
            allowed = attend_masks(row_ids, col_ids, begin, rows)
            pulled = []
            key_grad = jnp.zeros((k_ref.shape[0], HD), jnp.float32)
            value_grad = jnp.zeros((k_ref.shape[0], HD), jnp.float32)
            for h in range(heads):
                head = kv * heads + h
                query = q_ref[pl.ds(begin, rows), head * HD : (head + 1) * HD]
                grad = g_ref[pl.ds(begin, rows), head * HD : (head + 1) * HD]
                scores = SCORE_SCALE * lax.dot_general(
                    query, keys, COLS_DIMS, preferred_element_type=jnp.float32
                )
                scores = jnp.where(allowed, scores, NEGATIVE)
                weights = jnp.exp(scores - top_ref[pl.ds(begin, rows), head : head + 1])
                chances = weights / total_ref[pl.ds(begin, rows), head : head + 1]
                prob_grad = lax.dot_general(
                    grad, vals, COLS_DIMS, preferred_element_type=jnp.float32
                )
                delta = jnp.sum(chances * prob_grad, axis=-1, keepdims=True)
                score_grad = (chances * (prob_grad - delta)).astype(jnp.bfloat16)
                pulled.append(
                    SCORE_SCALE * jnp.dot(score_grad, keys, preferred_element_type=jnp.float32)
                )
                key_grad += lax.dot_general(
                    score_grad, query, ROWS_DIMS, preferred_element_type=jnp.float32
                )
                value_grad += lax.dot_general(
                    chances.astype(jnp.bfloat16), grad, ROWS_DIMS, preferred_element_type=jnp.float32
                )
            dq_ref[pl.ds(begin, rows), kv * heads * HD : (kv + 1) * heads * HD] = jnp.concatenate(
                pulled, axis=1
            )
            dk_ref[:, cols] += SCORE_SCALE * key_grad
            dv_ref[:, cols] += value_grad
            return carry

        lax.fori_loop(0, q_ref.shape[0] // rows, step, 0)


def attend_back(queries, keys, vals, grads_in, top, total, row_ids, col_ids):
    rows = queries.shape[0]
    return pl.pallas_call(
        functools.partial(attend_back_kernel, heads=H // KVH, rows=min(256, rows)),
        out_shape=[
            jax.ShapeDtypeStruct(queries.shape, jnp.float32),
            jax.ShapeDtypeStruct(keys.shape, jnp.float32),
            jax.ShapeDtypeStruct(keys.shape, jnp.float32),
        ],
        name="attend_back",
    )(queries, keys, vals, grads_in, top, total, row_ids, col_ids)


def after(value, *earlier):
    return lax.optimization_barrier((value, *earlier))[0]


def rounded(values):
    return lax.reduce_precision(values, 8, 7)


def rope_parts(seq_lengths, places):
    seq_ends = jnp.cumsum(seq_lengths)
    seq_starts = seq_ends - seq_lengths
    member = (places[:, None] >= seq_starts[None, :]) & (places[:, None] < seq_ends[None, :])
    offsets = jnp.sum(jnp.where(member, places[:, None] - seq_starts[None, :], 0), axis=-1)
    frequency = THETA ** (-jnp.arange(HD // 2, dtype=jnp.float32) * 2.0 / HD)
    angles = offsets.astype(jnp.float32)[:, None] * frequency[None, :]
    angles = jnp.concatenate([angles, angles], axis=-1)[:, None, :]
    seq_ids = locate(places, seq_ends)
    return seq_ids, jnp.cos(angles), jnp.sin(angles)


def per_device(
    tokens,
    cotangent,
    lengths,
    deal,
    routes,
    gates,
    q_weight,
    k_weight,
    v_weight,
    o_weight,
    gain_attn,
    gain_moe,
    in_weight,
    down_weight,
):
    n_dp = lax.axis_size("dp")
    n_ex = lax.axis_size("expert")
    tok_rows = tokens.shape[1]
    model = tokens.shape[2]
    group_rows = tok_rows * n_dp
    kv_here = KVH // n_dp
    heads_per = H // KVH
    q_cols = kv_here * heads_per * HD
    kv_cols = kv_here * HD
    own_experts = in_weight.shape[1]
    ff_here = FF // n_dp
    ff_cols = own_experts * ff_here
    w_rows = q_weight.shape[0]
    ex_index = lax.axis_index("expert")
    group_ids = jnp.arange(deal.shape[0], dtype=jnp.int32)
    dealt_of = jnp.argmax((deal[None, :] == group_ids[:, None]).astype(jnp.int32), axis=1)
    own_dealt = jnp.sum(jnp.where(deal == ex_index, group_ids, 0))

    def by_owner(weight):
        return weight.astype(jnp.bfloat16).reshape(w_rows, n_dp, weight.shape[1] // n_dp)

    length_parts = jnp.stack([lengths[0] // 128, lengths[0] % 128]).reshape(-1).astype(jnp.bfloat16)
    n_len = length_parts.shape[0]
    extra = jnp.concatenate(
        [
            gain_attn.astype(jnp.bfloat16)[:, None],
            gain_moe.astype(jnp.bfloat16)[:, None],
            jnp.broadcast_to(length_parts[None, :], (w_rows, n_len)),
            jnp.zeros((w_rows, 126 - n_len), jnp.bfloat16),
        ],
        axis=1,
    )

    def pack_in(tie):
        return (
            tie(in_weight)
            .astype(jnp.bfloat16)
            .reshape(in_weight.shape[0], own_experts, 2, n_dp, ff_here)
            .transpose(3, 0, 2, 1, 4)
            .reshape(n_dp, in_weight.shape[0], 2 * ff_cols)
        )

    attn_out = jnp.concatenate(
        [
            by_owner(q_weight),
            by_owner(k_weight),
            by_owner(v_weight),
            by_owner(o_weight),
            jnp.broadcast_to(extra[:, None, :], (w_rows, n_dp, 128)),
        ],
        axis=2,
    ).transpose(1, 0, 2)
    attn_in = lax.all_to_all(attn_out, "dp", split_axis=0, concat_axis=0, tiled=True)

    group_tokens, (_, in_out, _, _) = dp_gather(tokens[0], (None, pack_in, None, None))
    attn_two = jnp.stack([attn_in, swap_core(attn_in)])
    attn_four = joined(attn_two, swap_x(attn_two))
    in_w = lax.all_to_all(
        after(in_out, group_tokens, attn_in), "dp", split_axis=0, concat_axis=0, tiled=True
    ).reshape(model, 2 * ff_cols)
    z_own, y_own = lax.axis_index("dp") // 2, lax.axis_index("dp") % 2
    slot_dp = 2 * jnp.asarray(SLOT_Z, jnp.int32)[:, z_own]
    block_dp = jnp.stack([slot_dp + y_own, slot_dp + 1 - y_own], axis=1).reshape(-1)
    places = (block_dp[:, None] * tok_rows + jnp.arange(tok_rows, dtype=jnp.int32)).reshape(-1)


    def of_expert(index):
        return lax.dynamic_index_in_dim(attn_four, index ^ ex_index, 0, keepdims=False)

    attn_all = jnp.stack([of_expert(e) for e in range(n_ex)])
    attn_w = attn_all.transpose(1, 0, 2, 3).reshape(model, -1)
    qkv_cols = q_cols + 2 * kv_cols
    qkv_w = attn_w[:, :qkv_cols]
    o_w = attn_w[:, qkv_cols : qkv_cols + q_cols]
    side = attn_w[:, qkv_cols + q_cols :]
    gain_one = side[:, 0].astype(jnp.float32)
    gain_two = side[:, 1].astype(jnp.float32)
    own_parts = of_expert(own_dealt)[
        0, 0, qkv_cols + q_cols + 2 : qkv_cols + q_cols + 2 + n_len
    ].astype(jnp.int32)
    seq_lengths = own_parts[: n_len // 2] * 128 + own_parts[n_len // 2 :]

    down_w = down_weight.astype(jnp.bfloat16).transpose(1, 0, 2).reshape(ff_cols, model)

    every = jnp.arange(E, dtype=jnp.int32)[None, :]
    dense = sum(
        jnp.where(routes[0][:, k : k + 1] == every, gates[0][:, k : k + 1], 0.0)
        for k in range(TOPK)
    )
    dense_top = rounded(dense)
    dense_mid = rounded(dense - dense_top)
    meta = jnp.concatenate(
        [
            dense_top,
            dense_mid,
            dense - dense_top - dense_mid,
            jnp.zeros((tok_rows, 128 - 3 * E), jnp.float32),
        ],
        axis=1,
    ).astype(jnp.bfloat16)

    seq_ids, cosine, sine_table = rope_parts(seq_lengths, places)
    group_inputs = group_tokens.astype(jnp.float32)
    first_scale = lax.rsqrt(jnp.mean(group_inputs * group_inputs, axis=-1, keepdims=True) + EPSILON)
    row_ids = jnp.stack([seq_ids, places], axis=1)
    col_ids = jnp.stack([seq_ids, places], axis=0)

    def project(tie):
        normed = (tie(group_inputs) * first_scale * gain_one).astype(jnp.bfloat16)
        qkv = jnp.dot(normed, qkv_w, preferred_element_type=jnp.float32)
        queries = (
            rotate(qkv[:, :q_cols].reshape(group_rows, kv_here * heads_per, HD), cosine, sine_table)
            .astype(jnp.bfloat16)
            .reshape(group_rows, q_cols)
        )
        keys = (
            rotate(
                qkv[:, q_cols : q_cols + kv_cols].reshape(group_rows, kv_here, HD),
                cosine,
                sine_table,
            )
            .astype(jnp.bfloat16)
            .reshape(group_rows, kv_cols)
        )
        vals = qkv[:, q_cols + kv_cols :].astype(jnp.bfloat16)
        return normed, queries, keys, vals

    def mix(tie, projected):
        _, queries, keys, vals = projected
        mixed = attend(tie(queries), keys, vals, row_ids, col_ids)
        part = lax.dot_general(mixed[0], o_w, COLS_DIMS, preferred_element_type=jnp.float32)
        return mixed, part.astype(jnp.bfloat16)

    cot_out = after(jnp.concatenate([cotangent[0], meta], axis=1), group_tokens)
    cot_all, branch, (projected, mixed) = gather_beside_sum(cot_out, project, mix)
    normed, queries, keys, vals = projected
    mixed_low, run_top, run_total = mixed
    rows_from, meta_from = far_order(ex_index, dealt_of)
    cot_rows, meta_all = take_blocks(
        jnp.stack([rows_from, meta_from]),
        cot_all,
        [(0, 0, model), (1, model // 128, 128)],
        tok_rows // 2,
    )
    inputs = tokens[0].astype(jnp.float32)
    middle = inputs + RESIDUAL * branch
    second_scale = lax.rsqrt(jnp.mean(middle * middle, axis=-1, keepdims=True) + EPSILON)
    sent_rows = (middle * second_scale * gain_two).astype(jnp.bfloat16)
    sent_rows = after(sent_rows, in_w, cot_rows)
    slot_rows = 8 * tok_rows

    def spread_gates(tie):
        column = jnp.arange(128, dtype=jnp.int32)[:, None]
        owner = ex_index * own_experts + jnp.arange(ff_cols, dtype=jnp.int32)[None, :] // ff_here
        spread = ((column % E == owner) & (column < 3 * E)).astype(jnp.bfloat16)
        return jnp.dot(tie(meta_all), spread, preferred_element_type=jnp.float32)

    def pull(tie):
        return lax.dot_general(
            tie(cot_rows), down_w, COLS_DIMS, preferred_element_type=jnp.float32
        )

    def up(tie, sent):
        return jnp.dot(tie(sent), in_w, preferred_element_type=jnp.float32)

    def down(gate_up, gates_here, pulled_here):
        gate_part = gate_up[:, :ff_cols]
        up_part = gate_up[:, ff_cols:]
        sigma = jax.nn.sigmoid(gate_part)
        silu = gate_part * sigma
        hidden = (silu * up_part).astype(jnp.bfloat16).astype(jnp.float32)
        weighted_here = (gates_here * hidden).astype(jnp.bfloat16)
        hidden_grad = RESIDUAL * gates_here * pulled_here
        gate_grad = hidden_grad * up_part * (sigma * (1.0 + gate_part * (1.0 - sigma)))
        up_grad = hidden_grad * silu
        grads_here = jnp.concatenate([gate_grad, up_grad], axis=1).astype(jnp.bfloat16)
        return weighted_here, grads_here

    def back(grads_here):
        return lax.dot_general(
            grads_here, in_w, COLS_DIMS, preferred_element_type=jnp.float32
        ).astype(jnp.bfloat16)

    sent_slots, ups, (gate_cols, pulled) = gather_slots(sent_rows, (spread_gates, pull, up))
    ups = ups + [up(lambda v: v, sent_slots[3])]
    weighted_slots, grad_slots = zip(
        *[
            down(
                ups[n],
                gate_cols[n * slot_rows : (n + 1) * slot_rows],
                pulled[n * slot_rows : (n + 1) * slot_rows],
            )
            for n in range(4)
        ]
    )
    sent_grad_slots = [back(g) for g in grad_slots]

    def out_rows(tie, works):
        return [
            jnp.dot(tie(part), down_w, preferred_element_type=jnp.float32).astype(jnp.bfloat16)
            for part in weighted_slots
        ]

    def in_terms(numbers, so_far):
        def work(tie, works):
            total = so_far()
            for n in numbers:
                term = lax.dot_general(
                    tie(sent_slots[n]), grad_slots[n], ROWS_DIMS, preferred_element_type=jnp.float32
                )
                total = term if total is None else total + term
            return total

        return work

    def down_terms(tie):
        return RESIDUAL * lax.dot_general(
            tie(joined(*weighted_slots)), cot_rows, ROWS_DIMS, preferred_element_type=jnp.float32
        )

    sent_grad, (_, out_slots, in_low, in_mid, in_high, _) = scatter_slots(
        sent_grad_slots,
        (
            None,
            out_rows,
            in_terms((0, 1), lambda: None),
            in_terms((2,), lambda: None),
            in_terms((3,), lambda: None),
            None,
        ),
    )
    in_term = (in_low + in_mid + in_high).astype(jnp.bfloat16)

    upstream = cotangent[0].astype(jnp.float32)
    scaled_grad = sent_grad * gain_two
    middle_grad = (
        upstream
        + second_scale * scaled_grad
        - middle
        * second_scale**3
        * jnp.mean(scaled_grad * middle, axis=-1, keepdims=True)
    )
    gain_two_part = jnp.sum(sent_grad * middle * second_scale, axis=0)
    branch_grad = (RESIDUAL * middle_grad).astype(jnp.bfloat16)

    def gather_one(tie, works):
        piece = tie(branch_grad)
        return over_dp(piece, Z_NEAR), over_dp(piece, Z_MIDDLE), swap_y(piece)

    def gather_two(tie, works):
        near, middle, _ = works[0]
        moved = over_dp(tie(near), Z_MIDDLE), over_dp(middle, Z_OUT), swap_y(near)
        return moved, down_terms(tie)

    def gather_three(tie, works):
        third = works[0][1] + works[1][0][1]
        return over_dp(tie(works[1][0][0]), Z_OUT), swap_y(third), third

    def gather_four(tie, works):
        fourth = works[1][0][0] + works[2][0]
        return swap_y(tie(fourth)), fourth

    def pull_attention(tie, works):
        (near, _, y0), ((_, _, y1), _), (_, y2, third), (y3, fourth) = works[:4]
        grad_all = joined(tie(branch_grad), y0, near, y1, third, y2, fourth, y3)
        o_term = lax.dot_general(grad_all, mixed_low, ROWS_DIMS, preferred_element_type=jnp.float32)
        grad_heads = jnp.dot(grad_all, o_w, preferred_element_type=jnp.float32).astype(
            jnp.bfloat16
        )
        return o_term, attend_back(
            queries, keys, vals, grad_heads, run_top, run_total, row_ids, col_ids
        )

    def pull_projections(tie, works):
        o_term, (query_grad, key_grad, value_grad) = works[4]
        query_low = turn_back(
            tie(query_grad).reshape(group_rows, kv_here * heads_per, HD), cosine, sine_table
        ).reshape(group_rows, q_cols)
        key_low = turn_back(
            key_grad.reshape(group_rows, kv_here, HD), cosine, sine_table
        ).reshape(group_rows, kv_cols)
        qkv_grad = jnp.concatenate([query_low, key_low, value_grad], axis=1).astype(jnp.bfloat16)
        normed_grad_part = lax.dot_general(
            qkv_grad, qkv_w, COLS_DIMS, preferred_element_type=jnp.float32
        )
        gain_one_part = jnp.sum(normed_grad_part * group_inputs * first_scale, axis=0)
        qkv_term = lax.dot_general(normed, qkv_grad, ROWS_DIMS, preferred_element_type=jnp.float32)
        grads = jnp.concatenate(
            [
                qkv_term,
                o_term,
                gain_one_part[:, None],
                gain_two_part[:, None],
                jnp.zeros((model, 126), jnp.float32),
            ],
            axis=1,
        ).astype(jnp.bfloat16)
        return normed_grad_part.astype(jnp.bfloat16), grads

    expert_sum, works = scatter_slots(
        [after(out_slots[n], sent_grad) for n in range(4)],
        (gather_one, gather_two, gather_three, gather_four, pull_attention, pull_projections),
    )
    in_back = lax.all_to_all(
        after(in_term, works[3]).reshape(n_dp, in_weight.shape[0], 2 * ff_cols),
        "dp",
        split_axis=0,
        concat_axis=0,
        tiled=True,
    )
    output = middle + RESIDUAL * expert_sum
    down_grad = works[1][1].reshape(own_experts, ff_here, model).transpose(1, 0, 2)
    normed_grad_part, grads = works[5]
    total = DpScatter(normed_grad_part)
    grads = grads.reshape(n_dp, n_ex, w_rows, -1)
    own_g, core_g, x_g, xc_g = [
        lax.dynamic_index_in_dim(grads, ex_index ^ k, 1, keepdims=False) for k in range(n_ex)
    ]
    core_pair = jnp.stack([core_g, xc_g])
    (sums, from_core), _ = one_round((total.step(), swap_core(core_pair)), (core_pair,))
    total.keep(sums)
    x_g = added(x_g, from_core[1])
    (sums, from_x), _ = one_round((total.step(), swap_x(x_g)), (x_g,))
    total.keep(sums)
    grads = lax.all_to_all(
        after(added(own_g, from_core[0], from_x), in_back), "dp", split_axis=0, concat_axis=0, tiled=True
    )
    (sums, grads), _ = one_round((total.step(), grads), ())
    total.keep(sums)
    grads = grads.astype(jnp.float32)
    total.keep(one_round(total.step(), ())[0])
    normed_grad = total.total()
    in_grad = (
        in_back
        .reshape(n_dp, in_weight.shape[0], 2, own_experts, ff_here)
        .transpose(1, 3, 2, 0, 4)
        .reshape(in_weight.shape)
        .astype(jnp.float32)
    )

    def own_rows(begin, width):
        return grads[:, :, begin : begin + width].transpose(1, 0, 2).reshape(w_rows, n_dp * width)

    q_grad = own_rows(0, q_cols)
    k_grad = own_rows(q_cols, kv_cols)
    v_grad = own_rows(q_cols + kv_cols, kv_cols)
    o_grad = own_rows(qkv_cols, q_cols)
    gain_attn_grad = jnp.sum(grads[:, :, qkv_cols + q_cols], axis=0)
    gain_moe_grad = jnp.sum(grads[:, :, qkv_cols + q_cols + 1], axis=0)

    own_scale = lax.rsqrt(jnp.mean(inputs * inputs, axis=-1, keepdims=True) + EPSILON)
    scaled_one = normed_grad * gain_one
    input_grad = (
        middle_grad
        + own_scale * scaled_one
        - inputs * own_scale**3 * jnp.mean(scaled_one * inputs, axis=-1, keepdims=True)
    )
    return (
        output[None],
        input_grad[None],
        q_grad,
        k_grad,
        v_grad,
        o_grad,
        gain_attn_grad,
        gain_moe_grad,
        in_grad,
        down_grad,
    )


def per_layer(*args):
    return per_device(*args)


def solution(mesh):
    placed = (
        P("expert", "dp", None),
        P("expert", "dp", None),
        P("expert", None),
        P(),
        P("expert", "dp", None),
        P("expert", "dp", None),
        P(("dp", "expert"), None),
        P(("dp", "expert"), None),
        P(("dp", "expert"), None),
        P(("dp", "expert"), None),
        P(("dp", "expert")),
        P(("dp", "expert")),
        P("dp", "expert", None),
        P("dp", "expert", None),
    )
    n_dp = mesh.shape["dp"]
    split_heads = n_dp == 8 and mesh.shape["expert"] == 4
    return jax.shard_map(
        per_layer if split_heads else per_device_wide,
        mesh=mesh,
        in_specs=placed,
        out_specs=(
            P("expert", "dp", None),
            P("expert", "dp", None),
            P(("dp", "expert"), None),
            P(("dp", "expert"), None),
            P(("dp", "expert"), None),
            P(("dp", "expert"), None),
            P(("dp", "expert")),
            P(("dp", "expert")),
            P("dp", "expert", None),
            P("dp", "expert", None),
        ),
        check_vma=False,
    )
```

profile of v0, /device:TPU:0, one launch (start us, length us, event | category | flops | bytes accessed | tf_op | source)
XLA Modules:
  0.0 889.9 jit_solution(12377677426776678452)
XLA Ops:
  14.9 5.0 all-to-all-start
  26.1 8.5 copy.180
  34.6 5.6 copy.181
  49.8 5.0 collective-permute-done.7
  54.8 4.0 collective-permute-done.6
  77.7 10.8 %collective-permute-done.12 = bf16[2,8,48,640]{3,2,0,1:T(8,128)(2,1)S(1)} collective-permute-done((bf16[2,8,48,640]{3,2,0,1:T(8,128)(2,1)S(1)}, bf16[2,8,48,640]{3,2,0,1:T(8,128)(2,1)S(1)}, u32[]{:S(2)}, u32[]{:S(2)}) %collective-permute-start.12) | collective-permute-done | bytes 983072 | tf_op jit(solution)/shard_map/ppermute | solution.py:409
  116.1 11.1 %attend.1 = (bf16[1024,192]{1,0:T(8,128)(2,1)}, f32[1024,3]{1,0:T(8,128)}, f32[1024,3]{1,0:T(8,128)}) custom-call(bf16[1024,192]{1,0:T(8,128)(2,1)} %add_convert_fusion.10.q_ref, bf16[1024,64]{1,0:T(8,128)(2,1)} %get-tuple-element.221.k_ref, bf16[1024,64]{1,0:T(8,128)(2,1)} %copy.211.v_ref, s32[1024,2]{1,0:T(8,128)} %copy.193.row_ids, ...), custom_call_target="tpu_custom_call" | custom-call | tf_op jit(solution)/shard_map/attend/pallas_call | solution.py:720
  151.6 5.3 collective-permute-start.23
  166.0 7.1 collective-permute-start.27
  179.8 12.0 %collective-permute-done.25 = bf16[256,1664]{1,0:T(8,128)(2,1)S(1)} collective-permute-done((bf16[256,1664]{1,0:T(8,128)(2,1)S(1)}, bf16[256,1664]{1,0:T(8,128)(2,1)S(1)}, u32[]{:S(2)}, u32[]{:S(2)}) %collective-permute-start.25) | collective-permute-done | bytes 852000 | tf_op jit(solution)/shard_map/ppermute | solution.py:409
  198.5 3.6 collective-permute-done.30
  206.8 7.4 copy.194
  214.3 4.5 all-to-all-start.1
  218.8 3.8 convert_element_type.819
  228.4 6.3 constant_dynamic-update-slice_fusion.20.refs_0_.refs_1_.refs_2_.refs_3_.refs_4_.refs_5_.refs_6_.refs_7_.refs_8_.refs_9_.refs_10_.refs_11_.refs_12_.refs_13_.refs_14_.refs_15_
  234.7 12.6 %take_blocks.1 = (bf16[4096,1536]{1,0:T(8,128)(2,1)}, bf16[4096,128]{1,0:T(8,128)(2,1)}) custom-call(s32[2,64]{1,0:T(2,128)} %pad_add_fusion.2.index_ref, bf16[4096,1664]{1,0:T(8,128)(2,1)} %constant_dynamic-update-slice_fusion.20.refs_0_.refs_1_.refs_2_.refs_3_.refs_4_.refs_5_.refs_6_.refs_7_.refs_8_.refs_9_.refs_10_.refs_11_.refs_12_.refs_13_.refs_14_.refs_15_, ...), custom_call_target="tpu_custom_call" | custom-call | tf_op jit(solution)/shard_map/take_blocks/pallas_call | solution.py:650
  247.3 60.0 %all-to-all-done.1 = bf16[8,192,1280]{2,1,0:T(8,128)(2,1)} async-done(((bf16[8,192,1280]{2,1,0:T(8,128)(2,1)}), bf16[8,192,1280]{2,1,0:T(8,128)(2,1)}, u32[]{:S(2)}, u32[]{:S(2)}) %all-to-all-start.1) | async-done | bytes 3932192 | tf_op jit(solution)/shard_map/all_to_all | solution.py:887
  311.0 3.4 collective-permute-done.36
  325.7 7.5 collective-permute-done.42
  334.7 4.2 collective-permute-done.43
  345.4 15.4 %fusion.91 = f32[4096,640]{1,0:T(8,128)} fusion(bf16[4096,1536]{1,0:T(8,128)(2,1)} %get-tuple-element.265, bf16[640,1536]{1,0:T(8,128)(2,1)S(1)} %bitcast.202), kind=kOutput, calls=%fused_computation.485 | convolution fusion | flops 8053063680 | bytes 25034752 | tf_op jit(solution)/shard_map/dot_general | solution.py:988
  361.5 6.4 collective-permute-done.48
  373.4 6.3 fusion.92
  392.9 7.5 fusion.93
  408.5 6.0 multiply_convert_fusion.4
  414.6 8.1 convolution_convert_fusion.6
  425.0 6.6 convolution_convert_fusion.5
  434.2 7.5 fusion.94
  443.6 8.0 fusion.95
  451.6 7.2 multiply_convert_fusion.14
  458.8 7.6 convolution_convert_fusion.8
  468.1 7.2 convolution_convert_fusion.7
  488.5 4.2 convolution_convert_fusion.2
  492.7 4.0 convolution_convert_fusion.3
  501.7 6.9 fusion.4
  510.1 8.6 convolution_add_fusion
  521.0 9.3 %collective-permute-start.69 = (bf16[128,1536]{1,0:T(8,128)(2,1)S(1)}, bf16[128,1536]{1,0:T(8,128)(2,1)S(1)}, u32[]{:S(2)}, u32[]{:S(2)}) collective-permute-start(bf16[128,1536]{1,0:T(8,128)(2,1)S(1)} %pad_maximum_fusion.32), channel_id=1, source_target_pairs={{0,8},{4,12},{24,16},{28,20},{1,9},{5,13},{25,17},{29,21},{2,10},{... | collective-permute-start | bytes 1179656 | tf_op jit(solution)/shard_map/ppermute | solution.py:405
  530.3 9.3 %fusion.5 = f32[1536,1280]{1,0:T(8,128)} fusion(bf16[1024,1536]{1,0:T(8,128)(2,1)} %constant_dynamic-update-slice_fusion.71, bf16[1024,640]{1,0:T(8,128)(2,1)S(1)} %copy-done.63, bf16[1024,640]{1,0:T(8,128)(2,1)S(1)} %copy-done.62), kind=kOutput, calls=%fused_computation.61 | convolution fusion | flops 4031774720 | bytes 13631488 | tf_op jit(solution)/shard_map/dot_general | solution.py:1037
  545.5 8.2 collective-permute-done.70
  564.3 6.6 fusion.6
  574.7 4.8 collective-permute-done.82
  587.9 12.7 %pad_maximum_fusion = bf16[4096,640]{1,0:T(8,128)(2,1)S(1)} fusion(bf16[1024,640]{1,0:T(8,128)(2,1)} %copy-done.16, bf16[1024,640]{1,0:T(8,128)(2,1)S(1)} %get-tuple-element.290, bf16[1024,640]{1,0:T(8,128)(2,1)} %copy-done.15, bf16[1024,640]{1,0:T(8,128)(2,1)S(1)} %get-tuple-element.287), kind=kLoop, calls=%fused_computation.6 | loop fusion | flops 20971520 | bytes 10485760 | tf_op jit(solution)/shard_map/concatenate | solution.py:425
  610.6 13.1 %convolution_multiply_fusion = f32[640,1536]{1,0:T(8,128)} fusion(bf16[4096,640]{1,0:T(8,128)(2,1)S(1)} %pad_maximum_fusion, bf16[4096,1536]{1,0:T(8,128)(2,1)} %get-tuple-element.265), kind=kOutput, calls=%fused_computation.7 | convolution fusion | flops 8054046720 | bytes 21757952 | tf_op jit(solution)/shard_map/dot_general | solution.py:1046
  636.6 5.4 collective-permute-done.94
  644.0 10.8 %add_convert_fusion = bf16[1536,1280]{1,0:T(8,128)(2,1)} fusion(f32[1536,1280]{1,0:T(8,128)} %fusion.6, f32[1536,1280]{1,0:T(8,128)} %convolution_add_fusion, f32[1536,1280]{1,0:T(8,128)} %fusion.5), kind=kLoop, calls=%fused_computation.2 | loop fusion | flops 5898240 | bytes 27525120 | tf_op jit(solution)/shard_map/convert_element_type | solution.py:1061
  661.4 6.5 collective-permute-start.102
  671.8 17.2 %collective-permute-done.103 = bf16[64,1536]{1,0:T(8,128)(2,1)S(1)} collective-permute-done((bf16[64,1536]{1,0:T(8,128)(2,1)S(1)}, bf16[64,1536]{1,0:T(8,128)(2,1)S(1)}, u32[]{:S(2)}, u32[]{:S(2)}) %collective-permute-start.103) | collective-permute-done | bytes 196640 | tf_op jit(solution)/shard_map/ppermute | solution.py:405
  690.7 5.9 collective-permute-done.104
  704.3 4.9 all-to-all-start.2
  722.5 16.4 %attend_back.1 = (f32[1024,192]{1,0:T(8,128)}, f32[1024,64]{1,0:T(8,128)}, f32[1024,64]{1,0:T(8,128)}) custom-call(bf16[1024,192]{1,0:T(8,128)(2,1)} %add_convert_fusion.10.q_ref, bf16[1024,64]{1,0:T(8,128)(2,1)} %get-tuple-element.221.k_ref, bf16[1024,64]{1,0:T(8,128)(2,1)} %copy.211.v_ref, bf16[1024,192]{1,0:T(8,128)(2,1)} %copy.195.g_ref, ...), custom_call_target="tpu_custom_call" | custom-call | tf_op jit(solution)/shard_map/attend_back/pallas_call | solution.py:783
  740.3 3.7 fusion.96
  750.9 3.4 collective-permute-start.114
  770.6 3.5 multiply_reduce_fusion
  778.4 7.3 concatenate.235
  797.3 6.0 collective-permute-done.118
  804.2 20.4 %collective-permute-start.120 = (bf16[128,1536]{1,0:T(8,128)(2,1)S(1)}, bf16[128,1536]{1,0:T(8,128)(2,1)S(1)}, u32[]{:S(2)}, u32[]{:S(2)}) collective-permute-start(bf16[128,1536]{1,0:T(8,128)(2,1)S(1)} %add_convert_fusion.15), channel_id=1, source_target_pairs={{0,8},{4,12},{24,16},{28,20},{1,9},{5,13},{25,17},{29,21},{2,10},{... | collective-permute-start | bytes 1179656 | tf_op jit(solution)/shard_map/ppermute | solution.py:405
  826.8 4.1 collective-permute-done.120
  831.7 4.4 collective-permute-start.124
  837.1 3.7 all-to-all-start.3
  842.5 7.4 copy.206
  849.9 3.9 convert_bitcast_fusion
  853.9 4.8 copy.207
  858.7 10.4 %copy.208 = f32[192,10,1024]{2,0,1:T(8,128)} copy(f32[192,10,1024]{0,2,1:T(8,128)} %bitcast.179) | data formatting | bytes 15728640
  873.6 5.8 collective-permute-start.126
  (754 shorter events, 360.5 us)
Async XLA Ops:
  0.7 20.6 %collective-permute-start = (bf16[128,1536]{1,0:T(8,128)(2,1)}, bf16[128,1536]{1,0:T(8,128)(2,1)}, u32[]{:S(2)}, u32[]{:S(2)}) collective-permute-start(bf16[128,1536]{1,0:T(8,128)(2,1)} %bitcast.194), channel_id=1, source_target_pairs={{0,8},{4,12},{8,0},{12,4},{16,24},{20,28},{24,16},{28,20},{1,9},{5... | collective-permute-start | bytes 1179656 | tf_op jit(solution)/shard_map/ppermute | solution.py:405
  14.9 34.8 %all-to-all-start = ((bf16[8,48,640]{2,1,0:T(8,128)(2,1)}), bf16[8,48,640]{2,1,0:T(8,128)(2,1)}, u32[]{:S(2)}, u32[]{:S(2)}) async-start(bf16[8,48,640]{2,1,0:T(8,128)(2,1)} %copy.184), calls=%async_computation | async-start | bytes 983040 | tf_op jit(solution)/shard_map/all_to_all | solution.py:882
  21.3 21.0 %collective-permute-start.3 = (bf16[128,1536]{1,0:T(8,128)(2,1)}, bf16[128,1536]{1,0:T(8,128)(2,1)}, u32[]{:S(2)}, u32[]{:S(2)}) collective-permute-start(bf16[128,1536]{1,0:T(8,128)(2,1)} %collective-permute-done), channel_id=1, source_target_pairs={{8,16},{12,20},{16,8},{20,12},{9,17},{13,21},{17,9},{21,13},{10,18... | collective-permute-start | bytes 1179656 | tf_op jit(solution)/shard_map/ppermute | solution.py:405
  22.8 19.5 %collective-permute-start.5 = (bf16[128,1536]{1,0:T(8,128)(2,1)}, bf16[128,1536]{1,0:T(8,128)(2,1)}, u32[]{:S(2)}, u32[]{:S(2)}) collective-permute-start(bf16[128,1536]{1,0:T(8,128)(2,1)} %collective-permute-done), channel_id=1, source_target_pairs={{0,4},{4,0},{8,12},{12,8},{16,20},{20,16},{24,28},{28,24},{1,5},{5... | collective-permute-start | bytes 1179656 | tf_op jit(solution)/shard_map/ppermute | solution.py:405
  68.1 20.5 %collective-permute-start.12 = (bf16[2,8,48,640]{3,2,0,1:T(8,128)(2,1)S(1)}, bf16[2,8,48,640]{3,2,0,1:T(8,128)(2,1)S(1)}, u32[]{:S(2)}, u32[]{:S(2)}) collective-permute-start(bf16[2,8,48,640]{3,2,0,1:T(8,128)(2,1)S(1)} %pad_maximum_fusion.15), channel_id=1, source_target_pairs={{0,2},{1,3},{2,0},{3,1},{4,6},{5,7},{6,4},{7,5},{8,10},{9,11},{10,... | collective-permute-start | bytes 2949128 | tf_op jit(solution)/shard_map/ppermute | solution.py:409
  72.2 38.3 %collective-permute-start.10 = (bf16[128,1664]{1,0:T(8,128)(2,1)}, bf16[128,1664]{1,0:T(8,128)(2,1)}, u32[]{:S(2)}, u32[]{:S(2)}) collective-permute-start(bf16[128,1664]{1,0:T(8,128)(2,1)} %concatenate.184), channel_id=1, source_target_pairs={{8,16},{12,20},{16,8},{20,12},{9,17},{13,21},{17,9},{21,13},{10,18... | collective-permute-start | bytes 1277960 | tf_op jit(solution)/shard_map/ppermute | solution.py:405
  73.7 36.9 %collective-permute-start.9 = (bf16[128,1664]{1,0:T(8,128)(2,1)}, bf16[128,1664]{1,0:T(8,128)(2,1)}, u32[]{:S(2)}, u32[]{:S(2)}) collective-permute-start(bf16[128,1664]{1,0:T(8,128)(2,1)} %concatenate.184), channel_id=1, source_target_pairs={{0,8},{4,12},{8,0},{12,4},{16,24},{20,28},{24,16},{28,20},{1,9},{5... | collective-permute-start | bytes 1277960 | tf_op jit(solution)/shard_map/ppermute | solution.py:405
  75.6 54.0 %collective-permute-start.15 = (bf16[128,1664]{1,0:T(8,128)(2,1)}, bf16[128,1664]{1,0:T(8,128)(2,1)}, u32[]{:S(2)}, u32[]{:S(2)}) collective-permute-start(bf16[128,1664]{1,0:T(8,128)(2,1)} %concatenate.184), channel_id=1, source_target_pairs={{0,4},{4,0},{8,12},{12,8},{16,20},{20,16},{24,28},{28,24},{1,5},{5... | collective-permute-start | bytes 1277960 | tf_op jit(solution)/shard_map/ppermute | solution.py:405
  110.5 19.1 %collective-permute-start.13 = (bf16[128,1664]{1,0:T(8,128)(2,1)}, bf16[128,1664]{1,0:T(8,128)(2,1)}, u32[]{:S(2)}, u32[]{:S(2)}) collective-permute-start(bf16[128,1664]{1,0:T(8,128)(2,1)} %collective-permute-done.9), channel_id=1, source_target_pairs={{8,16},{12,20},{16,8},{20,12},{9,17},{13,21},{17,9},{21,13},{10,18... | collective-permute-start | bytes 1277960 | tf_op jit(solution)/shard_map/ppermute | solution.py:405
  112.0 29.2 %collective-permute-start.17 = (bf16[128,1664]{1,0:T(8,128)(2,1)}, bf16[128,1664]{1,0:T(8,128)(2,1)}, u32[]{:S(2)}, u32[]{:S(2)}) collective-permute-start(bf16[128,1664]{1,0:T(8,128)(2,1)} %collective-permute-done.9), channel_id=1, source_target_pairs={{0,4},{4,0},{8,12},{12,8},{16,20},{20,16},{24,28},{28,24},{1,5},{5... | collective-permute-start | bytes 1277960 | tf_op jit(solution)/shard_map/ppermute | solution.py:405
  130.9 17.9 %collective-permute-start.18 = (bf16[256,1664]{1,0:T(8,128)(2,1)S(1)}, bf16[256,1664]{1,0:T(8,128)(2,1)S(1)}, u32[]{:S(2)}, u32[]{:S(2)}) collective-permute-start(bf16[256,1664]{1,0:T(8,128)(2,1)S(1)} %pad_maximum_fusion.17), channel_id=1, source_target_pairs={{0,2},{1,3},{2,0},{3,1},{4,6},{5,7},{6,4},{7,5},{8,10},{9,11},{10,... | collective-permute-start | bytes 2555912 | tf_op jit(solution)/shard_map/ppermute | solution.py:409
  138.2 26.2 %collective-permute-start.21 = (bf16[128,1664]{1,0:T(8,128)(2,1)S(1)}, bf16[128,1664]{1,0:T(8,128)(2,1)S(1)}, u32[]{:S(2)}, u32[]{:S(2)}) collective-permute-start(bf16[128,1664]{1,0:T(8,128)(2,1)S(1)} %add.876), channel_id=1, source_target_pairs={{0,4},{4,0},{8,12},{12,8},{16,20},{20,16},{24,28},{28,24},{1,5},{5... | collective-permute-start | bytes 1277960 | tf_op jit(solution)/shard_map/ppermute | solution.py:405
  141.2 22.1 %collective-permute-start.24 = (bf16[128,1536]{1,0:T(8,128)(2,1)S(1)}, bf16[128,1536]{1,0:T(8,128)(2,1)S(1)}, u32[]{:S(2)}, u32[]{:S(2)}) collective-permute-start(bf16[128,1536]{1,0:T(8,128)(2,1)S(1)} %get-tuple-element.505), channel_id=1, source_target_pairs={{0,4},{4,0},{8,12},{12,8},{16,20},{20,16},{24,28},{28,24},{1,5},{5... | collective-permute-start | bytes 1179656 | tf_op jit(solution)/shard_map/ppermute | solution.py:405
  144.6 34.2 %collective-permute-start.28 = (bf16[128,1536]{1,0:T(8,128)(2,1)S(1)}, bf16[128,1536]{1,0:T(8,128)(2,1)S(1)}, u32[]{:S(2)}, u32[]{:S(2)}) collective-permute-start(bf16[128,1536]{1,0:T(8,128)(2,1)S(1)} %get-tuple-element.504), channel_id=1, source_target_pairs={{0,4},{4,0},{8,12},{12,8},{16,20},{20,16},{24,28},{28,24},{1,5},{5... | collective-permute-start | bytes 1179656 | tf_op jit(solution)/shard_map/ppermute | solution.py:405
  173.1 18.6 %collective-permute-start.25 = (bf16[256,1664]{1,0:T(8,128)(2,1)S(1)}, bf16[256,1664]{1,0:T(8,128)(2,1)S(1)}, u32[]{:S(2)}, u32[]{:S(2)}) collective-permute-start(bf16[256,1664]{1,0:T(8,128)(2,1)S(1)} %pad_maximum_fusion.19), channel_id=1, source_target_pairs={{0,2},{1,3},{2,0},{3,1},{4,6},{5,7},{6,4},{7,5},{8,10},{9,11},{10,... | collective-permute-start | bytes 2555912 | tf_op jit(solution)/shard_map/ppermute | solution.py:409
  178.7 19.8 %collective-permute-start.32 = (bf16[128,1536]{1,0:T(8,128)(2,1)S(1)}, bf16[128,1536]{1,0:T(8,128)(2,1)S(1)}, u32[]{:S(2)}, u32[]{:S(2)}) collective-permute-start(bf16[128,1536]{1,0:T(8,128)(2,1)S(1)} %get-tuple-element.503), channel_id=1, source_target_pairs={{0,4},{4,0},{8,12},{12,8},{16,20},{20,16},{24,28},{28,24},{1,5},{5... | collective-permute-start | bytes 1179656 | tf_op jit(solution)/shard_map/ppermute | solution.py:405
  206.7 21.7 %collective-permute-start.33 = (bf16[2048,1664]{1,0:T(8,128)(2,1)}, bf16[2048,1664]{1,0:T(8,128)(2,1)}, u32[]{:S(2)}, u32[]{:S(2)}) collective-permute-start(bf16[2048,1664]{1,0:T(8,128)(2,1)} %get-tuple-element.550), channel_id=1, source_target_pairs={{0,1},{1,0},{2,3},{3,2},{4,5},{5,4},{6,7},{7,6},{8,9},{9,8},{10,11... | collective-permute-start | bytes 20447240 | tf_op jit(solution)/shard_map/ppermute | solution.py:409
  214.3 93.0 %all-to-all-start.1 = ((bf16[8,192,1280]{2,1,0:T(8,128)(2,1)}), bf16[8,192,1280]{2,1,0:T(8,128)(2,1)}, u32[]{:S(2)}, u32[]{:S(2)}) async-start(bf16[8,192,1280]{2,1,0:T(8,128)(2,1)} %copy.194), calls=%async_computation.1 | async-start | bytes 7864320 | tf_op jit(solution)/shard_map/all_to_all | solution.py:887
  318.5 20.4 %collective-permute-start.38 = (bf16[128,1536]{1,0:T(8,128)(2,1)S(1)}, bf16[128,1536]{1,0:T(8,128)(2,1)S(1)}, u32[]{:S(2)}, u32[]{:S(2)}) collective-permute-start(bf16[128,1536]{1,0:T(8,128)(2,1)S(1)} %collective-permute-done.34), channel_id=1, source_target_pairs={{8,16},{12,20},{16,8},{20,12},{9,17},{13,21},{17,9},{21,13},{10,18... | collective-permute-start | bytes 1179656 | tf_op jit(solution)/shard_map/ppermute | solution.py:405
  319.3 19.6 %collective-permute-start.41 = (bf16[128,1536]{1,0:T(8,128)(2,1)S(1)}, bf16[128,1536]{1,0:T(8,128)(2,1)S(1)}, u32[]{:S(2)}, u32[]{:S(2)}) collective-permute-start(bf16[128,1536]{1,0:T(8,128)(2,1)S(1)} %pad_maximum_fusion.25), channel_id=1, source_target_pairs={{0,4},{4,0},{8,12},{12,8},{16,20},{20,16},{24,28},{28,24},{1,5},{5... | collective-permute-start | bytes 1179656 | tf_op jit(solution)/shard_map/ppermute | solution.py:405
  320.8 18.1 %collective-permute-start.40 = (bf16[128,1536]{1,0:T(8,128)(2,1)S(1)}, bf16[128,1536]{1,0:T(8,128)(2,1)S(1)}, u32[]{:S(2)}, u32[]{:S(2)}) collective-permute-start(bf16[128,1536]{1,0:T(8,128)(2,1)S(1)} %pad_maximum_fusion.24), channel_id=1, source_target_pairs={{0,2},{1,3},{2,0},{3,1},{4,6},{5,7},{6,4},{7,5},{8,10},{9,11},{10,... | collective-permute-start | bytes 1179656 | tf_op jit(solution)/shard_map/ppermute | solution.py:409
  339.0 28.9 %collective-permute-start.46 = (bf16[128,1536]{1,0:T(8,128)(2,1)S(1)}, bf16[128,1536]{1,0:T(8,128)(2,1)S(1)}, u32[]{:S(2)}, u32[]{:S(2)}) collective-permute-start(bf16[128,1536]{1,0:T(8,128)(2,1)S(1)} %pad_maximum_fusion.27), channel_id=1, source_target_pairs={{0,4},{4,0},{8,12},{12,8},{16,20},{20,16},{24,28},{28,24},{1,5},{5... | collective-permute-start | bytes 1179656 | tf_op jit(solution)/shard_map/ppermute | solution.py:405
  340.6 27.3 %collective-permute-start.45 = (bf16[128,1536]{1,0:T(8,128)(2,1)S(1)}, bf16[128,1536]{1,0:T(8,128)(2,1)S(1)}, u32[]{:S(2)}, u32[]{:S(2)}) collective-permute-start(bf16[128,1536]{1,0:T(8,128)(2,1)S(1)} %pad_maximum_fusion.26), channel_id=1, source_target_pairs={{0,2},{1,3},{2,0},{3,1},{4,6},{5,7},{6,4},{7,5},{8,10},{9,11},{10,... | collective-permute-start | bytes 1179656 | tf_op jit(solution)/shard_map/ppermute | solution.py:409
  342.3 25.6 %collective-permute-start.49 = (bf16[512,1536]{1,0:T(8,128)(2,1)S(1)}, bf16[512,1536]{1,0:T(8,128)(2,1)S(1)}, u32[]{:S(2)}, u32[]{:S(2)}) collective-permute-start(bf16[512,1536]{1,0:T(8,128)(2,1)S(1)} %get-tuple-element.607), channel_id=1, source_target_pairs={{0,1},{1,0},{2,3},{3,2},{4,5},{5,4},{6,7},{7,6},{8,9},{9,8},{10,11... | collective-permute-start | bytes 4718600 | tf_op jit(solution)/shard_map/ppermute | solution.py:409
  343.2 17.7 %collective-permute-start.47 = (bf16[64,1536]{1,0:T(8,128)(2,1)S(1)}, bf16[64,1536]{1,0:T(8,128)(2,1)S(1)}, u32[]{:S(2)}, u32[]{:S(2)}) collective-permute-start(bf16[64,1536]{1,0:T(8,128)(2,1)S(1)} %get-tuple-element.591), channel_id=1, source_target_pairs={{0,4},{4,0},{8,12},{12,8},{16,20},{20,16},{24,28},{28,24},{1,5},{5... | collective-permute-start | bytes 589832 | tf_op jit(solution)/shard_map/ppermute | solution.py:405
  343.7 24.2 %collective-permute-start.44 = (bf16[128,1536]{1,0:T(8,128)(2,1)S(1)}, bf16[128,1536]{1,0:T(8,128)(2,1)S(1)}, u32[]{:S(2)}, u32[]{:S(2)}) collective-permute-start(bf16[128,1536]{1,0:T(8,128)(2,1)S(1)} %collective-permute-done.38), channel_id=1, source_target_pairs={{8,0},{12,4},{16,24},{20,28},{9,1},{13,5},{17,25},{21,29},{10,2},{... | collective-permute-start | bytes 1179656 | tf_op jit(solution)/shard_map/ppermute | solution.py:405
  368.0 18.6 %collective-permute-start.51 = (bf16[128,1536]{1,0:T(8,128)(2,1)S(1)}, bf16[128,1536]{1,0:T(8,128)(2,1)S(1)}, u32[]{:S(2)}, u32[]{:S(2)}) collective-permute-start(bf16[128,1536]{1,0:T(8,128)(2,1)S(1)} %pad_maximum_fusion.29), channel_id=1, source_target_pairs={{0,4},{4,0},{8,12},{12,8},{16,20},{20,16},{24,28},{28,24},{1,5},{5... | collective-permute-start | bytes 1179656 | tf_op jit(solution)/shard_map/ppermute | solution.py:405
  407.3 34.5 %collective-permute-start.58 = (bf16[512,1536]{1,0:T(8,128)(2,1)}, bf16[512,1536]{1,0:T(8,128)(2,1)S(1)}, u32[]{:S(2)}, u32[]{:S(2)}) collective-permute-start(bf16[512,1536]{1,0:T(8,128)(2,1)} %get-tuple-element.592), channel_id=1, source_target_pairs={{0,1},{1,0},{2,3},{3,2},{4,5},{5,4},{6,7},{7,6},{8,9},{9,8},{10,11... | collective-permute-start | bytes 4718600 | tf_op jit(solution)/shard_map/ppermute | solution.py:409
  424.0 84.7 %collective-permute-start.68 = (bf16[512,1536]{1,0:T(8,128)(2,1)}, bf16[512,1536]{1,0:T(8,128)(2,1)}, u32[]{:S(2)}, u32[]{:S(2)}) collective-permute-start(bf16[512,1536]{1,0:T(8,128)(2,1)} %slice.675), channel_id=1, source_target_pairs={{0,1},{1,0},{2,3},{3,2},{4,5},{5,4},{6,7},{7,6},{8,9},{9,8},{10,11... | collective-permute-start | bytes 4718600 | tf_op jit(solution)/shard_map/ppermute | solution.py:409
  433.7 85.0 %collective-permute-start.67 = (bf16[512,1536]{1,0:T(8,128)(2,1)}, bf16[512,1536]{1,0:T(8,128)(2,1)}, u32[]{:S(2)}, u32[]{:S(2)}) collective-permute-start(bf16[512,1536]{1,0:T(8,128)(2,1)} %slice.674), channel_id=1, source_target_pairs={{0,1},{1,0},{2,3},{3,2},{4,5},{5,4},{6,7},{7,6},{8,9},{9,8},{10,11... | collective-permute-start | bytes 4718600 | tf_op jit(solution)/shard_map/ppermute | solution.py:409
  476.9 19.8 %collective-permute-start.62 = (bf16[512,1536]{1,0:T(8,128)(2,1)S(1)}, bf16[512,1536]{1,0:T(8,128)(2,1)}, u32[]{:S(2)}, u32[]{:S(2)}) collective-permute-start(bf16[512,1536]{1,0:T(8,128)(2,1)S(1)} %slice.665), channel_id=1, source_target_pairs={{0,1},{1,0},{2,3},{3,2},{4,5},{5,4},{6,7},{7,6},{8,9},{9,8},{10,11... | collective-permute-start | bytes 4718600 | tf_op jit(solution)/shard_map/ppermute | solution.py:409
  499.0 19.6 %collective-permute-start.65 = (bf16[128,1536]{1,0:T(8,128)(2,1)S(1)}, bf16[128,1536]{1,0:T(8,128)(2,1)S(1)}, u32[]{:S(2)}, u32[]{:S(2)}) collective-permute-start(bf16[128,1536]{1,0:T(8,128)(2,1)S(1)} %get-tuple-element.541), channel_id=1, source_target_pairs={{0,2},{1,3},{2,0},{3,1},{4,6},{5,7},{6,4},{7,5},{8,10},{9,11},{10,... | collective-permute-start | bytes 1179656 | tf_op jit(solution)/shard_map/ppermute | solution.py:409
  499.7 19.0 %collective-permute-start.66 = (bf16[128,1536]{1,0:T(8,128)(2,1)S(1)}, bf16[128,1536]{1,0:T(8,128)(2,1)S(1)}, u32[]{:S(2)}, u32[]{:S(2)}) collective-permute-start(bf16[128,1536]{1,0:T(8,128)(2,1)S(1)} %get-tuple-element.540), channel_id=1, source_target_pairs={{0,4},{4,0},{8,12},{12,8},{16,20},{20,16},{24,28},{28,24},{1,5},{5... | collective-permute-start | bytes 1179656 | tf_op jit(solution)/shard_map/ppermute | solution.py:405
  521.0 34.5 %collective-permute-start.69 = (bf16[128,1536]{1,0:T(8,128)(2,1)S(1)}, bf16[128,1536]{1,0:T(8,128)(2,1)S(1)}, u32[]{:S(2)}, u32[]{:S(2)}) collective-permute-start(bf16[128,1536]{1,0:T(8,128)(2,1)S(1)} %pad_maximum_fusion.32), channel_id=1, source_target_pairs={{0,8},{4,12},{24,16},{28,20},{1,9},{5,13},{25,17},{29,21},{2,10},{... | collective-permute-start | bytes 1179656 | tf_op jit(solution)/shard_map/ppermute | solution.py:405
  581.7 21.4 %collective-permute-start.84 = (bf16[512,1536]{1,0:T(8,128)(2,1)}, bf16[512,1536]{1,0:T(8,128)(2,1)}, u32[]{:S(2)}, u32[]{:S(2)}) collective-permute-start(bf16[512,1536]{1,0:T(8,128)(2,1)} %slice.588), channel_id=1, source_target_pairs={{0,1},{1,0},{2,3},{3,2},{4,5},{5,4},{6,7},{7,6},{8,9},{9,8},{10,11... | collective-permute-start | bytes 4718600 | tf_op jit(solution)/shard_map/ppermute | solution.py:409
  583.0 20.1 %collective-permute-start.85 = (bf16[128,1536]{1,0:T(8,128)(2,1)S(1)}, bf16[128,1536]{1,0:T(8,128)(2,1)}, u32[]{:S(2)}, u32[]{:S(2)}) collective-permute-start(bf16[128,1536]{1,0:T(8,128)(2,1)S(1)} %get-tuple-element.353), channel_id=1, source_target_pairs={{0,8},{4,12},{8,0},{12,4},{16,24},{20,28},{24,16},{28,20},{1,9},{5... | collective-permute-start | bytes 1179656 | tf_op jit(solution)/shard_map/ppermute | solution.py:405
  584.3 18.7 %collective-permute-start.86 = (bf16[128,1536]{1,0:T(8,128)(2,1)S(1)}, bf16[128,1536]{1,0:T(8,128)(2,1)}, u32[]{:S(2)}, u32[]{:S(2)}) collective-permute-start(bf16[128,1536]{1,0:T(8,128)(2,1)S(1)} %get-tuple-element.353), channel_id=1, source_target_pairs={{8,16},{12,20},{16,8},{20,12},{9,17},{13,21},{17,9},{21,13},{10,18... | collective-permute-start | bytes 1179656 | tf_op jit(solution)/shard_map/ppermute | solution.py:405
  587.9 21.4 %collective-permute-start.90 = (bf16[512,1536]{1,0:T(8,128)(2,1)}, bf16[512,1536]{1,0:T(8,128)(2,1)}, u32[]{:S(2)}, u32[]{:S(2)}) collective-permute-start(bf16[512,1536]{1,0:T(8,128)(2,1)} %slice.592), channel_id=1, source_target_pairs={{0,1},{1,0},{2,3},{3,2},{4,5},{5,4},{6,7},{7,6},{8,9},{9,8},{10,11... | collective-permute-start | bytes 4718600 | tf_op jit(solution)/shard_map/ppermute | solution.py:409
  603.1 21.1 %collective-permute-start.93 = (bf16[128,1536]{1,0:T(8,128)(2,1)}, bf16[128,1536]{1,0:T(8,128)(2,1)S(1)}, u32[]{:S(2)}, u32[]{:S(2)}) collective-permute-start(bf16[128,1536]{1,0:T(8,128)(2,1)} %collective-permute-done.85), channel_id=1, source_target_pairs={{0,4},{4,0},{8,12},{12,8},{16,20},{20,16},{24,28},{28,24},{1,5},{5... | collective-permute-start | bytes 1179656 | tf_op jit(solution)/shard_map/ppermute | solution.py:405
  625.8 29.1 %collective-permute-start.101 = (bf16[128,1536]{1,0:T(8,128)(2,1)S(1)}, bf16[128,1536]{1,0:T(8,128)(2,1)}, u32[]{:S(2)}, u32[]{:S(2)}) collective-permute-start(bf16[128,1536]{1,0:T(8,128)(2,1)S(1)} %add.954), channel_id=1, source_target_pairs={{0,4},{4,0},{8,12},{12,8},{16,20},{20,16},{24,28},{28,24},{1,5},{5... | collective-permute-start | bytes 1179656 | tf_op jit(solution)/shard_map/ppermute | solution.py:405
  631.6 23.3 %collective-permute-start.100 = (bf16[128,1536]{1,0:T(8,128)(2,1)}, bf16[128,1536]{1,0:T(8,128)(2,1)}, u32[]{:S(2)}, u32[]{:S(2)}) collective-permute-start(bf16[128,1536]{1,0:T(8,128)(2,1)} %collective-permute-done.91), channel_id=1, source_target_pairs={{8,0},{12,4},{16,24},{20,28},{9,1},{13,5},{17,25},{21,29},{10,2},{... | collective-permute-start | bytes 1179656 | tf_op jit(solution)/shard_map/ppermute | solution.py:405
  632.9 22.0 %collective-permute-start.96 = (bf16[128,1536]{1,0:T(8,128)(2,1)}, bf16[128,1536]{1,0:T(8,128)(2,1)}, u32[]{:S(2)}, u32[]{:S(2)}) collective-permute-start(bf16[128,1536]{1,0:T(8,128)(2,1)} %get-tuple-element.525), channel_id=1, source_target_pairs={{0,2},{1,3},{2,0},{3,1},{4,6},{5,7},{6,4},{7,5},{8,10},{9,11},{10,... | collective-permute-start | bytes 1179656 | tf_op jit(solution)/shard_map/ppermute | solution.py:409
  635.4 19.4 %collective-permute-start.97 = (bf16[128,1536]{1,0:T(8,128)(2,1)}, bf16[128,1536]{1,0:T(8,128)(2,1)}, u32[]{:S(2)}, u32[]{:S(2)}) collective-permute-start(bf16[128,1536]{1,0:T(8,128)(2,1)} %get-tuple-element.524), channel_id=1, source_target_pairs={{0,4},{4,0},{8,12},{12,8},{16,20},{20,16},{24,28},{28,24},{1,5},{5... | collective-permute-start | bytes 1179656 | tf_op jit(solution)/shard_map/ppermute | solution.py:405
  661.4 36.5 %collective-permute-start.102 = (bf16[128,1536]{1,0:T(8,128)(2,1)S(1)}, bf16[128,1536]{1,0:T(8,128)(2,1)S(1)}, u32[]{:S(2)}, u32[]{:S(2)}) collective-permute-start(bf16[128,1536]{1,0:T(8,128)(2,1)S(1)} %pad_maximum_fusion.34), channel_id=1, source_target_pairs={{0,8},{4,12},{24,16},{28,20},{1,9},{5,13},{25,17},{29,21},{2,10},{... | collective-permute-start | bytes 1179656 | tf_op jit(solution)/shard_map/ppermute | solution.py:405
  667.9 29.3 %collective-permute-start.107 = (bf16[128,1536]{1,0:T(8,128)(2,1)S(1)}, bf16[128,1536]{1,0:T(8,128)(2,1)S(1)}, u32[]{:S(2)}, u32[]{:S(2)}) collective-permute-start(bf16[128,1536]{1,0:T(8,128)(2,1)S(1)} %add.961), channel_id=1, source_target_pairs={{0,4},{4,0},{8,12},{12,8},{16,20},{20,16},{24,28},{28,24},{1,5},{5... | collective-permute-start | bytes 1179656 | tf_op jit(solution)/shard_map/ppermute | solution.py:405
  668.7 29.2 %collective-permute-start.105 = (bf16[128,1536]{1,0:T(8,128)(2,1)S(1)}, bf16[128,1536]{1,0:T(8,128)(2,1)S(1)}, u32[]{:S(2)}, u32[]{:S(2)}) collective-permute-start(bf16[128,1536]{1,0:T(8,128)(2,1)S(1)} %get-tuple-element.521), channel_id=1, source_target_pairs={{0,2},{1,3},{2,0},{3,1},{4,6},{5,7},{6,4},{7,5},{8,10},{9,11},{10,... | collective-permute-start | bytes 1179656 | tf_op jit(solution)/shard_map/ppermute | solution.py:409
  669.4 28.5 %collective-permute-start.106 = (bf16[128,1536]{1,0:T(8,128)(2,1)S(1)}, bf16[128,1536]{1,0:T(8,128)(2,1)S(1)}, u32[]{:S(2)}, u32[]{:S(2)}) collective-permute-start(bf16[128,1536]{1,0:T(8,128)(2,1)S(1)} %get-tuple-element.520), channel_id=1, source_target_pairs={{0,4},{4,0},{8,12},{12,8},{16,20},{20,16},{24,28},{28,24},{1,5},{5... | collective-permute-start | bytes 1179656 | tf_op jit(solution)/shard_map/ppermute | solution.py:405
  670.7 18.3 %collective-permute-start.103 = (bf16[64,1536]{1,0:T(8,128)(2,1)S(1)}, bf16[64,1536]{1,0:T(8,128)(2,1)S(1)}, u32[]{:S(2)}, u32[]{:S(2)}) collective-permute-start(bf16[64,1536]{1,0:T(8,128)(2,1)S(1)} %slice.713), channel_id=1, source_target_pairs={{0,4},{4,0},{8,12},{12,8},{16,20},{20,16},{24,28},{28,24},{1,5},{5... | collective-permute-start | bytes 589832 | tf_op jit(solution)/shard_map/ppermute | solution.py:405
  696.5 42.4 %collective-permute-start.112 = (bf16[128,1536]{1,0:T(8,128)(2,1)}, bf16[128,1536]{1,0:T(8,128)(2,1)}, u32[]{:S(2)}, u32[]{:S(2)}) collective-permute-start(bf16[128,1536]{1,0:T(8,128)(2,1)} %get-tuple-element.517), channel_id=1, source_target_pairs={{0,2},{1,3},{2,0},{3,1},{4,6},{5,7},{6,4},{7,5},{8,10},{9,11},{10,... | collective-permute-start | bytes 1179656 | tf_op jit(solution)/shard_map/ppermute | solution.py:409
  697.2 46.8 %collective-permute-start.113 = (bf16[128,1536]{1,0:T(8,128)(2,1)}, bf16[128,1536]{1,0:T(8,128)(2,1)}, u32[]{:S(2)}, u32[]{:S(2)}) collective-permute-start(bf16[128,1536]{1,0:T(8,128)(2,1)} %get-tuple-element.516), channel_id=1, source_target_pairs={{0,4},{4,0},{8,12},{12,8},{16,20},{20,16},{24,28},{28,24},{1,5},{5... | collective-permute-start | bytes 1179656 | tf_op jit(solution)/shard_map/ppermute | solution.py:405
  700.8 43.8 %collective-permute-start.109 = (bf16[128,1536]{1,0:T(8,128)(2,1)}, bf16[128,1536]{1,0:T(8,128)(2,1)}, u32[]{:S(2)}, u32[]{:S(2)}) collective-permute-start(bf16[128,1536]{1,0:T(8,128)(2,1)} %pad_maximum_fusion.35), channel_id=1, source_target_pairs={{0,8},{4,12},{24,16},{28,20},{1,9},{5,13},{25,17},{29,21},{2,10},{... | collective-permute-start | bytes 1179656 | tf_op jit(solution)/shard_map/ppermute | solution.py:405
  702.9 41.8 %collective-permute-start.108 = (bf16[128,1536]{1,0:T(8,128)(2,1)}, bf16[128,1536]{1,0:T(8,128)(2,1)}, u32[]{:S(2)}, u32[]{:S(2)}) collective-permute-start(bf16[128,1536]{1,0:T(8,128)(2,1)} %add_convert_fusion.22), channel_id=1, source_target_pairs={{8,16},{12,20},{16,8},{20,12},{9,17},{13,21},{17,9},{21,13},{10,18... | collective-permute-start | bytes 1179656 | tf_op jit(solution)/shard_map/ppermute | solution.py:405
  704.3 132.8 %all-to-all-start.2 = ((bf16[8,192,1280]{2,1,0:T(8,128)(2,1)}), bf16[8,192,1280]{2,1,0:T(8,128)(2,1)}, u32[]{:S(2)}, u32[]{:S(2)}) async-start(bf16[8,192,1280]{2,1,0:T(8,128)(2,1)} %bitcast.183), calls=%async_computation.2 | async-start | bytes 7864320 | tf_op jit(solution)/shard_map/all_to_all | solution.py:1133
  720.5 23.4 %collective-permute-start.110 = (bf16[64,1536]{1,0:T(8,128)(2,1)}, bf16[64,1536]{1,0:T(8,128)(2,1)}, u32[]{:S(2)}, u32[]{:S(2)}) collective-permute-start(bf16[64,1536]{1,0:T(8,128)(2,1)} %slice.721), channel_id=1, source_target_pairs={{0,4},{4,0},{8,12},{12,8},{16,20},{20,16},{24,28},{28,24},{1,5},{5... | collective-permute-start | bytes 589832 | tf_op jit(solution)/shard_map/ppermute | solution.py:405
  747.6 38.2 %collective-permute-start.115 = (bf16[128,1536]{1,0:T(8,128)(2,1)}, bf16[128,1536]{1,0:T(8,128)(2,1)}, u32[]{:S(2)}, u32[]{:S(2)}) collective-permute-start(bf16[128,1536]{1,0:T(8,128)(2,1)} %add_convert_fusion.17), channel_id=1, source_target_pairs={{8,16},{12,20},{16,8},{20,12},{9,17},{13,21},{17,9},{21,13},{10,18... | collective-permute-start | bytes 1179656 | tf_op jit(solution)/shard_map/ppermute | solution.py:405
  750.9 34.9 %collective-permute-start.114 = (bf16[128,1536]{1,0:T(8,128)(2,1)}, bf16[128,1536]{1,0:T(8,128)(2,1)}, u32[]{:S(2)}, u32[]{:S(2)}) collective-permute-start(bf16[128,1536]{1,0:T(8,128)(2,1)} %add_convert_fusion.18), channel_id=1, source_target_pairs={{0,8},{4,12},{8,0},{12,4},{16,24},{20,28},{24,16},{28,20},{1,9},{5... | collective-permute-start | bytes 1179656 | tf_op jit(solution)/shard_map/ppermute | solution.py:405
  792.7 34.1 %collective-permute-start.121 = (bf16[128,1536]{1,0:T(8,128)(2,1)S(1)}, bf16[128,1536]{1,0:T(8,128)(2,1)S(1)}, u32[]{:S(2)}, u32[]{:S(2)}) collective-permute-start(bf16[128,1536]{1,0:T(8,128)(2,1)S(1)} %get-tuple-element.501), channel_id=1, source_target_pairs={{0,4},{4,0},{8,12},{12,8},{16,20},{20,16},{24,28},{28,24},{1,5},{5... | collective-permute-start | bytes 1179656 | tf_op jit(solution)/shard_map/ppermute | solution.py:405
  793.3 75.8 %collective-permute-start.125 = (bf16[128,1536]{1,0:T(8,128)(2,1)}, bf16[128,1536]{1,0:T(8,128)(2,1)}, u32[]{:S(2)}, u32[]{:S(2)}) collective-permute-start(bf16[128,1536]{1,0:T(8,128)(2,1)} %get-tuple-element.500), channel_id=1, source_target_pairs={{0,4},{4,0},{8,12},{12,8},{16,20},{20,16},{24,28},{28,24},{1,5},{5... | collective-permute-start | bytes 1179656 | tf_op jit(solution)/shard_map/ppermute | solution.py:405
  794.8 89.6 %collective-permute-start.128 = (bf16[128,1536]{1,0:T(8,128)(2,1)}, bf16[128,1536]{1,0:T(8,128)(2,1)S(1)}, u32[]{:S(2)}, u32[]{:S(2)}) collective-permute-start(bf16[128,1536]{1,0:T(8,128)(2,1)} %get-tuple-element.499), channel_id=1, source_target_pairs={{0,4},{4,0},{8,12},{12,8},{16,20},{20,16},{24,28},{28,24},{1,5},{5... | collective-permute-start | bytes 1179656 | tf_op jit(solution)/shard_map/ppermute | solution.py:405
  803.4 27.5 %collective-permute-start.122 = (bf16[8,48,640]{2,1,0:T(8,128)(2,1)S(1)}, bf16[8,48,640]{2,1,0:T(8,128)(2,1)S(1)}, u32[]{:S(2)}, u32[]{:S(2)}) collective-permute-start(bf16[8,48,640]{2,1,0:T(8,128)(2,1)S(1)} %fusion.13), channel_id=1, source_target_pairs={{0,2},{1,3},{2,0},{3,1},{4,6},{5,7},{6,4},{7,5},{8,10},{9,11},{10,... | collective-permute-start | bytes 1474568 | tf_op jit(solution)/shard_map/ppermute | solution.py:409
  804.2 26.7 %collective-permute-start.120 = (bf16[128,1536]{1,0:T(8,128)(2,1)S(1)}, bf16[128,1536]{1,0:T(8,128)(2,1)S(1)}, u32[]{:S(2)}, u32[]{:S(2)}) collective-permute-start(bf16[128,1536]{1,0:T(8,128)(2,1)S(1)} %add_convert_fusion.15), channel_id=1, source_target_pairs={{0,8},{4,12},{24,16},{28,20},{1,9},{5,13},{25,17},{29,21},{2,10},{... | collective-permute-start | bytes 1179656 | tf_op jit(solution)/shard_map/ppermute | solution.py:405
  831.7 37.4 %collective-permute-start.124 = (bf16[128,1536]{1,0:T(8,128)(2,1)S(1)}, bf16[128,1536]{1,0:T(8,128)(2,1)S(1)}, u32[]{:S(2)}, u32[]{:S(2)}) collective-permute-start(bf16[128,1536]{1,0:T(8,128)(2,1)S(1)} %add_convert_fusion.13), channel_id=1, source_target_pairs={{0,8},{4,12},{24,16},{28,20},{1,9},{5,13},{25,17},{29,21},{2,10},{... | collective-permute-start | bytes 1179656 | tf_op jit(solution)/shard_map/ppermute | solution.py:405
  837.1 32.0 %all-to-all-start.3 = ((bf16[8,48,640]{2,1,0:T(8,128)(2,1)}), bf16[8,48,640]{2,1,0:T(8,128)(2,1)S(1)}, u32[]{:S(2)}, u32[]{:S(2)}) async-start(bf16[8,48,640]{2,1,0:T(8,128)(2,1)} %fusion.12), calls=%async_computation.3 | async-start | bytes 983040 | tf_op jit(solution)/shard_map/all_to_all | solution.py:1154
  841.8 27.2 %collective-permute-start.123 = (bf16[128,1536]{1,0:T(8,128)(2,1)S(1)}, bf16[128,1536]{1,0:T(8,128)(2,1)S(1)}, u32[]{:S(2)}, u32[]{:S(2)}) collective-permute-start(bf16[128,1536]{1,0:T(8,128)(2,1)S(1)} %add_convert_fusion.14), channel_id=1, source_target_pairs={{8,16},{12,20},{16,8},{20,12},{9,17},{13,21},{17,9},{21,13},{10,18... | collective-permute-start | bytes 1179656 | tf_op jit(solution)/shard_map/ppermute | solution.py:405
  (179 other events, 2002.4 us)
where the time goes:
time: 902 us; the launch traced here: 890 us
  starting transfers between devices  205 us (23%)
  waiting for transfers between devices  193 us (21%)
  local copies, waits for them, and re-layouts  159 us (18%)
  matrix products  150 us (17%)
  other arithmetic  139 us (15%)
  Pallas kernels  40.1 us (4%)
    ppermute x84, starting transfers between devices, over_dp(): return lax.ppermute(piece, 'dp', moves)  150 us
    ppermute x84, waiting for transfers between devices, over_dp(): return lax.ppermute(piece, 'dp', moves)  78.5 us
    unnamed x281, local copies, waits for them, and re-layouts  63.1 us
    all_to_all x1, waiting for transfers between devices, per_device(): lax.all_to_all(after(in_out, group_tokens, attn_in), 'dp', split_axis=0,...  60 us
    ppermute x45, waiting for transfers between devices, over_expert(): return lax.ppermute(piece, 'expert', moves)  54.1 us
    ppermute x45, starting transfers between devices, over_expert(): return lax.ppermute(piece, 'expert', moves)  37.2 us
    convert_element_type x50, other arithmetic, added(): return total.astype(jnp.bfloat16)  34.2 us
    dot_general x4, matrix products, work(): lax.dot_general(tie(sent_slots[n]), grad_slots[n], ROWS_DIMS, preferred_e...  31.4 us
  transfers between devices with their start and end apart: 133, of which 31 were waited for; matrix products, arithmetic and copies ran while one was open for 46% of the time, Pallas kernels for 5%

commit v1 on v0

--- a/solution.py
+++ b/solution.py
@@ -444,17 +444,24 @@
 
 
 def dp_gather(piece, covers=(None, None, None, None)):
-    (near, middle, y0), work1 = one_round(
+    works = []
+
+    def run(outs, ins, cover):
+        outs, work = one_round(outs, ins, cover and (lambda tie: cover(tie, works)))
+        works.append(work)
+        return outs
+
+    near, middle, y0 = run(
         (over_dp(piece, Z_NEAR), over_dp(piece, Z_MIDDLE), swap_y(piece)), (piece,), covers[0]
     )
-    (far, out1, y1), work2 = one_round(
+    far, out1, y1 = run(
         (over_dp(near, Z_MIDDLE), over_dp(middle, Z_OUT), swap_y(near)), (near, middle), covers[1]
     )
     third = middle + out1
-    (out2, y2), work3 = one_round((over_dp(far, Z_OUT), swap_y(third)), (far, third), covers[2])
+    out2, y2 = run((over_dp(far, Z_OUT), swap_y(third)), (far, third), covers[2])
     fourth = far + out2
-    y3, work4 = one_round(swap_y(fourth), (fourth,), covers[3])
-    return joined(piece, y0, near, y1, third, y2, fourth, y3), (work1, work2, work3, work4)
+    y3 = run(swap_y(fourth), (fourth,), covers[3])
+    return joined(piece, y0, near, y1, third, y2, fourth, y3), works
 
 
 class DpScatter:
@@ -498,26 +505,31 @@
         return total
 
 
-def gather_beside_sum(piece, project, mix):
-    (near, middle), projected = one_round(
-        (over_dp(piece, Z_NEAR), over_dp(piece, Z_MIDDLE)), (piece,), project
-    )
-    (far, out1, y0), (mixed, part) = one_round(
-        (over_dp(near, Z_MIDDLE), over_dp(middle, Z_OUT), swap_y(piece)),
-        (near, middle),
-        lambda tie: mix(tie, projected),
-    )
-    third = middle + out1
+def gather_beside_sum(piece, attention):
+    (near, middle, y0), attended = one_round(
+        (over_dp(piece, Z_NEAR), over_dp(piece, Z_MIDDLE), swap_y(piece)), (piece,), attention
+    )
+    part = attended[-1]
     pair0 = joined(piece, y0)
     total = DpScatter(part)
-    (out2, y1, x0, sums), _ = one_round(
-        (over_dp(far, Z_OUT), swap_y(near), swap_x(pair0), total.step()), (far, pair0)
+    (far, out1, y1, x0, sums), _ = one_round(
+        (
+            over_dp(near, Z_MIDDLE),
+            over_dp(middle, Z_OUT),
+            swap_y(near),
+            swap_x(pair0),
+            total.step(),
+        ),
+        (near, middle, pair0),
+    )
+    total.keep(sums)
+    third = middle + out1
+    pair1 = joined(near, y1)
+    (out2, y2, x1, sums), _ = one_round(
+        (over_dp(far, Z_OUT), swap_y(third), swap_x(pair1), total.step()), (far, third, pair1)
     )
     total.keep(sums)
     fourth = far + out2
-    pair1 = joined(near, y1)
-    (y2, x1, sums), _ = one_round((swap_y(third), swap_x(pair1), total.step()), (third, pair1))
-    total.keep(sums)
     pair2 = joined(third, y2)
     (y3, x2, sums), _ = one_round((swap_y(fourth), swap_x(pair2), total.step()), (fourth, pair2))
     total.keep(sums)
@@ -525,102 +537,120 @@
     (x3, sums), _ = one_round((swap_x(pair3), total.step()), (pair3,))
     total.keep(sums)
     here = joined(pair0, x0, pair1, x1, pair2, x2, pair3, x3)
-    return joined(here, swap_core(here)), total.total(), (projected, mixed)
-
-
-def gather_slots(piece, covers):
-    y, x, core = swap_y, swap_x, swap_core
-    t0, l0 = halves(piece)
-    outs = over_dp(piece, Z_NEAR), over_dp(piece, Z_MIDDLE), y(t0), x(l0)
-    (near, middle, yt0, xl0), _ = one_round(outs, (piece,))
-    t1, l1 = halves(near)
-    top0, low0 = joined(t0, yt0), joined(l0, xl0)
-    outs = over_dp(near, Z_MIDDLE), over_dp(middle, Z_OUT), x(top0), y(low0), y(t1), x(l1)
-    (far, out1, xt0, yl0, yt1, xl1), work2 = one_round(outs, (top0, low0), covers[0])
-    third = middle + out1
-    t2, l2 = halves(third)
-    top1, low1, here0 = joined(t1, yt1), joined(l1, xl1), joined(top0, xt0, low0, yl0)
-    outs = over_dp(far, Z_OUT), x(top1), y(low1), y(t2), x(l2), core(here0)
-    (out2, xt1, yl1, yt2, xl2, core0), work3 = one_round(outs, (top1, low1), covers[1])
-    fourth = far + out2
-    t3, l3 = halves(fourth)
-    slot0 = joined(here0, core0)
-    top2, low2, here1 = joined(t2, yt2), joined(l2, xl2), joined(top1, xt1, low1, yl1)
-    outs = x(top2), y(low2), y(t3), x(l3), core(here1)
-    (xt2, yl2, yt3, xl3, core1), work4 = one_round(
-        outs, (top2, low2), lambda tie: covers[2](tie, slot0)
-    )
-    slot1 = joined(here1, core1)
-    top3, low3, here2 = joined(t3, yt3), joined(l3, xl3), joined(top2, xt2, low2, yl2)
-    outs = x(top3), y(low3), core(here2)
-    (xt3, yl3, core2), work5 = one_round(outs, (top3, low3), lambda tie: covers[2](tie, slot1))
-    slot2 = joined(here2, core2)
-    here3 = joined(top3, xt3, low3, yl3)
-    core3, work6 = one_round(core(here3), (here3,), lambda tie: covers[2](tie, slot2))
-    slot3 = joined(here3, core3)
-    return [slot0, slot1, slot2, slot3], [work4, work5, work6], (work2, work3)
-
-
-def scatter_slots(totals, covers):
-    y, x, core = swap_y, swap_x, swap_core
-
-    def big(here):
-        top, low = halves(here)
-        (ta, tb), (la, lb) = halves(top), halves(low)
-        return (ta, la), (x(tb), y(lb))
-
-    def small(top, low):
-        (ta, tb), (la, lb) = halves(top), halves(low)
-        return (ta, la), (y(tb), x(lb))
-
+    return joined(here, swap_core(here)), total.total(), attended
+
+
+def gather_pairs(piece, covers):
     works = []
 
-    def run(outs, ins, cover):
+    def run(outs, ins, cover=None):
         outs, work = one_round(outs, ins, cover and (lambda tie: cover(tie, works)))
         works.append(work)
         return outs
 
-    (m0, o0), (m1, o1), (m2, o2), (m3, o3) = [halves(t) for t in totals]
-    c3 = run(core(o3), (o3,), covers[0])
-    h3 = added(m3, c3)
-    k3, b3 = big(h3)
-    (b3, c2) = run((b3, core(o2)), (h3,), covers[1])
-    p3 = [added(k, v) for k, v in zip(k3, b3)]
-    h2 = added(m2, c2)
-    k2, b2 = big(h2)
-    s3, a3 = small(*p3)
-    (a3, b2, c1, c0) = run((a3, b2, core(o1), core(o0)), (h2, *p3), covers[2])
-    fourth = joined(*[added(k, v) for k, v in zip(s3, a3)])
-    p2 = [added(k, v) for k, v in zip(k2, b2)]
-    h1, h0 = added(m1, c1), added(m0, c0)
-    k1, b1 = big(h1)
-    s2, a2 = small(*p2)
-    (z3, a2, b1) = run(
-        (over_dp(fourth, Z_IN), a2, b1), (fourth, h1, *p2), covers[3]
-    )
-    fourth = added(fourth, z3)
-    third = joined(*[added(k, v) for k, v in zip(s2, a2)])
-    p1 = [added(k, v) for k, v in zip(k1, b1)]
-    k0, b0 = big(h0)
-    s1, a1 = small(*p1)
-    (z3, z2, a1, b0) = run(
-        (over_dp(fourth, Z_MIDDLE), over_dp(third, Z_IN), a1, b0), (fourth, third, *p1), covers[4]
-    )
-    third = added(third, z2)
-    near = added(joined(*[added(k, v) for k, v in zip(s1, a1)]), z3)
-    p0 = [added(k, v) for k, v in zip(k0, b0)]
-    s0, a0 = small(*p0)
-    (z1, z2, a0) = run(
-        (over_dp(near, Z_NEAR), over_dp(third, Z_MIDDLE), a0), (near, third, *p0), covers[5]
-    )
-    own = joined(*[added(k, v) for k, v in zip(s0, a0)])
-    total = own.astype(jnp.float32) + z1.astype(jnp.float32) + z2.astype(jnp.float32)
-    return total, works
+    near, middle = run((over_dp(piece, Z_NEAR), over_dp(piece, Z_MIDDLE)), (piece,))
+
+    def split(first, second):
+        (ft, fl), (st, sl) = halves(first), halves(second)
+        return joined(ft, st), joined(fl, sl)
+
+    top, low = split(piece, near)
+    far, out1, y_top, x_low = run(
+        (over_dp(near, Z_MIDDLE), over_dp(middle, Z_OUT), swap_y(top), swap_x(low)),
+        (top, low),
+        covers[0],
+    )
+    third = middle + out1
+    top, low = joined(top, y_top), joined(low, x_low)
+    out2, x_top, y_low = run(
+        (over_dp(far, Z_OUT), swap_x(top), swap_y(low)), (top, low), covers[1]
+    )
+    here = joined(top, x_top, low, y_low)
+    top, low = split(third, far + out2)
+    y_top, x_low, there = run(
+        (swap_y(top), swap_x(low), swap_core(here)), (top, low, here), covers[2]
+    )
+    first = joined(here, there)
+    top, low = joined(top, y_top), joined(low, x_low)
+    x_top, y_low = run(
+        (swap_x(top), swap_y(low)), (top, low), lambda tie, works: covers[3](tie, works, first)
+    )
+    here = joined(top, x_top, low, y_low)
+    there = run(swap_core(here), (here,), covers[4])
+    return (first, joined(here, there)), works
+
+
+class PairScatter:
+    def __init__(self, totals):
+        (self.m0, self.o0), (self.m1, self.o1) = [halves(t) for t in totals]
+        self.round = 0
+
+    def across(self, parts, first, second, tie):
+        (ta, tb), (la, lb) = [halves(p) for p in parts]
+        return (ta, la), (first(tie(tb)), second(tie(lb)))
+
+    def both(self, kept, moved):
+        return [added(k, m) for k, m in zip(kept, moved)]
+
+    def step(self, tie=lambda v: v):
+        self.round += 1
+        if self.round == 1:
+            self.moved = swap_core(tie(self.o1))
+        elif self.round == 2:
+            parts = halves(added(self.m1, self.moved))
+            self.kept1, moved1 = self.across(parts, swap_x, swap_y, tie)
+            self.moved = moved1, swap_core(tie(self.o0))
+        elif self.round == 3:
+            parts1 = self.both(self.kept1, self.moved[0])
+            parts0 = halves(added(self.m0, self.moved[1]))
+            self.kept1, moved1 = self.across(parts1, swap_y, swap_x, tie)
+            self.kept0, moved0 = self.across(parts0, swap_x, swap_y, tie)
+            self.moved = moved1, moved0
+        elif self.round == 4:
+            (third_top, fourth_top), (third_low, fourth_low) = [
+                halves(p) for p in self.both(self.kept1, self.moved[0])
+            ]
+            self.third, self.fourth = joined(third_top, third_low), joined(fourth_top, fourth_low)
+            parts0 = self.both(self.kept0, self.moved[1])
+            self.kept0, moved0 = self.across(parts0, swap_y, swap_x, tie)
+            self.moved = moved0, over_dp(tie(self.fourth), Z_IN)
+        elif self.round == 5:
+            (own_top, near_top), (own_low, near_low) = [
+                halves(p) for p in self.both(self.kept0, self.moved[0])
+            ]
+            self.own, self.near = joined(own_top, own_low), joined(near_top, near_low)
+            fourth = added(self.fourth, self.moved[1])
+            self.moved = over_dp(tie(fourth), Z_MIDDLE), over_dp(tie(self.third), Z_IN)
+        else:
+            near, third = added(self.near, self.moved[0]), added(self.third, self.moved[1])
+            self.moved = over_dp(tie(near), Z_NEAR), over_dp(tie(third), Z_MIDDLE)
+        return self.moved
+
+    def keep(self, values):
+        self.moved = values
+
+    def total(self):
+        total = self.own.astype(jnp.float32)
+        for value in self.moved:
+            total = total + value.astype(jnp.float32)
+        return total
+
+
+def scatter_pairs(totals, covers):
+    works = []
+    scatter = PairScatter(totals)
+    for cover in covers:
+        outs = scatter.step()
+        outs, work = one_round(outs, (), cover and (lambda tie: cover(tie, works)))
+        scatter.keep(outs)
+        works.append(work)
+    return scatter.total(), works
 
 
 def far_order(ex_index, dealt_of):
     r = jnp.arange(64, dtype=jnp.int32)
-    slot, core, half, outer, inner = r // 16, r // 8 % 2, r // 4 % 2, r // 2 % 2, r % 2
+    pair, core, half, outer, inner = r // 32, r // 16 % 2, r // 8 % 2, r // 4 % 2, r // 2 % 2
+    slot = 2 * pair + r % 2
     flip_y = jnp.where(half == 0, inner, outer)
     flip_x = jnp.where(half == 0, outer, inner)
 
@@ -676,119 +706,169 @@
     return (seq_rows == col_ids[0:1, :]) & (col_ids[1:2, :] <= place_rows)
 
 
-def attend_kernel(q_ref, k_ref, v_ref, row_ids, col_ids, o_ref, top_ref, total_ref, *, heads, rows):
-    for kv in range(k_ref.shape[1] // HD):
-        keys = k_ref[:, kv * HD : (kv + 1) * HD]
-        vals = v_ref[:, kv * HD : (kv + 1) * HD]
-
-        def step(i, carry):
-            begin = pl.multiple_of(i * rows, rows)
-            allowed = attend_masks(row_ids, col_ids, begin, rows)
-            outs, tops, totals = [], [], []
-            for h in range(heads):
-                at = (kv * heads + h) * HD
-                scores = SCORE_SCALE * lax.dot_general(
-                    q_ref[pl.ds(begin, rows), at : at + HD],
-                    keys,
-                    COLS_DIMS,
-                    preferred_element_type=jnp.float32,
-                )
-                scores = jnp.where(allowed, scores, NEGATIVE)
-                top = jnp.max(scores, axis=-1, keepdims=True)
-                weights = jnp.exp(scores - top)
-                total = jnp.sum(weights, axis=-1, keepdims=True)
-                chances = (weights / total).astype(jnp.bfloat16)
-                outs.append(jnp.dot(chances, vals, preferred_element_type=jnp.float32))
-                tops.append(top)
-                totals.append(total)
-            begin_at = kv * heads
-            o_ref[pl.ds(begin, rows), begin_at * HD : (begin_at + heads) * HD] = jnp.concatenate(
-                outs, axis=1
-            ).astype(jnp.bfloat16)
-            top_ref[pl.ds(begin, rows), begin_at : begin_at + heads] = jnp.concatenate(tops, axis=1)
-            total_ref[pl.ds(begin, rows), begin_at : begin_at + heads] = jnp.concatenate(
-                totals, axis=1
+def front_kernel(
+    x_ref, gain_ref, w_ref, ow_ref, cos_ref, sin_ref, row_ids, col_ids,
+    normed_ref, q_ref, k_ref, v_ref, o_ref, top_ref, total_ref, part_ref, *, heads, rows
+):
+    q_cols = heads * HD
+    steps = x_ref.shape[0] // rows
+
+    def project(i, carry):
+        here = pl.ds(pl.multiple_of(i * rows, rows), rows)
+        inputs = x_ref[here, :].astype(jnp.float32)
+        scale = lax.rsqrt(jnp.mean(inputs * inputs, axis=-1, keepdims=True) + EPSILON)
+        normed = (inputs * scale * gain_ref[...]).astype(jnp.bfloat16)
+        normed_ref[here, :] = normed
+        qkv = jnp.dot(normed, w_ref[...], preferred_element_type=jnp.float32)
+        cosine, sine = cos_ref[here, :], sin_ref[here, :]
+        turned = []
+        for h in range(heads + 1):
+            turned.append(rotate(qkv[:, h * HD : (h + 1) * HD], cosine, sine))
+        q_ref[here, :] = jnp.concatenate(turned[:heads], axis=1).astype(jnp.bfloat16)
+        k_ref[here, :] = turned[heads].astype(jnp.bfloat16)
+        v_ref[here, :] = qkv[:, q_cols + HD :].astype(jnp.bfloat16)
+        return carry
+
+    lax.fori_loop(0, steps, project, 0)
+    keys, vals = k_ref[...], v_ref[...]
+
+    def step(i, carry):
+        begin = pl.multiple_of(i * rows, rows)
+        here = pl.ds(begin, rows)
+        allowed = attend_masks(row_ids, col_ids, begin, rows)
+        outs, tops, totals = [], [], []
+        for h in range(heads):
+            scores = SCORE_SCALE * lax.dot_general(
+                q_ref[here, h * HD : (h + 1) * HD],
+                keys,
+                COLS_DIMS,
+                preferred_element_type=jnp.float32,
             )
-            return carry
-
-        lax.fori_loop(0, q_ref.shape[0] // rows, step, 0)
-
-
-def attend(queries, keys, vals, row_ids, col_ids):
-    rows = queries.shape[0]
-    heads = queries.shape[1] // HD
+            scores = jnp.where(allowed, scores, NEGATIVE)
+            top = jnp.max(scores, axis=-1, keepdims=True)
+            weights = jnp.exp(scores - top)
+            total = jnp.sum(weights, axis=-1, keepdims=True)
+            chances = (weights / total).astype(jnp.bfloat16)
+            outs.append(jnp.dot(chances, vals, preferred_element_type=jnp.float32))
+            tops.append(top)
+            totals.append(total)
+        mixed = jnp.concatenate(outs, axis=1).astype(jnp.bfloat16)
+        o_ref[here, :] = mixed
+        top_ref[here, :] = jnp.concatenate(tops, axis=1)
+        total_ref[here, :] = jnp.concatenate(totals, axis=1)
+        part_ref[here, :] = lax.dot_general(
+            mixed, ow_ref[...], COLS_DIMS, preferred_element_type=jnp.float32
+        ).astype(jnp.bfloat16)
+        return carry
+
+    lax.fori_loop(0, steps, step, 0)
+
+
+def front(inputs, gain, qkv_w, o_w, cosine, sine, row_ids, col_ids):
+    rows, model = inputs.shape
+    heads = H // KVH
+    low = jnp.bfloat16
     return pl.pallas_call(
-        functools.partial(attend_kernel, heads=H // KVH, rows=min(256, rows)),
+        functools.partial(front_kernel, heads=heads, rows=min(256, rows)),
         out_shape=[
-            jax.ShapeDtypeStruct(queries.shape, jnp.bfloat16),
+            jax.ShapeDtypeStruct((rows, model), low),
+            jax.ShapeDtypeStruct((rows, heads * HD), low),
+            jax.ShapeDtypeStruct((rows, HD), low),
+            jax.ShapeDtypeStruct((rows, HD), low),
+            jax.ShapeDtypeStruct((rows, heads * HD), low),
             jax.ShapeDtypeStruct((rows, heads), jnp.float32),
             jax.ShapeDtypeStruct((rows, heads), jnp.float32),
+            jax.ShapeDtypeStruct((rows, model), low),
         ],
-        name="attend",
-    )(queries, keys, vals, row_ids, col_ids)
-
-
-def attend_back_kernel(
-    q_ref, k_ref, v_ref, g_ref, top_ref, total_ref, row_ids, col_ids, dq_ref, dk_ref, dv_ref, *, heads, rows
+        name="front",
+    )(inputs, gain, qkv_w, o_w, cosine, sine, row_ids, col_ids)
+
+
+def rear_kernel(
+    g_ref, ow_ref, q_ref, k_ref, v_ref, top_ref, total_ref, row_ids, col_ids, cos_ref, sin_ref,
+    w_ref, x_ref, qkvg_ref, part_ref, gain_ref, dk_ref, dv_ref, *, heads, rows
 ):
+    q_cols = heads * HD
+    steps = x_ref.shape[0] // rows
     dk_ref[...] = jnp.zeros_like(dk_ref)
     dv_ref[...] = jnp.zeros_like(dv_ref)
-    for kv in range(k_ref.shape[1] // HD):
-        cols = slice(kv * HD, (kv + 1) * HD)
-        keys = k_ref[:, cols]
-        vals = v_ref[:, cols]
-
-        def step(i, carry):
-            begin = pl.multiple_of(i * rows, rows)
-            allowed = attend_masks(row_ids, col_ids, begin, rows)
-            pulled = []
-            key_grad = jnp.zeros((k_ref.shape[0], HD), jnp.float32)
-            value_grad = jnp.zeros((k_ref.shape[0], HD), jnp.float32)
-            for h in range(heads):
-                head = kv * heads + h
-                query = q_ref[pl.ds(begin, rows), head * HD : (head + 1) * HD]
-                grad = g_ref[pl.ds(begin, rows), head * HD : (head + 1) * HD]
-                scores = SCORE_SCALE * lax.dot_general(
-                    query, keys, COLS_DIMS, preferred_element_type=jnp.float32
-                )
-                scores = jnp.where(allowed, scores, NEGATIVE)
-                weights = jnp.exp(scores - top_ref[pl.ds(begin, rows), head : head + 1])
-                chances = weights / total_ref[pl.ds(begin, rows), head : head + 1]
-                prob_grad = lax.dot_general(
-                    grad, vals, COLS_DIMS, preferred_element_type=jnp.float32
-                )
-                delta = jnp.sum(chances * prob_grad, axis=-1, keepdims=True)
-                score_grad = (chances * (prob_grad - delta)).astype(jnp.bfloat16)
-                pulled.append(
-                    SCORE_SCALE * jnp.dot(score_grad, keys, preferred_element_type=jnp.float32)
-                )
-                key_grad += lax.dot_general(
-                    score_grad, query, ROWS_DIMS, preferred_element_type=jnp.float32
-                )
-                value_grad += lax.dot_general(
-                    chances.astype(jnp.bfloat16), grad, ROWS_DIMS, preferred_element_type=jnp.float32
-                )
-            dq_ref[pl.ds(begin, rows), kv * heads * HD : (kv + 1) * heads * HD] = jnp.concatenate(
-                pulled, axis=1
+    gain_ref[...] = jnp.zeros_like(gain_ref)
+    keys, vals = k_ref[...], v_ref[...]
+
+    def step(i, carry):
+        begin = pl.multiple_of(i * rows, rows)
+        here = pl.ds(begin, rows)
+        allowed = attend_masks(row_ids, col_ids, begin, rows)
+        grads = jnp.dot(g_ref[here, :], ow_ref[...], preferred_element_type=jnp.float32).astype(
+            jnp.bfloat16
+        )
+        cosine, sine = cos_ref[here, :], sin_ref[here, :]
+        pulled = []
+        key_grad = jnp.zeros((k_ref.shape[0], HD), jnp.float32)
+        value_grad = jnp.zeros((k_ref.shape[0], HD), jnp.float32)
+        for h in range(heads):
+            query = q_ref[here, h * HD : (h + 1) * HD]
+            grad = grads[:, h * HD : (h + 1) * HD]
+            scores = SCORE_SCALE * lax.dot_general(
+                query, keys, COLS_DIMS, preferred_element_type=jnp.float32
             )
-            dk_ref[:, cols] += SCORE_SCALE * key_grad
-            dv_ref[:, cols] += value_grad
-            return carry
-
-        lax.fori_loop(0, q_ref.shape[0] // rows, step, 0)
-
-
-def attend_back(queries, keys, vals, grads_in, top, total, row_ids, col_ids):
-    rows = queries.shape[0]
+            scores = jnp.where(allowed, scores, NEGATIVE)
+            weights = jnp.exp(scores - top_ref[here, h : h + 1])
+            chances = weights / total_ref[here, h : h + 1]
+            prob_grad = lax.dot_general(grad, vals, COLS_DIMS, preferred_element_type=jnp.float32)
+            delta = jnp.sum(chances * prob_grad, axis=-1, keepdims=True)
+            score_grad = (chances * (prob_grad - delta)).astype(jnp.bfloat16)
+            query_grad = SCORE_SCALE * jnp.dot(
+                score_grad, keys, preferred_element_type=jnp.float32
+            )
+            pulled.append(turn_back(query_grad, cosine, sine))
+            key_grad += lax.dot_general(
+                score_grad, query, ROWS_DIMS, preferred_element_type=jnp.float32
+            )
+            value_grad += lax.dot_general(
+                chances.astype(jnp.bfloat16), grad, ROWS_DIMS, preferred_element_type=jnp.float32
+            )
+        qkvg_ref[here, 0:q_cols] = jnp.concatenate(pulled, axis=1).astype(jnp.bfloat16)
+        dk_ref[...] += SCORE_SCALE * key_grad
+        dv_ref[...] += value_grad
+        return carry
+
+    lax.fori_loop(0, steps, step, 0)
+
+    def finish(i, carry):
+        here = pl.ds(pl.multiple_of(i * rows, rows), rows)
+        key_low = turn_back(dk_ref[here, :], cos_ref[here, :], sin_ref[here, :])
+        qkvg_ref[here, q_cols:] = jnp.concatenate([key_low, dv_ref[here, :]], axis=1).astype(
+            jnp.bfloat16
+        )
+        part = lax.dot_general(
+            qkvg_ref[here, :], w_ref[...], COLS_DIMS, preferred_element_type=jnp.float32
+        )
+        part_ref[here, :] = part.astype(jnp.bfloat16)
+        inputs = x_ref[here, :].astype(jnp.float32)
+        scale = lax.rsqrt(jnp.mean(inputs * inputs, axis=-1, keepdims=True) + EPSILON)
+        gain_ref[...] += jnp.sum(part * inputs * scale, axis=0, keepdims=True)
+        return carry
+
+    lax.fori_loop(0, steps, finish, 0)
+
+
+def rear(grads_in, o_w, queries, keys, vals, top, total, row_ids, col_ids, cosine, sine, qkv_w, x):
+    rows, model = x.shape
+    heads = H // KVH
     return pl.pallas_call(
-        functools.partial(attend_back_kernel, heads=H // KVH, rows=min(256, rows)),
+        functools.partial(rear_kernel, heads=heads, rows=min(256, rows)),
         out_shape=[
-            jax.ShapeDtypeStruct(queries.shape, jnp.float32),
-            jax.ShapeDtypeStruct(keys.shape, jnp.float32),
-            jax.ShapeDtypeStruct(keys.shape, jnp.float32),
+            jax.ShapeDtypeStruct((rows, qkv_w.shape[1]), jnp.bfloat16),
+            jax.ShapeDtypeStruct((rows, model), jnp.bfloat16),
+            jax.ShapeDtypeStruct((1, model), jnp.float32),
         ],
-        name="attend_back",
-    )(queries, keys, vals, grads_in, top, total, row_ids, col_ids)
+        scratch_shapes=[
+            pltpu.VMEM((rows, HD), jnp.float32),
+            pltpu.VMEM((rows, HD), jnp.float32),
+        ],
+        name="rear",
+    )(grads_in, o_w, queries, keys, vals, top, total, row_ids, col_ids, cosine, sine, qkv_w, x)
 
 
 def after(value, *earlier):
@@ -831,7 +911,6 @@
     n_ex = lax.axis_size("expert")
     tok_rows = tokens.shape[1]
     model = tokens.shape[2]
-    group_rows = tok_rows * n_dp
     kv_here = KVH // n_dp
     heads_per = H // KVH
     q_cols = kv_here * heads_per * HD
@@ -859,6 +938,7 @@
         ],
         axis=1,
     )
+    d_rows = in_weight.shape[0]
 
     def pack_in(tie):
         return (
@@ -881,7 +961,9 @@
     ).transpose(1, 0, 2)
     attn_in = lax.all_to_all(attn_out, "dp", split_axis=0, concat_axis=0, tiled=True)
 
-    group_tokens, (_, in_out, _, _) = dp_gather(tokens[0], (None, pack_in, None, None))
+    group_tokens, (_, in_out, _, _) = dp_gather(
+        tokens[0], (None, lambda tie, works: pack_in(tie), None, None)
+    )
     attn_two = jnp.stack([attn_in, swap_core(attn_in)])
     attn_four = joined(attn_two, swap_x(attn_two))
     in_w = lax.all_to_all(
@@ -929,41 +1011,18 @@
     ).astype(jnp.bfloat16)
 
     seq_ids, cosine, sine_table = rope_parts(seq_lengths, places)
-    group_inputs = group_tokens.astype(jnp.float32)
-    first_scale = lax.rsqrt(jnp.mean(group_inputs * group_inputs, axis=-1, keepdims=True) + EPSILON)
+    cosine, sine_table = cosine[:, 0], sine_table[:, 0]
     row_ids = jnp.stack([seq_ids, places], axis=1)
     col_ids = jnp.stack([seq_ids, places], axis=0)
 
-    def project(tie):
-        normed = (tie(group_inputs) * first_scale * gain_one).astype(jnp.bfloat16)
-        qkv = jnp.dot(normed, qkv_w, preferred_element_type=jnp.float32)
-        queries = (
-            rotate(qkv[:, :q_cols].reshape(group_rows, kv_here * heads_per, HD), cosine, sine_table)
-            .astype(jnp.bfloat16)
-            .reshape(group_rows, q_cols)
-        )
-        keys = (
-            rotate(
-                qkv[:, q_cols : q_cols + kv_cols].reshape(group_rows, kv_here, HD),
-                cosine,
-                sine_table,
-            )
-            .astype(jnp.bfloat16)
-            .reshape(group_rows, kv_cols)
-        )
-        vals = qkv[:, q_cols + kv_cols :].astype(jnp.bfloat16)
-        return normed, queries, keys, vals
-
-    def mix(tie, projected):
-        _, queries, keys, vals = projected
-        mixed = attend(tie(queries), keys, vals, row_ids, col_ids)
-        part = lax.dot_general(mixed[0], o_w, COLS_DIMS, preferred_element_type=jnp.float32)
-        return mixed, part.astype(jnp.bfloat16)
+    def attention(tie):
+        return front(
+            tie(group_tokens), gain_one[None], qkv_w, o_w, cosine, sine_table, row_ids, col_ids
+        )
 
     cot_out = after(jnp.concatenate([cotangent[0], meta], axis=1), group_tokens)
-    cot_all, branch, (projected, mixed) = gather_beside_sum(cot_out, project, mix)
-    normed, queries, keys, vals = projected
-    mixed_low, run_top, run_total = mixed
+    cot_all, branch, attended = gather_beside_sum(cot_out, attention)
+    normed, queries, keys, vals, mixed_low, run_top, run_total, _ = attended
     rows_from, meta_from = far_order(ex_index, dealt_of)
     cot_rows, meta_all = take_blocks(
         jnp.stack([rows_from, meta_from]),
@@ -976,21 +1035,21 @@
     second_scale = lax.rsqrt(jnp.mean(middle * middle, axis=-1, keepdims=True) + EPSILON)
     sent_rows = (middle * second_scale * gain_two).astype(jnp.bfloat16)
     sent_rows = after(sent_rows, in_w, cot_rows)
-    slot_rows = 8 * tok_rows
-
-    def spread_gates(tie):
+    part_rows = 16 * tok_rows
+
+    def spread_gates(tie, works):
         column = jnp.arange(128, dtype=jnp.int32)[:, None]
         owner = ex_index * own_experts + jnp.arange(ff_cols, dtype=jnp.int32)[None, :] // ff_here
         spread = ((column % E == owner) & (column < 3 * E)).astype(jnp.bfloat16)
         return jnp.dot(tie(meta_all), spread, preferred_element_type=jnp.float32)
 
-    def pull(tie):
+    def pull(tie, works):
         return lax.dot_general(
             tie(cot_rows), down_w, COLS_DIMS, preferred_element_type=jnp.float32
         )
 
-    def up(tie, sent):
-        return jnp.dot(tie(sent), in_w, preferred_element_type=jnp.float32)
+    def up(sent):
+        return jnp.dot(sent, in_w, preferred_element_type=jnp.float32)
 
     def down(gate_up, gates_here, pulled_here):
         gate_part = gate_up[:, :ff_cols]
@@ -1010,56 +1069,72 @@
             grads_here, in_w, COLS_DIMS, preferred_element_type=jnp.float32
         ).astype(jnp.bfloat16)
 
-    sent_slots, ups, (gate_cols, pulled) = gather_slots(sent_rows, (spread_gates, pull, up))
-    ups = ups + [up(lambda v: v, sent_slots[3])]
-    weighted_slots, grad_slots = zip(
-        *[
-            down(
-                ups[n],
-                gate_cols[n * slot_rows : (n + 1) * slot_rows],
-                pulled[n * slot_rows : (n + 1) * slot_rows],
-            )
-            for n in range(4)
-        ]
-    )
-    sent_grad_slots = [back(g) for g in grad_slots]
-
-    def out_rows(tie, works):
-        return [
-            jnp.dot(tie(part), down_w, preferred_element_type=jnp.float32).astype(jnp.bfloat16)
-            for part in weighted_slots
-        ]
-
-    def in_terms(numbers, so_far):
-        def work(tie, works):
-            total = so_far()
-            for n in numbers:
-                term = lax.dot_general(
-                    tie(sent_slots[n]), grad_slots[n], ROWS_DIMS, preferred_element_type=jnp.float32
-                )
-                total = term if total is None else total + term
-            return total
-
-        return work
-
-    def down_terms(tie):
-        return RESIDUAL * lax.dot_general(
-            tie(joined(*weighted_slots)), cot_rows, ROWS_DIMS, preferred_element_type=jnp.float32
-        )
-
-    sent_grad, (_, out_slots, in_low, in_mid, in_high, _) = scatter_slots(
-        sent_grad_slots,
-        (
-            None,
-            out_rows,
-            in_terms((0, 1), lambda: None),
-            in_terms((2,), lambda: None),
-            in_terms((3,), lambda: None),
-            None,
-        ),
-    )
-    in_term = (in_low + in_mid + in_high).astype(jnp.bfloat16)
-
+    def of_part(number, works, gate_up):
+        rows_here = slice(number * part_rows, (number + 1) * part_rows)
+        return down(gate_up, works[2][rows_here], works[3][rows_here])
+
+    def first_up(tie, works, sent):
+        return up(tie(sent))
+
+    def first_down(tie, works):
+        weighted_here, grads_here = of_part(0, works, tie(works[4]))
+        return weighted_here, grads_here, back(grads_here)
+
+    sent_parts, works = gather_pairs(
+        sent_rows, (None, spread_gates, pull, first_up, first_down)
+    )
+    weighted_first, grads_first, back_first = works[5]
+    weighted_second, grads_second = of_part(1, works, up(sent_parts[1]))
+
+    def out_first(tie, works):
+        return jnp.dot(tie(weighted_first), down_w, preferred_element_type=jnp.float32).astype(
+            jnp.bfloat16
+        )
+
+    def out_second(tie, works):
+        return jnp.dot(tie(weighted_second), down_w, preferred_element_type=jnp.float32).astype(
+            jnp.bfloat16
+        )
+
+    def in_first(tie, works):
+        return lax.dot_general(
+            tie(sent_parts[0]), grads_first, ROWS_DIMS, preferred_element_type=jnp.float32
+        )
+
+    out_sum = []
+
+    def in_second(tie, works):
+        out_sum.append(PairScatter(works[:2]))
+        term = works[2] + lax.dot_general(
+            tie(sent_parts[1]), grads_second, ROWS_DIMS, preferred_element_type=jnp.float32
+        )
+        return term, out_sum[0].step(tie)
+
+    def down_first(tie, works):
+        out_sum[0].keep(works[3][1])
+        term = lax.dot_general(
+            tie(weighted_first), cot_rows[:part_rows], ROWS_DIMS, preferred_element_type=jnp.float32
+        )
+        return term, out_sum[0].step(tie)
+
+    def down_second(tie, works):
+        out_sum[0].keep(works[4][1])
+        term = works[4][0] + lax.dot_general(
+            tie(weighted_second),
+            cot_rows[part_rows:],
+            ROWS_DIMS,
+            preferred_element_type=jnp.float32,
+        )
+        return term, out_sum[0].step(tie)
+
+    sent_grad, works = scatter_pairs(
+        (back_first, back(grads_second)),
+        (out_first, out_second, in_first, in_second, down_first, down_second),
+    )
+    out_sum = out_sum[0]
+    out_sum.keep(works[5][1])
+    in_term = works[3][0].astype(jnp.bfloat16)
+    down_grad = (RESIDUAL * works[5][0]).reshape(own_experts, ff_here, model).transpose(1, 0, 2)
     upstream = cotangent[0].astype(jnp.float32)
     scaled_grad = sent_grad * gain_two
     middle_grad = (
@@ -1072,100 +1147,89 @@
     gain_two_part = jnp.sum(sent_grad * middle * second_scale, axis=0)
     branch_grad = (RESIDUAL * middle_grad).astype(jnp.bfloat16)
 
-    def gather_one(tie, works):
-        piece = tie(branch_grad)
-        return over_dp(piece, Z_NEAR), over_dp(piece, Z_MIDDLE), swap_y(piece)
-
-    def gather_two(tie, works):
-        near, middle, _ = works[0]
-        moved = over_dp(tie(near), Z_MIDDLE), over_dp(middle, Z_OUT), swap_y(near)
-        return moved, down_terms(tie)
-
-    def gather_three(tie, works):
-        third = works[0][1] + works[1][0][1]
-        return over_dp(tie(works[1][0][0]), Z_OUT), swap_y(third), third
-
-    def gather_four(tie, works):
-        fourth = works[1][0][0] + works[2][0]
-        return swap_y(tie(fourth)), fourth
-
-    def pull_attention(tie, works):
-        (near, _, y0), ((_, _, y1), _), (_, y2, third), (y3, fourth) = works[:4]
-        grad_all = joined(tie(branch_grad), y0, near, y1, third, y2, fourth, y3)
-        o_term = lax.dot_general(grad_all, mixed_low, ROWS_DIMS, preferred_element_type=jnp.float32)
-        grad_heads = jnp.dot(grad_all, o_w, preferred_element_type=jnp.float32).astype(
-            jnp.bfloat16
-        )
-        return o_term, attend_back(
-            queries, keys, vals, grad_heads, run_top, run_total, row_ids, col_ids
-        )
-
-    def pull_projections(tie, works):
-        o_term, (query_grad, key_grad, value_grad) = works[4]
-        query_low = turn_back(
-            tie(query_grad).reshape(group_rows, kv_here * heads_per, HD), cosine, sine_table
-        ).reshape(group_rows, q_cols)
-        key_low = turn_back(
-            key_grad.reshape(group_rows, kv_here, HD), cosine, sine_table
-        ).reshape(group_rows, kv_cols)
-        qkv_grad = jnp.concatenate([query_low, key_low, value_grad], axis=1).astype(jnp.bfloat16)
-        normed_grad_part = lax.dot_general(
-            qkv_grad, qkv_w, COLS_DIMS, preferred_element_type=jnp.float32
-        )
-        gain_one_part = jnp.sum(normed_grad_part * group_inputs * first_scale, axis=0)
-        qkv_term = lax.dot_general(normed, qkv_grad, ROWS_DIMS, preferred_element_type=jnp.float32)
+    def out_step(tie, works):
+        if works:
+            out_sum.keep(works[-1])
+        return out_sum.step(tie)
+
+    branch_grad_all, works = dp_gather(branch_grad, (out_step, out_step, out_step, None))
+    out_sum.keep(works[2])
+    output = middle + RESIDUAL * out_sum.total()
+    in_back = lax.all_to_all(
+        after(in_term, branch_grad_all).reshape(n_dp, in_weight.shape[0], 2 * ff_cols),
+        "dp",
+        split_axis=0,
+        concat_axis=0,
+        tiled=True,
+    )
+
+
+    qkv_grad, normed_grad_part, gain_one_part = rear(
+        branch_grad_all,
+        o_w,
+        queries,
+        keys,
+        vals,
+        run_top,
+        run_total,
+        row_ids,
+        col_ids,
+        cosine,
+        sine_table,
+        qkv_w,
+        group_tokens,
+    )
+    total = DpScatter(normed_grad_part)
+
+    def weight_grads(tie):
+        qkv_term = lax.dot_general(
+            normed, tie(qkv_grad), ROWS_DIMS, preferred_element_type=jnp.float32
+        )
+        o_term = lax.dot_general(
+            branch_grad_all, mixed_low, ROWS_DIMS, preferred_element_type=jnp.float32
+        )
         grads = jnp.concatenate(
             [
                 qkv_term,
                 o_term,
-                gain_one_part[:, None],
+                gain_one_part[0][:, None],
                 gain_two_part[:, None],
                 jnp.zeros((model, 126), jnp.float32),
             ],
             axis=1,
         ).astype(jnp.bfloat16)
-        return normed_grad_part.astype(jnp.bfloat16), grads
-
-    expert_sum, works = scatter_slots(
-        [after(out_slots[n], sent_grad) for n in range(4)],
-        (gather_one, gather_two, gather_three, gather_four, pull_attention, pull_projections),
-    )
-    in_back = lax.all_to_all(
-        after(in_term, works[3]).reshape(n_dp, in_weight.shape[0], 2 * ff_cols),
-        "dp",
-        split_axis=0,
-        concat_axis=0,
-        tiled=True,
-    )
-    output = middle + RESIDUAL * expert_sum
-    down_grad = works[1][1].reshape(own_experts, ff_here, model).transpose(1, 0, 2)
-    normed_grad_part, grads = works[5]
-    total = DpScatter(normed_grad_part)
-    grads = grads.reshape(n_dp, n_ex, w_rows, -1)
-    own_g, core_g, x_g, xc_g = [
-        lax.dynamic_index_in_dim(grads, ex_index ^ k, 1, keepdims=False) for k in range(n_ex)
-    ]
+        grads = grads.reshape(n_dp, n_ex, w_rows, -1)
+        return [
+            lax.dynamic_index_in_dim(grads, ex_index ^ k, 1, keepdims=False) for k in range(n_ex)
+        ]
+
+    def unpack_first(tie):
+        return (
+            tie(in_back)
+            .reshape(n_dp, d_rows, 2, own_experts, ff_here)
+            .transpose(3, 1, 2, 0, 4)
+            .reshape(own_experts, d_rows, 2 * FF)
+        )
+
+    sums, (own_g, core_g, x_g, xc_g) = one_round(total.step(), (normed_grad_part,), weight_grads)
+    total.keep(sums)
     core_pair = jnp.stack([core_g, xc_g])
     (sums, from_core), _ = one_round((total.step(), swap_core(core_pair)), (core_pair,))
     total.keep(sums)
     x_g = added(x_g, from_core[1])
-    (sums, from_x), _ = one_round((total.step(), swap_x(x_g)), (x_g,))
+    (sums, from_x), unpacked = one_round((total.step(), swap_x(x_g)), (x_g,), unpack_first)
     total.keep(sums)
     grads = lax.all_to_all(
-        after(added(own_g, from_core[0], from_x), in_back), "dp", split_axis=0, concat_axis=0, tiled=True
-    )
-    (sums, grads), _ = one_round((total.step(), grads), ())
+        added(own_g, from_core[0], from_x), "dp", split_axis=0, concat_axis=0, tiled=True
+    )
+    (sums, grads), in_grad = one_round(
+        (total.step(), grads),
+        (from_x,),
+        lambda tie: tie(unpacked).transpose(1, 0, 2).astype(jnp.float32),
+    )
     total.keep(sums)
     grads = grads.astype(jnp.float32)
-    total.keep(one_round(total.step(), ())[0])
     normed_grad = total.total()
-    in_grad = (
-        in_back
-        .reshape(n_dp, in_weight.shape[0], 2, own_experts, ff_here)
-        .transpose(1, 3, 2, 0, 4)
-        .reshape(in_weight.shape)
-        .astype(jnp.float32)
-    )
 
     def own_rows(begin, width):
         return grads[:, :, begin : begin + width].transpose(1, 0, 2).reshape(w_rows, n_dp * width)

time: 902 us -> 864 us (0.958)
  waiting for transfers between devices: 193 us -> 254 us
  starting transfers between devices: 205 us -> 147 us
  local copies, waits for them, and re-layouts: 159 us -> 137 us
  other arithmetic: 139 us -> 120 us
  matrix products: 150 us -> 132 us
  Pallas kernels: 40.1 us -> 57.3 us
    ppermute x84 -> x72, waiting for transfers between devices: 78.5 us -> 145 us  [over_dp(): return lax.ppermute(piece, 'dp', moves)]
    ppermute x84 -> x72, starting transfers between devices: 150 us -> 106 us  [over_dp(): return lax.ppermute(piece, 'dp', moves)]
    pallas_call x2, Pallas kernels: 27.4 us -> 44.6 us  [the longest x1 24.4 us: rear(): pl.pallas_call(functools.partial(rear_kernel, heads=heads, rows=min(256,...]
    convert_element_type x8 -> x1, other arithmetic: 24.4 us -> 7.46 us  [per_device(): tie(unpacked).transpose(1, 0, 2).astype(jnp.float32)]
    unnamed x281 -> x148, local copies, waits for them, and re-layouts: 63.1 us -> 48.1 us
    ppermute x45 -> x27, starting transfers between devices: 37.2 us -> 23.4 us  [over_expert(): return lax.ppermute(piece, 'expert', moves)]
    dot_general x19 -> x10, matrix products: 103 us -> 90.3 us  [the longest x2 29.2 us: up(): return jnp.dot(sent, in_w, preferred_element_type=jnp.float32)]
    concatenate x18 -> x17, other arithmetic: 17.7 us -> 5.15 us  [joined(): return jnp.concatenate(arrays, axis=0)]
  transfers between devices with their start and end apart: 133 -> 103, of which waited for: 31 -> 39; matrix products, arithmetic and copies ran while one was open for 46% -> 35% of each run, Pallas kernels for 5% -> 7%
where the time goes in v1:
time: 864 us; the launch traced here: 852 us
  waiting for transfers between devices  254 us (29%)
  starting transfers between devices  147 us (17%)
  local copies, waits for them, and re-layouts  137 us (16%)
  matrix products  132 us (15%)
  other arithmetic  120 us (14%)
  Pallas kernels  57.3 us (7%)
    ppermute x72, waiting for transfers between devices, over_dp(): return lax.ppermute(piece, 'dp', moves)  145 us
    ppermute x72, starting transfers between devices, over_dp(): return lax.ppermute(piece, 'dp', moves)  106 us
    all_to_all x1, waiting for transfers between devices, per_device(): lax.all_to_all(after(in_out, group_tokens, attn_in), 'dp', split_axis=0,...  62.7 us
    unnamed x148, local copies, waits for them, and re-layouts  48.1 us
    ppermute x27, waiting for transfers between devices, over_expert(): return lax.ppermute(piece, 'expert', moves)  42.8 us
    convert_element_type x34, other arithmetic, added(): return total.astype(jnp.bfloat16)  36 us
    dot_general x2, matrix products, up(): return jnp.dot(sent, in_w, preferred_element_type=jnp.float32)  29.2 us
    pallas_call x1, Pallas kernels, rear(): pl.pallas_call(functools.partial(rear_kernel, heads=heads, rows=min(256,...  24.4 us
  transfers between devices with their start and end apart: 103, of which 39 were waited for; matrix products, arithmetic and copies ran while one was open for 35% of the time, Pallas kernels for 7%

profile of v1, /device:TPU:0, one launch (start us, length us, event | category | flops | bytes accessed | tf_op | source)
XLA Modules:
  0.0 851.6 jit_solution(9699899096606620291)
XLA Ops:
  14.9 5.0 all-to-all-start
  27.9 8.5 %copy.108 = bf16[192,10,1024]{0,2,1:T(8,128)(2,1)} copy(f32[192,10,1024]{2,0,1:T(8,128)} %param.27) | data formatting | bytes 11796480 | tf_op jit(solution)/shard_map/optimization_barrier | solution.py:875
  36.5 5.7 copy.109
  49.6 5.1 collective-permute-done.7
  54.6 4.0 collective-permute-done.6
  69.4 4.2 collective-permute-done.8
  79.4 3.7 collective-permute-done.13
  96.6 20.3 %front.1 = (bf16[1024,1536]{1,0:T(8,128)(2,1)}, bf16[1024,192]{1,0:T(8,128)(2,1)}, bf16[1024,64]{1,0:T(8,128)(2,1)}, bf16[1024,64]{1,0:T(8,128)(2,1)}, bf16[1024...) custom-call(bf16[1024,1536]{1,0:T(8,128)(2,1)} %copy-done.3, ...), custom_call_target="tpu_custom_call" | custom-call | tf_op jit(solution)/shard_map/front/pallas_call | solution.py:771
  128.0 8.2 collective-permute-done.18
  141.5 5.1 collective-permute-start.22
  170.5 5.5 collective-permute-done.24
  176.0 4.9 collective-permute-done.25
  187.8 4.5 collective-permute-done.30
  195.9 7.4 copy.119
  203.4 4.7 all-to-all-start.1
  214.9 6.2 constant_dynamic-update-slice_fusion.20.refs_0_.refs_1_.refs_2_.refs_3_.refs_4_.refs_5_.refs_6_.refs_7_.refs_8_.refs_9_.refs_10_.refs_11_.refs_12_.refs_13_.refs_14_.refs_15_
  221.1 12.7 %take_blocks.1 = (bf16[4096,1536]{1,0:T(8,128)(2,1)}, bf16[4096,128]{1,0:T(8,128)(2,1)}) custom-call(s32[2,64]{1,0:T(2,128)} %pad_add_fusion.2.index_ref, bf16[4096,1664]{1,0:T(8,128)(2,1)} %constant_dynamic-update-slice_fusion.20.refs_0_.refs_1_.refs_2_.refs_3_.refs_4_.refs_5_.refs_6_.refs_7_.refs_8_.refs_9_.refs_10_.refs_11_.refs_12_.refs_13_.refs_14_.refs_15_, ...), custom_call_target="tpu_custom_call" | custom-call | tf_op jit(solution)/shard_map/take_blocks/pallas_call | solution.py:680
  233.8 62.7 %all-to-all-done.1 = bf16[8,192,1280]{2,1,0:T(8,128)(2,1)} async-done(((bf16[8,192,1280]{2,1,0:T(8,128)(2,1)}), bf16[8,192,1280]{2,1,0:T(8,128)(2,1)}, u32[]{:S(2)}, u32[]{:S(2)}) %all-to-all-start.1) | async-done | bytes 3932192 | tf_op jit(solution)/shard_map/all_to_all | solution.py:969
  298.8 8.4 collective-permute-done.34
  313.1 5.5 collective-permute-done.39
  319.9 6.8 collective-permute-done.37
  336.4 4.8 collective-permute-done.40
  353.0 16.3 %fusion.79 = f32[4096,640]{1,0:T(8,128)} fusion(bf16[4096,1536]{1,0:T(8,128)(2,1)} %get-tuple-element.225, bf16[640,1536]{1,0:T(8,128)(2,1)S(1)} %bitcast.171), kind=kOutput, calls=%fused_computation.407 | convolution fusion | flops 8053063680 | bytes 25034752 | tf_op jit(solution)/shard_map/dot_general | solution.py:1047
  372.2 15.2 %fusion.80 = f32[2048,1280]{1,0:T(8,128)} fusion(bf16[2048,1536]{1,0:T(8,128)(2,1)S(1)} %constant_dynamic-update-slice_fusion.41, bf16[1536,1280]{1,0:T(8,128)(2,1)} %bitcast.42), kind=kOutput, calls=%fused_computation.408 | convolution fusion | flops 8053063680 | bytes 20709376 | tf_op jit(solution)/shard_map/dot_general | solution.py:1052
  394.6 8.3 multiply_convert_fusion.5
  405.6 12.2 %convolution_convert_fusion.3 = bf16[2048,1536]{1,0:T(8,128)(2,1)} fusion(bf16[1536,1280]{1,0:T(8,128)(2,1)} %bitcast.42, bf16[2048,640]{1,0:T(8,128)(2,1)S(1)} %get-tuple-element.388, bf16[2048,640]{1,0:T(8,128)(2,1)S(1)} %get-tuple-element.387), kind=kOutput, calls=%fused_computation.4 | convolution fusion | flops 8066695168 | bytes 15466496 | tf_op jit(solution)/shard_map/dot_general | solution.py:1068
  419.7 14.0 %fusion.81 = f32[2048,1280]{1,0:T(8,128)} fusion(bf16[2048,1536]{1,0:T(8,128)(2,1)} %constant_dynamic-update-slice_fusion.58, bf16[1536,1280]{1,0:T(8,128)(2,1)} %bitcast.42), kind=kOutput, calls=%fused_computation.409 | convolution fusion | flops 8053063680 | bytes 20709376 | tf_op jit(solution)/shard_map/dot_general | solution.py:1052
  433.7 8.4 multiply_convert_fusion.3
  442.1 11.9 %convolution_convert_fusion.2 = bf16[2048,1536]{1,0:T(8,128)(2,1)S(1)} fusion(bf16[1536,1280]{1,0:T(8,128)(2,1)} %bitcast.42, bf16[2048,640]{1,0:T(8,128)(2,1)S(1)} %get-tuple-element.386, bf16[2048,640]{1,0:T(8,128)(2,1)S(1)} %get-tuple-element.385), kind=kOutput, calls=%fused_computation.3 | convolution fusion | flops 8066695168 | bytes 15466496 | tf_op jit(solution)/shard_map/dot_general | solution.py:1068
  455.2 12.7 %fusion.82 = f32[1536,1280]{1,0:T(8,128)S(1)} fusion(bf16[2048,1536]{1,0:T(8,128)(2,1)} %copy-done.39, bf16[2048,1280]{1,0:T(8,128)(2,1)} %pad_maximum_fusion), kind=kOutput, calls=%fused_computation.410 | convolution fusion | flops 8053063680 | bytes 19398656 | tf_op jit(solution)/shard_map/dot_general | solution.py:1100
  468.0 5.2 convolution_convert_fusion.1
  473.2 5.0 add_convert_fusion.3
  480.7 7.0 convolution_convert_fusion
  487.8 10.8 %collective-permute-done.50 = bf16[256,1536]{1,0:T(8,128)(2,1)S(1)} collective-permute-done((bf16[256,1536]{1,0:T(8,128)(2,1)S(1)}, bf16[256,1536]{1,0:T(8,128)(2,1)S(1)}, u32[]{:S(2)}, u32[]{:S(2)}) %collective-permute-start.50) | collective-permute-done | bytes 786464 | tf_op jit(solution)/shard_map/ppermute | solution.py:409
  509.5 14.4 %fusion.6 = f32[1536,1280]{1,0:T(8,128)} fusion(bf16[2048,1536]{1,0:T(8,128)(2,1)} %constant_dynamic-update-slice_fusion.58, bf16[2048,640]{1,0:T(8,128)(2,1)} %copy-done.15, bf16[2048,640]{1,0:T(8,128)(2,1)} %copy-done.14), kind=kOutput, calls=%fused_computation.29 | convolution fusion | flops 8063549440 | bytes 19398656 | tf_op jit(solution)/shard_map/dot_general | solution.py:1108
  525.8 6.7 collective-permute-done.53
  542.5 9.1 %fusion.2 = f32[640,1536]{1,0:T(8,128)} fusion(bf16[2048,640]{1,0:T(8,128)(2,1)S(1)} %copy-done.13, bf16[4096,1536]{1,0:T(8,128)(2,1)} %get-tuple-element.225), kind=kOutput, calls=%fused_computation.9 | convolution fusion | flops 4026531840 | bytes 12845056 | tf_op jit(solution)/shard_map/dot_general | solution.py:1115
  553.4 6.2 add.878
  561.2 4.0 add_convert_fusion.1
  572.3 13.1 %collective-permute-done.63 = bf16[256,1536]{1,0:T(8,128)(2,1)S(1)} collective-permute-done((bf16[256,1536]{1,0:T(8,128)(2,1)S(1)}, bf16[256,1536]{1,0:T(8,128)(2,1)S(1)}, u32[]{:S(2)}, u32[]{:S(2)}) %collective-permute-start.63) | collective-permute-done | bytes 786464 | tf_op jit(solution)/shard_map/ppermute | solution.py:409
  595.1 22.0 %collective-permute-done.68 = bf16[128,1536]{1,0:T(8,128)(2,1)S(1)} collective-permute-done((bf16[128,1536]{1,0:T(8,128)(2,1)S(1)}, bf16[128,1536]{1,0:T(8,128)(2,1)S(1)}, u32[]{:S(2)}, u32[]{:S(2)}) %collective-permute-start.68) | collective-permute-done | bytes 393248 | tf_op jit(solution)/shard_map/ppermute | solution.py:405
  617.0 6.7 fusion
  637.1 9.2 %collective-permute-done.77 = bf16[128,1536]{1,0:T(8,128)(2,1)S(1)} collective-permute-done((bf16[128,1536]{1,0:T(8,128)(2,1)S(1)}, bf16[128,1536]{1,0:T(8,128)(2,1)S(1)}, u32[]{:S(2)}, u32[]{:S(2)}) %collective-permute-start.77) | collective-permute-done | bytes 393248 | tf_op jit(solution)/shard_map/ppermute | solution.py:405
  647.4 7.4 collective-permute-done.74
  657.9 5.6 collective-permute-start.82
  671.3 7.8 collective-permute-start.85
  681.5 7.6 collective-permute-done.85
  689.1 4.3 collective-permute-done.83
  696.2 6.6 collective-permute-done.87
  703.5 4.7 all-to-all-start.2
  709.8 24.4 %rear.1 = (bf16[1024,320]{1,0:T(8,128)(2,1)}, bf16[1024,1536]{1,0:T(8,128)(2,1)}, f32[1,1536]{1,0:T(1,128)}) custom-call(bf16[1024,1536]{1,0:T(8,128)(2,1)} %constant_dynamic-update-slice_fusion.67.g_ref, bf16[1536,192]{1,0:T(8,128)(2,1)} %slice.456.ow_ref, bf16[1024,192]{1,0:T(8,128)(2,1)} %get-tuple-element.288.q_ref, ...), custom_call_target="tpu_custom_call" | custom-call | tf_op jit(solution)/shard_map/rear/pallas_call | solution.py:859
  738.6 3.3 convolution_convert_fusion.4
  748.7 4.4 concatenate.177
  753.4 5.2 collective-permute-done.88
  763.8 7.6 collective-permute-done.90
  771.4 4.0 collective-permute-done.89
  779.0 5.2 collective-permute-start.93
  789.3 3.8 all-to-all-done.2
  793.1 7.4 copy.127
  800.5 5.8 copy.128
  808.3 3.5 all-to-all-start.3
  815.2 4.7 collective-permute-start.96
  819.9 7.5 convert_bitcast_fusion
  831.5 10.4 %copy.133 = f32[192,10,1024]{2,0,1:T(8,128)} copy(f32[192,10,1024]{0,2,1:T(8,128)} %convert_bitcast_fusion) | data formatting | bytes 15728640
  (508 shorter events, 285.1 us)
Async XLA Ops:
  0.7 20.5 %collective-permute-start = (bf16[128,1536]{1,0:T(8,128)(2,1)}, bf16[128,1536]{1,0:T(8,128)(2,1)}, u32[]{:S(2)}, u32[]{:S(2)}) collective-permute-start(bf16[128,1536]{1,0:T(8,128)(2,1)} %bitcast.165), channel_id=1, source_target_pairs={{0,8},{4,12},{8,0},{12,4},{16,24},{20,28},{24,16},{28,20},{1,9},{5... | collective-permute-start | bytes 1179656 | tf_op jit(solution)/shard_map/ppermute | solution.py:405
  3.8 17.4 %collective-permute-start.1 = (bf16[128,1536]{1,0:T(8,128)(2,1)}, bf16[128,1536]{1,0:T(8,128)(2,1)}, u32[]{:S(2)}, u32[]{:S(2)}) collective-permute-start(bf16[128,1536]{1,0:T(8,128)(2,1)} %bitcast.166), channel_id=1, source_target_pairs={{8,16},{12,20},{16,8},{20,12},{9,17},{13,21},{17,9},{21,13},{10,18... | collective-permute-start | bytes 1179656 | tf_op jit(solution)/shard_map/ppermute | solution.py:405
  5.2 15.9 %collective-permute-start.2 = (bf16[128,1536]{1,0:T(8,128)(2,1)}, bf16[128,1536]{1,0:T(8,128)(2,1)}, u32[]{:S(2)}, u32[]{:S(2)}) collective-permute-start(bf16[128,1536]{1,0:T(8,128)(2,1)} %bitcast.167), channel_id=1, source_target_pairs={{0,4},{4,0},{8,12},{12,8},{16,20},{20,16},{24,28},{28,24},{1,5},{5... | collective-permute-start | bytes 1179656 | tf_op jit(solution)/shard_map/ppermute | solution.py:405
  14.9 32.2 %all-to-all-start = ((bf16[8,48,640]{2,1,0:T(8,128)(2,1)}), bf16[8,48,640]{2,1,0:T(8,128)(2,1)}, u32[]{:S(2)}, u32[]{:S(2)}) async-start(bf16[8,48,640]{2,1,0:T(8,128)(2,1)} %bitcast.25), calls=%async_computation | async-start | bytes 983040 | tf_op jit(solution)/shard_map/all_to_all | solution.py:962
  21.2 21.0 %collective-permute-start.3 = (bf16[128,1536]{1,0:T(8,128)(2,1)}, bf16[128,1536]{1,0:T(8,128)(2,1)}, u32[]{:S(2)}, u32[]{:S(2)}) collective-permute-start(bf16[128,1536]{1,0:T(8,128)(2,1)} %collective-permute-done), channel_id=1, source_target_pairs={{8,16},{12,20},{16,8},{20,12},{9,17},{13,21},{17,9},{21,13},{10,18... | collective-permute-start | bytes 1179656 | tf_op jit(solution)/shard_map/ppermute | solution.py:405
  22.6 19.6 %collective-permute-start.5 = (bf16[128,1536]{1,0:T(8,128)(2,1)}, bf16[128,1536]{1,0:T(8,128)(2,1)}, u32[]{:S(2)}, u32[]{:S(2)}) collective-permute-start(bf16[128,1536]{1,0:T(8,128)(2,1)} %collective-permute-done), channel_id=1, source_target_pairs={{0,4},{4,0},{8,12},{12,8},{16,20},{20,16},{24,28},{28,24},{1,5},{5... | collective-permute-start | bytes 1179656 | tf_op jit(solution)/shard_map/ppermute | solution.py:405
  24.6 17.5 %collective-permute-start.4 = (bf16[128,1536]{1,0:T(8,128)(2,1)}, bf16[128,1536]{1,0:T(8,128)(2,1)}, u32[]{:S(2)}, u32[]{:S(2)}) collective-permute-start(bf16[128,1536]{1,0:T(8,128)(2,1)} %collective-permute-done.1), channel_id=1, source_target_pairs={{8,0},{12,4},{16,24},{20,28},{9,1},{13,5},{17,25},{21,29},{10,2},{... | collective-permute-start | bytes 1179656 | tf_op jit(solution)/shard_map/ppermute | solution.py:405
  61.9 21.2 %collective-permute-start.13 = (bf16[2,8,48,640]{3,2,0,1:T(8,128)(2,1)}, bf16[2,8,48,640]{3,2,0,1:T(8,128)(2,1)}, u32[]{:S(2)}, u32[]{:S(2)}) collective-permute-start(bf16[2,8,48,640]{3,2,0,1:T(8,128)(2,1)} %pad_maximum_fusion.6), channel_id=1, source_target_pairs={{0,2},{1,3},{2,0},{3,1},{4,6},{5,7},{6,4},{7,5},{8,10},{9,11},{10,... | collective-permute-start | bytes 2949128 | tf_op jit(solution)/shard_map/ppermute | solution.py:409
  74.6 42.2 %collective-permute-start.10 = (bf16[128,1664]{1,0:T(8,128)(2,1)}, bf16[128,1664]{1,0:T(8,128)(2,1)}, u32[]{:S(2)}, u32[]{:S(2)}) collective-permute-start(bf16[128,1664]{1,0:T(8,128)(2,1)} %concatenate.138), channel_id=1, source_target_pairs={{8,16},{12,20},{16,8},{20,12},{9,17},{13,21},{17,9},{21,13},{10,18... | collective-permute-start | bytes 1277960 | tf_op jit(solution)/shard_map/ppermute | solution.py:405
  76.4 40.4 %collective-permute-start.11 = (bf16[128,1664]{1,0:T(8,128)(2,1)}, bf16[128,1664]{1,0:T(8,128)(2,1)}, u32[]{:S(2)}, u32[]{:S(2)}) collective-permute-start(bf16[128,1664]{1,0:T(8,128)(2,1)} %concatenate.138), channel_id=1, source_target_pairs={{0,4},{4,0},{8,12},{12,8},{16,20},{20,16},{24,28},{28,24},{1,5},{5... | collective-permute-start | bytes 1277960 | tf_op jit(solution)/shard_map/ppermute | solution.py:405
  77.5 39.4 %collective-permute-start.9 = (bf16[128,1664]{1,0:T(8,128)(2,1)}, bf16[128,1664]{1,0:T(8,128)(2,1)}, u32[]{:S(2)}, u32[]{:S(2)}) collective-permute-start(bf16[128,1664]{1,0:T(8,128)(2,1)} %concatenate.138), channel_id=1, source_target_pairs={{0,8},{4,12},{8,0},{12,4},{16,24},{20,28},{24,16},{28,20},{1,9},{5... | collective-permute-start | bytes 1277960 | tf_op jit(solution)/shard_map/ppermute | solution.py:405
  116.9 20.4 %collective-permute-start.14 = (bf16[128,1664]{1,0:T(8,128)(2,1)}, bf16[128,1664]{1,0:T(8,128)(2,1)S(1)}, u32[]{:S(2)}, u32[]{:S(2)}) collective-permute-start(bf16[128,1664]{1,0:T(8,128)(2,1)} %collective-permute-done.9), channel_id=1, source_target_pairs={{8,16},{12,20},{16,8},{20,12},{9,17},{13,21},{17,9},{21,13},{10,18... | collective-permute-start | bytes 1277960 | tf_op jit(solution)/shard_map/ppermute | solution.py:405
  117.6 19.7 %collective-permute-start.16 = (bf16[128,1664]{1,0:T(8,128)(2,1)}, bf16[128,1664]{1,0:T(8,128)(2,1)S(1)}, u32[]{:S(2)}, u32[]{:S(2)}) collective-permute-start(bf16[128,1664]{1,0:T(8,128)(2,1)} %collective-permute-done.9), channel_id=1, source_target_pairs={{0,4},{4,0},{8,12},{12,8},{16,20},{20,16},{24,28},{28,24},{1,5},{5... | collective-permute-start | bytes 1277960 | tf_op jit(solution)/shard_map/ppermute | solution.py:405
  119.8 18.0 %collective-permute-start.17 = (bf16[256,1664]{1,0:T(8,128)(2,1)S(1)}, bf16[256,1664]{1,0:T(8,128)(2,1)S(1)}, u32[]{:S(2)}, u32[]{:S(2)}) collective-permute-start(bf16[256,1664]{1,0:T(8,128)(2,1)S(1)} %pad_maximum_fusion.8), channel_id=1, source_target_pairs={{0,2},{1,3},{2,0},{3,1},{4,6},{5,7},{6,4},{7,5},{8,10},{9,11},{10,... | collective-permute-start | bytes 2555912 | tf_op jit(solution)/shard_map/ppermute | solution.py:409
  136.3 17.8 %collective-permute-start.23 = (bf16[128,1536]{1,0:T(8,128)(2,1)S(1)}, bf16[128,1536]{1,0:T(8,128)(2,1)S(1)}, u32[]{:S(2)}, u32[]{:S(2)}) collective-permute-start(bf16[128,1536]{1,0:T(8,128)(2,1)S(1)} %get-tuple-element.413), channel_id=1, source_target_pairs={{0,4},{4,0},{8,12},{12,8},{16,20},{20,16},{24,28},{28,24},{1,5},{5... | collective-permute-start | bytes 1179656 | tf_op jit(solution)/shard_map/ppermute | solution.py:405
  138.9 19.7 %collective-permute-start.21 = (bf16[256,1664]{1,0:T(8,128)(2,1)S(1)}, bf16[256,1664]{1,0:T(8,128)(2,1)S(1)}, u32[]{:S(2)}, u32[]{:S(2)}) collective-permute-start(bf16[256,1664]{1,0:T(8,128)(2,1)S(1)} %pad_maximum_fusion.9), channel_id=1, source_target_pairs={{0,2},{1,3},{2,0},{3,1},{4,6},{5,7},{6,4},{7,5},{8,10},{9,11},{10,... | collective-permute-start | bytes 2555912 | tf_op jit(solution)/shard_map/ppermute | solution.py:409
  154.1 14.8 %collective-permute-start.28 = (bf16[128,1536]{1,0:T(8,128)(2,1)S(1)}, bf16[128,1536]{1,0:T(8,128)(2,1)S(1)}, u32[]{:S(2)}, u32[]{:S(2)}) collective-permute-start(bf16[128,1536]{1,0:T(8,128)(2,1)S(1)} %get-tuple-element.412), channel_id=1, source_target_pairs={{0,4},{4,0},{8,12},{12,8},{16,20},{20,16},{24,28},{28,24},{1,5},{5... | collective-permute-start | bytes 1179656 | tf_op jit(solution)/shard_map/ppermute | solution.py:405
  162.7 18.3 %collective-permute-start.25 = (bf16[256,1664]{1,0:T(8,128)(2,1)S(1)}, bf16[256,1664]{1,0:T(8,128)(2,1)S(1)}, u32[]{:S(2)}, u32[]{:S(2)}) collective-permute-start(bf16[256,1664]{1,0:T(8,128)(2,1)S(1)} %pad_maximum_fusion.10), channel_id=1, source_target_pairs={{0,2},{1,3},{2,0},{3,1},{4,6},{5,7},{6,4},{7,5},{8,10},{9,11},{10,... | collective-permute-start | bytes 2555912 | tf_op jit(solution)/shard_map/ppermute | solution.py:409
  168.9 18.9 %collective-permute-start.32 = (bf16[128,1536]{1,0:T(8,128)(2,1)S(1)}, bf16[128,1536]{1,0:T(8,128)(2,1)S(1)}, u32[]{:S(2)}, u32[]{:S(2)}) collective-permute-start(bf16[128,1536]{1,0:T(8,128)(2,1)S(1)} %get-tuple-element.411), channel_id=1, source_target_pairs={{0,4},{4,0},{8,12},{12,8},{16,20},{20,16},{24,28},{28,24},{1,5},{5... | collective-permute-start | bytes 1179656 | tf_op jit(solution)/shard_map/ppermute | solution.py:405
  195.9 18.9 %collective-permute-start.33 = (bf16[2048,1664]{1,0:T(8,128)(2,1)}, bf16[2048,1664]{1,0:T(8,128)(2,1)}, u32[]{:S(2)}, u32[]{:S(2)}) collective-permute-start(bf16[2048,1664]{1,0:T(8,128)(2,1)} %get-tuple-element.428), channel_id=1, source_target_pairs={{0,1},{1,0},{2,3},{3,2},{4,5},{5,4},{6,7},{7,6},{8,9},{9,8},{10,11... | collective-permute-start | bytes 20447240 | tf_op jit(solution)/shard_map/ppermute | solution.py:409
  203.4 93.2 %all-to-all-start.1 = ((bf16[8,192,1280]{2,1,0:T(8,128)(2,1)}), bf16[8,192,1280]{2,1,0:T(8,128)(2,1)}, u32[]{:S(2)}, u32[]{:S(2)}) async-start(bf16[8,192,1280]{2,1,0:T(8,128)(2,1)} %copy.119), calls=%async_computation.1 | async-start | bytes 7864320 | tf_op jit(solution)/shard_map/all_to_all | solution.py:969
  311.8 14.9 %collective-permute-start.37 = (bf16[128,1536]{1,0:T(8,128)(2,1)}, bf16[128,1536]{1,0:T(8,128)(2,1)}, u32[]{:S(2)}, u32[]{:S(2)}) collective-permute-start(bf16[128,1536]{1,0:T(8,128)(2,1)} %collective-permute-done.35), channel_id=1, source_target_pairs={{8,0},{12,4},{16,24},{20,28},{9,1},{13,5},{17,25},{21,29},{10,2},{... | collective-permute-start | bytes 1179656 | tf_op jit(solution)/shard_map/ppermute | solution.py:405
  326.8 17.0 %collective-permute-start.42 = (bf16[256,1536]{1,0:T(8,128)(2,1)S(1)}, bf16[256,1536]{1,0:T(8,128)(2,1)S(1)}, u32[]{:S(2)}, u32[]{:S(2)}) collective-permute-start(bf16[256,1536]{1,0:T(8,128)(2,1)S(1)} %pad_maximum_fusion.13), channel_id=1, source_target_pairs={{0,4},{4,0},{8,12},{12,8},{16,20},{20,16},{24,28},{28,24},{1,5},{5... | collective-permute-start | bytes 2359304 | tf_op jit(solution)/shard_map/ppermute | solution.py:405
  328.3 16.7 %collective-permute-start.41 = (bf16[256,1536]{1,0:T(8,128)(2,1)S(1)}, bf16[256,1536]{1,0:T(8,128)(2,1)S(1)}, u32[]{:S(2)}, u32[]{:S(2)}) collective-permute-start(bf16[256,1536]{1,0:T(8,128)(2,1)S(1)} %pad_maximum_fusion.12), channel_id=1, source_target_pairs={{0,2},{1,3},{2,0},{3,1},{4,6},{5,7},{6,4},{7,5},{8,10},{9,11},{10,... | collective-permute-start | bytes 2359304 | tf_op jit(solution)/shard_map/ppermute | solution.py:409
  349.9 19.3 %collective-permute-start.45 = (bf16[1024,1536]{1,0:T(8,128)(2,1)}, bf16[1024,1536]{1,0:T(8,128)(2,1)S(1)}, u32[]{:S(2)}, u32[]{:S(2)}) collective-permute-start(bf16[1024,1536]{1,0:T(8,128)(2,1)} %get-tuple-element.441), channel_id=1, source_target_pairs={{0,1},{1,0},{2,3},{3,2},{4,5},{5,4},{6,7},{7,6},{8,9},{9,8},{10,11... | collective-permute-start | bytes 9437192 | tf_op jit(solution)/shard_map/ppermute | solution.py:409
  351.7 17.6 %collective-permute-start.44 = (bf16[128,1536]{1,0:T(8,128)(2,1)S(1)}, bf16[128,1536]{1,0:T(8,128)(2,1)S(1)}, u32[]{:S(2)}, u32[]{:S(2)}) collective-permute-start(bf16[128,1536]{1,0:T(8,128)(2,1)S(1)} %pad_maximum_fusion.20), channel_id=1, source_target_pairs={{0,2},{1,3},{2,0},{3,1},{4,6},{5,7},{6,4},{7,5},{8,10},{9,11},{10,... | collective-permute-start | bytes 1179656 | tf_op jit(solution)/shard_map/ppermute | solution.py:409
  352.3 17.0 %collective-permute-start.43 = (bf16[128,1536]{1,0:T(8,128)(2,1)S(1)}, bf16[128,1536]{1,0:T(8,128)(2,1)S(1)}, u32[]{:S(2)}, u32[]{:S(2)}) collective-permute-start(bf16[128,1536]{1,0:T(8,128)(2,1)S(1)} %pad_maximum_fusion.19), channel_id=1, source_target_pairs={{0,4},{4,0},{8,12},{12,8},{16,20},{20,16},{24,28},{28,24},{1,5},{5... | collective-permute-start | bytes 1179656 | tf_op jit(solution)/shard_map/ppermute | solution.py:405
  369.4 19.3 %collective-permute-start.47 = (bf16[256,1536]{1,0:T(8,128)(2,1)S(1)}, bf16[256,1536]{1,0:T(8,128)(2,1)S(1)}, u32[]{:S(2)}, u32[]{:S(2)}) collective-permute-start(bf16[256,1536]{1,0:T(8,128)(2,1)S(1)} %pad_maximum_fusion.15), channel_id=1, source_target_pairs={{0,4},{4,0},{8,12},{12,8},{16,20},{20,16},{24,28},{28,24},{1,5},{5... | collective-permute-start | bytes 2359304 | tf_op jit(solution)/shard_map/ppermute | solution.py:405
  370.5 19.1 %collective-permute-start.46 = (bf16[256,1536]{1,0:T(8,128)(2,1)S(1)}, bf16[256,1536]{1,0:T(8,128)(2,1)S(1)}, u32[]{:S(2)}, u32[]{:S(2)}) collective-permute-start(bf16[256,1536]{1,0:T(8,128)(2,1)S(1)} %pad_maximum_fusion.14), channel_id=1, source_target_pairs={{0,2},{1,3},{2,0},{3,1},{4,6},{5,7},{6,4},{7,5},{8,10},{9,11},{10,... | collective-permute-start | bytes 2359304 | tf_op jit(solution)/shard_map/ppermute | solution.py:409
  394.6 23.3 %collective-permute-start.48 = (bf16[1024,1536]{1,0:T(8,128)(2,1)}, bf16[1024,1536]{1,0:T(8,128)(2,1)S(1)}, u32[]{:S(2)}, u32[]{:S(2)}) collective-permute-start(bf16[1024,1536]{1,0:T(8,128)(2,1)} %get-tuple-element.436), channel_id=1, source_target_pairs={{0,1},{1,0},{2,3},{3,2},{4,5},{5,4},{6,7},{7,6},{8,9},{9,8},{10,11... | collective-permute-start | bytes 9437192 | tf_op jit(solution)/shard_map/ppermute | solution.py:409
  454.3 18.9 %collective-permute-start.49 = (bf16[1024,1536]{1,0:T(8,128)(2,1)S(1)}, bf16[1024,1536]{1,0:T(8,128)(2,1)}, u32[]{:S(2)}, u32[]{:S(2)}) collective-permute-start(bf16[1024,1536]{1,0:T(8,128)(2,1)S(1)} %slice.465), channel_id=1, source_target_pairs={{0,1},{1,0},{2,3},{3,2},{4,5},{5,4},{6,7},{7,6},{8,9},{9,8},{10,11... | collective-permute-start | bytes 9437192 | tf_op jit(solution)/shard_map/ppermute | solution.py:409
  455.1 32.7 %collective-permute-start.52 = (bf16[1024,1536]{1,0:T(8,128)(2,1)S(1)}, bf16[1024,1536]{1,0:T(8,128)(2,1)S(1)}, u32[]{:S(2)}, u32[]{:S(2)}) collective-permute-start(bf16[1024,1536]{1,0:T(8,128)(2,1)S(1)} %slice.389), channel_id=1, source_target_pairs={{0,1},{1,0},{2,3},{3,2},{4,5},{5,4},{6,7},{7,6},{8,9},{9,8},{10,11... | collective-permute-start | bytes 9437192 | tf_op jit(solution)/shard_map/ppermute | solution.py:409
  478.4 20.2 %collective-permute-start.50 = (bf16[256,1536]{1,0:T(8,128)(2,1)S(1)}, bf16[256,1536]{1,0:T(8,128)(2,1)S(1)}, u32[]{:S(2)}, u32[]{:S(2)}) collective-permute-start(bf16[256,1536]{1,0:T(8,128)(2,1)S(1)} %get-tuple-element.410), channel_id=1, source_target_pairs={{0,2},{1,3},{2,0},{3,1},{4,6},{5,7},{6,4},{7,5},{8,10},{9,11},{10,... | collective-permute-start | bytes 2359304 | tf_op jit(solution)/shard_map/ppermute | solution.py:409
  479.9 19.9 %collective-permute-start.51 = (bf16[256,1536]{1,0:T(8,128)(2,1)S(1)}, bf16[256,1536]{1,0:T(8,128)(2,1)}, u32[]{:S(2)}, u32[]{:S(2)}) collective-permute-start(bf16[256,1536]{1,0:T(8,128)(2,1)S(1)} %get-tuple-element.409), channel_id=1, source_target_pairs={{0,4},{4,0},{8,12},{12,8},{16,20},{20,16},{24,28},{28,24},{1,5},{5... | collective-permute-start | bytes 2359304 | tf_op jit(solution)/shard_map/ppermute | solution.py:405
  503.7 28.7 %collective-permute-start.55 = (bf16[256,1536]{1,0:T(8,128)(2,1)}, bf16[256,1536]{1,0:T(8,128)(2,1)S(1)}, u32[]{:S(2)}, u32[]{:S(2)}) collective-permute-start(bf16[256,1536]{1,0:T(8,128)(2,1)} %get-tuple-element.406), channel_id=1, source_target_pairs={{0,2},{1,3},{2,0},{3,1},{4,6},{5,7},{6,4},{7,5},{8,10},{9,11},{10,... | collective-permute-start | bytes 2359304 | tf_op jit(solution)/shard_map/ppermute | solution.py:409
  504.8 27.6 %collective-permute-start.56 = (bf16[256,1536]{1,0:T(8,128)(2,1)S(1)}, bf16[256,1536]{1,0:T(8,128)(2,1)S(1)}, u32[]{:S(2)}, u32[]{:S(2)}) collective-permute-start(bf16[256,1536]{1,0:T(8,128)(2,1)S(1)} %get-tuple-element.405), channel_id=1, source_target_pairs={{0,4},{4,0},{8,12},{12,8},{16,20},{20,16},{24,28},{28,24},{1,5},{5... | collective-permute-start | bytes 2359304 | tf_op jit(solution)/shard_map/ppermute | solution.py:405
  507.2 25.2 %collective-permute-start.53 = (bf16[128,1536]{1,0:T(8,128)(2,1)S(1)}, bf16[128,1536]{1,0:T(8,128)(2,1)}, u32[]{:S(2)}, u32[]{:S(2)}) collective-permute-start(bf16[128,1536]{1,0:T(8,128)(2,1)S(1)} %slice.471), channel_id=1, source_target_pairs={{0,4},{4,0},{8,12},{12,8},{16,20},{20,16},{24,28},{28,24},{1,5},{5... | collective-permute-start | bytes 1179656 | tf_op jit(solution)/shard_map/ppermute | solution.py:405
  508.5 23.9 %collective-permute-start.54 = (bf16[128,1536]{1,0:T(8,128)(2,1)S(1)}, bf16[128,1536]{1,0:T(8,128)(2,1)S(1)}, u32[]{:S(2)}, u32[]{:S(2)}) collective-permute-start(bf16[128,1536]{1,0:T(8,128)(2,1)S(1)} %slice.473), channel_id=1, source_target_pairs={{0,2},{1,3},{2,0},{3,1},{4,6},{5,7},{6,4},{7,5},{8,10},{9,11},{10,... | collective-permute-start | bytes 1179656 | tf_op jit(solution)/shard_map/ppermute | solution.py:409
  525.8 35.5 %collective-permute-start.60 = (bf16[1024,1536]{1,0:T(8,128)(2,1)}, bf16[1024,1536]{1,0:T(8,128)(2,1)}, u32[]{:S(2)}, u32[]{:S(2)}) collective-permute-start(bf16[1024,1536]{1,0:T(8,128)(2,1)} %slice.404), channel_id=1, source_target_pairs={{0,1},{1,0},{2,3},{3,2},{4,5},{5,4},{6,7},{7,6},{8,9},{9,8},{10,11... | collective-permute-start | bytes 9437192 | tf_op jit(solution)/shard_map/ppermute | solution.py:409
  536.3 23.3 %collective-permute-start.59 = (bf16[128,1536]{1,0:T(8,128)(2,1)}, bf16[128,1536]{1,0:T(8,128)(2,1)}, u32[]{:S(2)}, u32[]{:S(2)}) collective-permute-start(bf16[128,1536]{1,0:T(8,128)(2,1)} %pad_maximum_fusion.21), channel_id=1, source_target_pairs={{0,8},{4,12},{24,16},{28,20},{1,9},{5,13},{25,17},{29,21},{2,10},{... | collective-permute-start | bytes 1179656 | tf_op jit(solution)/shard_map/ppermute | solution.py:405
  540.2 21.0 %collective-permute-start.57 = (bf16[128,1536]{1,0:T(8,128)(2,1)}, bf16[128,1536]{1,0:T(8,128)(2,1)}, u32[]{:S(2)}, u32[]{:S(2)}) collective-permute-start(bf16[128,1536]{1,0:T(8,128)(2,1)} %slice.480), channel_id=1, source_target_pairs={{0,4},{4,0},{8,12},{12,8},{16,20},{20,16},{24,28},{28,24},{1,5},{5... | collective-permute-start | bytes 1179656 | tf_op jit(solution)/shard_map/ppermute | solution.py:405
  541.9 19.3 %collective-permute-start.58 = (bf16[128,1536]{1,0:T(8,128)(2,1)}, bf16[128,1536]{1,0:T(8,128)(2,1)}, u32[]{:S(2)}, u32[]{:S(2)}) collective-permute-start(bf16[128,1536]{1,0:T(8,128)(2,1)} %slice.482), channel_id=1, source_target_pairs={{0,2},{1,3},{2,0},{3,1},{4,6},{5,7},{6,4},{7,5},{8,10},{9,11},{10,... | collective-permute-start | bytes 1179656 | tf_op jit(solution)/shard_map/ppermute | solution.py:409
  553.4 18.9 %collective-permute-start.65 = (bf16[1024,1536]{1,0:T(8,128)(2,1)}, bf16[1024,1536]{1,0:T(8,128)(2,1)}, u32[]{:S(2)}, u32[]{:S(2)}) collective-permute-start(bf16[1024,1536]{1,0:T(8,128)(2,1)} %slice.411), channel_id=1, source_target_pairs={{0,1},{1,0},{2,3},{3,2},{4,5},{5,4},{6,7},{7,6},{8,9},{9,8},{10,11... | collective-permute-start | bytes 9437192 | tf_op jit(solution)/shard_map/ppermute | solution.py:409
  565.4 20.0 %collective-permute-start.63 = (bf16[256,1536]{1,0:T(8,128)(2,1)S(1)}, bf16[256,1536]{1,0:T(8,128)(2,1)S(1)}, u32[]{:S(2)}, u32[]{:S(2)}) collective-permute-start(bf16[256,1536]{1,0:T(8,128)(2,1)S(1)} %get-tuple-element.402), channel_id=1, source_target_pairs={{0,2},{1,3},{2,0},{3,1},{4,6},{5,7},{6,4},{7,5},{8,10},{9,11},{10,... | collective-permute-start | bytes 2359304 | tf_op jit(solution)/shard_map/ppermute | solution.py:409
  566.9 19.7 %collective-permute-start.64 = (bf16[256,1536]{1,0:T(8,128)(2,1)S(1)}, bf16[256,1536]{1,0:T(8,128)(2,1)S(1)}, u32[]{:S(2)}, u32[]{:S(2)}) collective-permute-start(bf16[256,1536]{1,0:T(8,128)(2,1)S(1)} %get-tuple-element.401), channel_id=1, source_target_pairs={{0,4},{4,0},{8,12},{12,8},{16,20},{20,16},{24,28},{28,24},{1,5},{5... | collective-permute-start | bytes 2359304 | tf_op jit(solution)/shard_map/ppermute | solution.py:405
  589.4 37.0 %collective-permute-start.70 = (bf16[256,1536]{1,0:T(8,128)(2,1)S(1)}, bf16[256,1536]{1,0:T(8,128)(2,1)S(1)}, u32[]{:S(2)}, u32[]{:S(2)}) collective-permute-start(bf16[256,1536]{1,0:T(8,128)(2,1)S(1)} %get-tuple-element.398), channel_id=1, source_target_pairs={{0,2},{1,3},{2,0},{3,1},{4,6},{5,7},{6,4},{7,5},{8,10},{9,11},{10,... | collective-permute-start | bytes 2359304 | tf_op jit(solution)/shard_map/ppermute | solution.py:409
  590.1 36.4 %collective-permute-start.71 = (bf16[256,1536]{1,0:T(8,128)(2,1)S(1)}, bf16[256,1536]{1,0:T(8,128)(2,1)S(1)}, u32[]{:S(2)}, u32[]{:S(2)}) collective-permute-start(bf16[256,1536]{1,0:T(8,128)(2,1)S(1)} %get-tuple-element.397), channel_id=1, source_target_pairs={{0,4},{4,0},{8,12},{12,8},{16,20},{20,16},{24,28},{28,24},{1,5},{5... | collective-permute-start | bytes 2359304 | tf_op jit(solution)/shard_map/ppermute | solution.py:405
  591.6 25.4 %collective-permute-start.68 = (bf16[128,1536]{1,0:T(8,128)(2,1)S(1)}, bf16[128,1536]{1,0:T(8,128)(2,1)S(1)}, u32[]{:S(2)}, u32[]{:S(2)}) collective-permute-start(bf16[128,1536]{1,0:T(8,128)(2,1)S(1)} %slice.493), channel_id=1, source_target_pairs={{0,4},{4,0},{8,12},{12,8},{16,20},{20,16},{24,28},{28,24},{1,5},{5... | collective-permute-start | bytes 1179656 | tf_op jit(solution)/shard_map/ppermute | solution.py:405
  592.6 33.8 %collective-permute-start.69 = (bf16[128,1536]{1,0:T(8,128)(2,1)S(1)}, bf16[128,1536]{1,0:T(8,128)(2,1)S(1)}, u32[]{:S(2)}, u32[]{:S(2)}) collective-permute-start(bf16[128,1536]{1,0:T(8,128)(2,1)S(1)} %slice.495), channel_id=1, source_target_pairs={{0,2},{1,3},{2,0},{3,1},{4,6},{5,7},{6,4},{7,5},{8,10},{9,11},{10,... | collective-permute-start | bytes 1179656 | tf_op jit(solution)/shard_map/ppermute | solution.py:409
  594.2 32.2 %collective-permute-start.67 = (bf16[128,1536]{1,0:T(8,128)(2,1)S(1)}, bf16[128,1536]{1,0:T(8,128)(2,1)S(1)}, u32[]{:S(2)}, u32[]{:S(2)}) collective-permute-start(bf16[128,1536]{1,0:T(8,128)(2,1)S(1)} %add_convert_fusion.24), channel_id=1, source_target_pairs={{8,16},{12,20},{16,8},{20,12},{9,17},{13,21},{17,9},{21,13},{10,18... | collective-permute-start | bytes 1179656 | tf_op jit(solution)/shard_map/ppermute | solution.py:405
  629.3 18.1 %collective-permute-start.72 = (bf16[128,1536]{1,0:T(8,128)(2,1)S(1)}, bf16[128,1536]{1,0:T(8,128)(2,1)S(1)}, u32[]{:S(2)}, u32[]{:S(2)}) collective-permute-start(bf16[128,1536]{1,0:T(8,128)(2,1)S(1)} %get-tuple-element.377), channel_id=1, source_target_pairs={{0,8},{4,12},{8,0},{12,4},{16,24},{20,28},{24,16},{28,20},{1,9},{5... | collective-permute-start | bytes 1179656 | tf_op jit(solution)/shard_map/ppermute | solution.py:405
  631.4 14.9 %collective-permute-start.77 = (bf16[128,1536]{1,0:T(8,128)(2,1)S(1)}, bf16[128,1536]{1,0:T(8,128)(2,1)S(1)}, u32[]{:S(2)}, u32[]{:S(2)}) collective-permute-start(bf16[128,1536]{1,0:T(8,128)(2,1)S(1)} %pad_maximum_fusion.23), channel_id=1, source_target_pairs={{0,8},{4,12},{24,16},{28,20},{1,9},{5,13},{25,17},{29,21},{2,10},{... | collective-permute-start | bytes 1179656 | tf_op jit(solution)/shard_map/ppermute | solution.py:405
  671.3 17.8 %collective-permute-start.85 = (bf16[128,1536]{1,0:T(8,128)(2,1)S(1)}, bf16[128,1536]{1,0:T(8,128)(2,1)S(1)}, u32[]{:S(2)}, u32[]{:S(2)}) collective-permute-start(bf16[128,1536]{1,0:T(8,128)(2,1)S(1)} %add_convert_fusion.18), channel_id=1, source_target_pairs={{0,8},{4,12},{8,0},{12,4},{16,24},{20,28},{24,16},{28,20},{1,9},{5... | collective-permute-start | bytes 1179656 | tf_op jit(solution)/shard_map/ppermute | solution.py:405
  703.5 89.6 %all-to-all-start.2 = ((bf16[8,192,1280]{2,1,0:T(8,128)(2,1)}), bf16[8,192,1280]{2,1,0:T(8,128)(2,1)}, u32[]{:S(2)}, u32[]{:S(2)}) async-start(bf16[8,192,1280]{2,1,0:T(8,128)(2,1)} %bitcast.157), calls=%async_computation.2 | async-start | bytes 7864320 | tf_op jit(solution)/shard_map/all_to_all | solution.py:1158
  736.6 21.9 %collective-permute-start.88 = (bf16[128,1536]{1,0:T(8,128)(2,1)}, bf16[128,1536]{1,0:T(8,128)(2,1)}, u32[]{:S(2)}, u32[]{:S(2)}) collective-permute-start(bf16[128,1536]{1,0:T(8,128)(2,1)} %get-tuple-element.394), channel_id=1, source_target_pairs={{0,4},{4,0},{8,12},{12,8},{16,20},{20,16},{24,28},{28,24},{1,5},{5... | collective-permute-start | bytes 1179656 | tf_op jit(solution)/shard_map/ppermute | solution.py:405
  747.8 23.6 %collective-permute-start.90 = (bf16[128,1536]{1,0:T(8,128)(2,1)}, bf16[128,1536]{1,0:T(8,128)(2,1)}, u32[]{:S(2)}, u32[]{:S(2)}) collective-permute-start(bf16[128,1536]{1,0:T(8,128)(2,1)} %get-tuple-element.393), channel_id=1, source_target_pairs={{0,4},{4,0},{8,12},{12,8},{16,20},{20,16},{24,28},{28,24},{1,5},{5... | collective-permute-start | bytes 1179656 | tf_op jit(solution)/shard_map/ppermute | solution.py:405
  758.6 16.8 %collective-permute-start.91 = (bf16[2,8,48,640]{3,2,1,0:T(8,128)(2,1)S(1)}, bf16[2,8,48,640]{3,2,1,0:T(8,128)(2,1)S(1)}, u32[]{:S(2)}, u32[]{:S(2)}) collective-permute-start(bf16[2,8,48,640]{3,2,1,0:T(8,128)(2,1)S(1)} %pad_maximum_fusion.7), channel_id=1, source_target_pairs={{0,1},{1,0},{2,3},{3,2},{4,5},{5,4},{6,7},{7,6},{8,9},{9,8},{10,11... | collective-permute-start | bytes 2949128 | tf_op jit(solution)/shard_map/ppermute | solution.py:409
  760.0 15.4 %collective-permute-start.89 = (bf16[128,1536]{1,0:T(8,128)(2,1)S(1)}, bf16[128,1536]{1,0:T(8,128)(2,1)S(1)}, u32[]{:S(2)}, u32[]{:S(2)}) collective-permute-start(bf16[128,1536]{1,0:T(8,128)(2,1)S(1)} %add_convert_fusion.16), channel_id=1, source_target_pairs={{0,8},{4,12},{24,16},{28,20},{1,9},{5,13},{25,17},{29,21},{2,10},{... | collective-permute-start | bytes 1179656 | tf_op jit(solution)/shard_map/ppermute | solution.py:405
  763.8 42.5 %collective-permute-start.94 = (bf16[128,1536]{1,0:T(8,128)(2,1)}, bf16[128,1536]{1,0:T(8,128)(2,1)}, u32[]{:S(2)}, u32[]{:S(2)}) collective-permute-start(bf16[128,1536]{1,0:T(8,128)(2,1)} %get-tuple-element.392), channel_id=1, source_target_pairs={{0,4},{4,0},{8,12},{12,8},{16,20},{20,16},{24,28},{28,24},{1,5},{5... | collective-permute-start | bytes 1179656 | tf_op jit(solution)/shard_map/ppermute | solution.py:405
  776.4 29.9 %collective-permute-start.95 = (bf16[8,48,640]{2,1,0:T(8,128)(2,1)}, bf16[8,48,640]{2,1,0:T(8,128)(2,1)}, u32[]{:S(2)}, u32[]{:S(2)}) collective-permute-start(bf16[8,48,640]{2,1,0:T(8,128)(2,1)} %fusion.9), channel_id=1, source_target_pairs={{0,2},{1,3},{2,0},{3,1},{4,6},{5,7},{6,4},{7,5},{8,10},{9,11},{10,... | collective-permute-start | bytes 1474568 | tf_op jit(solution)/shard_map/ppermute | solution.py:409
  779.0 27.3 %collective-permute-start.93 = (bf16[128,1536]{1,0:T(8,128)(2,1)S(1)}, bf16[128,1536]{1,0:T(8,128)(2,1)}, u32[]{:S(2)}, u32[]{:S(2)}) collective-permute-start(bf16[128,1536]{1,0:T(8,128)(2,1)S(1)} %add_convert_fusion.14), channel_id=1, source_target_pairs={{0,8},{4,12},{24,16},{28,20},{1,9},{5,13},{25,17},{29,21},{2,10},{... | collective-permute-start | bytes 1179656 | tf_op jit(solution)/shard_map/ppermute | solution.py:405
  785.1 21.2 %collective-permute-start.92 = (bf16[128,1536]{1,0:T(8,128)(2,1)}, bf16[128,1536]{1,0:T(8,128)(2,1)}, u32[]{:S(2)}, u32[]{:S(2)}) collective-permute-start(bf16[128,1536]{1,0:T(8,128)(2,1)} %add_convert_fusion.15), channel_id=1, source_target_pairs={{8,16},{12,20},{16,8},{20,12},{9,17},{13,21},{17,9},{21,13},{10,18... | collective-permute-start | bytes 1179656 | tf_op jit(solution)/shard_map/ppermute | solution.py:405
  787.6 39.7 %collective-permute-start.98 = (bf16[128,1536]{1,0:T(8,128)(2,1)}, bf16[128,1536]{1,0:T(8,128)(2,1)S(1)}, u32[]{:S(2)}, u32[]{:S(2)}) collective-permute-start(bf16[128,1536]{1,0:T(8,128)(2,1)} %get-tuple-element.391), channel_id=1, source_target_pairs={{0,4},{4,0},{8,12},{12,8},{16,20},{20,16},{24,28},{28,24},{1,5},{5... | collective-permute-start | bytes 1179656 | tf_op jit(solution)/shard_map/ppermute | solution.py:405
  808.3 21.4 %all-to-all-start.3 = ((bf16[8,48,640]{2,1,0:T(8,128)(2,1)}), bf16[8,48,640]{2,1,0:T(8,128)(2,1)S(1)}, u32[]{:S(2)}, u32[]{:S(2)}) async-start(bf16[8,48,640]{2,1,0:T(8,128)(2,1)} %fusion.8), calls=%async_computation.3 | async-start | bytes 983040 | tf_op jit(solution)/shard_map/all_to_all | solution.py:1222
  (95 other events, 1314.0 us)

commit v2 on v1

--- a/solution.py
+++ b/solution.py
@@ -548,7 +548,9 @@
         works.append(work)
         return outs
 
-    near, middle = run((over_dp(piece, Z_NEAR), over_dp(piece, Z_MIDDLE)), (piece,))
+    near, middle = run(
+        (over_dp(piece, Z_NEAR), over_dp(piece, Z_MIDDLE)), (piece,), covers[0]
+    )
 
     def split(first, second):
         (ft, fl), (st, sl) = halves(first), halves(second)
@@ -558,25 +560,25 @@
     far, out1, y_top, x_low = run(
         (over_dp(near, Z_MIDDLE), over_dp(middle, Z_OUT), swap_y(top), swap_x(low)),
         (top, low),
-        covers[0],
+        covers[1],
     )
     third = middle + out1
     top, low = joined(top, y_top), joined(low, x_low)
     out2, x_top, y_low = run(
-        (over_dp(far, Z_OUT), swap_x(top), swap_y(low)), (top, low), covers[1]
+        (over_dp(far, Z_OUT), swap_x(top), swap_y(low)), (top, low), covers[2]
     )
     here = joined(top, x_top, low, y_low)
     top, low = split(third, far + out2)
     y_top, x_low, there = run(
-        (swap_y(top), swap_x(low), swap_core(here)), (top, low, here), covers[2]
+        (swap_y(top), swap_x(low), swap_core(here)), (top, low, here), covers[3]
     )
     first = joined(here, there)
     top, low = joined(top, y_top), joined(low, x_low)
     x_top, y_low = run(
-        (swap_x(top), swap_y(low)), (top, low), lambda tie, works: covers[3](tie, works, first)
+        (swap_x(top), swap_y(low)), (top, low), lambda tie, works: covers[4](tie, works, first)
     )
     here = joined(top, x_top, low, y_low)
-    there = run(swap_core(here), (here,), covers[4])
+    there = run(swap_core(here), (here,), covers[5])
     return (first, joined(here, there)), works
 
 
@@ -871,6 +873,54 @@
     )(grads_in, o_w, queries, keys, vals, top, total, row_ids, col_ids, cosine, sine, qkv_w, x)
 
 
+def pack_kernel(x_ref, o_ref, *, width):
+    experts = x_ref.shape[0]
+    half = x_ref.shape[2] // 2
+    for i in range(o_ref.shape[0]):
+        for g in range(2):
+            at = g * half + i * width
+            row = jnp.concatenate([x_ref[e, :, at : at + width] for e in range(experts)], axis=1)
+            o_ref[i, :, g * experts * width : (g + 1) * experts * width] = row.astype(jnp.bfloat16)
+
+
+def pack_weights(weight, devices, rows=48):
+    experts, d_rows, columns = weight.shape
+    width = columns // 2 // devices
+    return pl.pallas_call(
+        functools.partial(pack_kernel, width=width),
+        out_shape=jax.ShapeDtypeStruct((devices, d_rows, 2 * experts * width), jnp.bfloat16),
+        grid=(d_rows // rows,),
+        in_specs=[pl.BlockSpec((experts, rows, columns), lambda r: (0, r, 0))],
+        out_specs=pl.BlockSpec((devices, rows, 2 * experts * width), lambda r: (0, r, 0)),
+        name="pack_weights",
+    )(weight)
+
+
+def unpack_kernel(x_ref, o_ref, *, width):
+    experts = o_ref.shape[0]
+    half = o_ref.shape[2] // 2
+    for e in range(experts):
+        for g in range(2):
+            at = (g * experts + e) * width
+            row = jnp.concatenate(
+                [x_ref[i, :, at : at + width] for i in range(x_ref.shape[0])], axis=1
+            )
+            o_ref[e, :, g * half : (g + 1) * half] = row.astype(jnp.float32)
+
+
+def unpack_grads(moved, experts, rows=48):
+    devices, d_rows, columns = moved.shape
+    width = columns // 2 // experts
+    return pl.pallas_call(
+        functools.partial(unpack_kernel, width=width),
+        out_shape=jax.ShapeDtypeStruct((experts, d_rows, 2 * devices * width), jnp.float32),
+        grid=(d_rows // rows,),
+        in_specs=[pl.BlockSpec((devices, rows, columns), lambda r: (0, r, 0))],
+        out_specs=pl.BlockSpec((experts, rows, 2 * devices * width), lambda r: (0, r, 0)),
+        name="unpack_grads",
+    )(moved)
+
+
 def after(value, *earlier):
     return lax.optimization_barrier((value, *earlier))[0]
 
@@ -938,16 +988,9 @@
         ],
         axis=1,
     )
-    d_rows = in_weight.shape[0]
 
     def pack_in(tie):
-        return (
-            tie(in_weight)
-            .astype(jnp.bfloat16)
-            .reshape(in_weight.shape[0], own_experts, 2, n_dp, ff_here)
-            .transpose(3, 0, 2, 1, 4)
-            .reshape(n_dp, in_weight.shape[0], 2 * ff_cols)
-        )
+        return pack_weights(tie(in_weight).transpose(1, 0, 2), n_dp)
 
     attn_out = jnp.concatenate(
         [
@@ -1024,29 +1067,31 @@
     cot_all, branch, attended = gather_beside_sum(cot_out, attention)
     normed, queries, keys, vals, mixed_low, run_top, run_total, _ = attended
     rows_from, meta_from = far_order(ex_index, dealt_of)
-    cot_rows, meta_all = take_blocks(
-        jnp.stack([rows_from, meta_from]),
-        cot_all,
-        [(0, 0, model), (1, model // 128, 128)],
-        tok_rows // 2,
-    )
     inputs = tokens[0].astype(jnp.float32)
     middle = inputs + RESIDUAL * branch
     second_scale = lax.rsqrt(jnp.mean(middle * middle, axis=-1, keepdims=True) + EPSILON)
     sent_rows = (middle * second_scale * gain_two).astype(jnp.bfloat16)
-    sent_rows = after(sent_rows, in_w, cot_rows)
+    sent_rows = after(sent_rows, in_w, cot_all)
     part_rows = 16 * tok_rows
+
+    def order_rows(tie, works):
+        return take_blocks(
+            jnp.stack([rows_from, meta_from]),
+            tie(cot_all),
+            [(0, 0, model), (1, model // 128, 128)],
+            tok_rows // 2,
+        )
+
+    def pull(tie, works):
+        return lax.dot_general(
+            tie(works[0][0]), down_w, COLS_DIMS, preferred_element_type=jnp.float32
+        )
 
     def spread_gates(tie, works):
         column = jnp.arange(128, dtype=jnp.int32)[:, None]
         owner = ex_index * own_experts + jnp.arange(ff_cols, dtype=jnp.int32)[None, :] // ff_here
         spread = ((column % E == owner) & (column < 3 * E)).astype(jnp.bfloat16)
-        return jnp.dot(tie(meta_all), spread, preferred_element_type=jnp.float32)
-
-    def pull(tie, works):
-        return lax.dot_general(
-            tie(cot_rows), down_w, COLS_DIMS, preferred_element_type=jnp.float32
-        )
+        return jnp.dot(tie(works[0][1]), spread, preferred_element_type=jnp.float32)
 
     def up(sent):
         return jnp.dot(sent, in_w, preferred_element_type=jnp.float32)
@@ -1071,7 +1116,7 @@
 
     def of_part(number, works, gate_up):
         rows_here = slice(number * part_rows, (number + 1) * part_rows)
-        return down(gate_up, works[2][rows_here], works[3][rows_here])
+        return down(gate_up, works[2][rows_here], works[1][rows_here])
 
     def first_up(tie, works, sent):
         return up(tie(sent))
@@ -1081,8 +1126,9 @@
         return weighted_here, grads_here, back(grads_here)
 
     sent_parts, works = gather_pairs(
-        sent_rows, (None, spread_gates, pull, first_up, first_down)
-    )
+        sent_rows, (order_rows, pull, spread_gates, None, first_up, first_down)
+    )
+    cot_rows = works[0][0]
     weighted_first, grads_first, back_first = works[5]
     weighted_second, grads_second = of_part(1, works, up(sent_parts[1]))
 
@@ -1203,21 +1249,13 @@
             lax.dynamic_index_in_dim(grads, ex_index ^ k, 1, keepdims=False) for k in range(n_ex)
         ]
 
-    def unpack_first(tie):
-        return (
-            tie(in_back)
-            .reshape(n_dp, d_rows, 2, own_experts, ff_here)
-            .transpose(3, 1, 2, 0, 4)
-            .reshape(own_experts, d_rows, 2 * FF)
-        )
-
     sums, (own_g, core_g, x_g, xc_g) = one_round(total.step(), (normed_grad_part,), weight_grads)
     total.keep(sums)
     core_pair = jnp.stack([core_g, xc_g])
     (sums, from_core), _ = one_round((total.step(), swap_core(core_pair)), (core_pair,))
     total.keep(sums)
     x_g = added(x_g, from_core[1])
-    (sums, from_x), unpacked = one_round((total.step(), swap_x(x_g)), (x_g,), unpack_first)
+    (sums, from_x), _ = one_round((total.step(), swap_x(x_g)), (x_g,))
     total.keep(sums)
     grads = lax.all_to_all(
         added(own_g, from_core[0], from_x), "dp", split_axis=0, concat_axis=0, tiled=True
@@ -1225,7 +1263,7 @@
     (sums, grads), in_grad = one_round(
         (total.step(), grads),
         (from_x,),
-        lambda tie: tie(unpacked).transpose(1, 0, 2).astype(jnp.float32),
+        lambda tie: unpack_grads(tie(in_back), own_experts).transpose(1, 0, 2),
     )
     total.keep(sums)
     grads = grads.astype(jnp.float32)

time: 864 us -> 845 us (0.978)
  local copies, waits for them, and re-layouts: 137 us -> 90.3 us
  waiting for transfers between devices: 254 us -> 269 us
  starting transfers between devices: 147 us -> 161 us
  Pallas kernels: 57.3 us -> 69.4 us
  other arithmetic: 120 us -> 111 us
    optimization_barrier x3 -> x0, local copies, waits for them, and re-layouts: 23.4 us -> none  [after(): return lax.optimization_barrier((value, *earlier))[0]]
    pallas_call x0 -> x2, Pallas kernels: none -> 12.2 us  [the longest x1 6.11 us: unpack_grads(): pl.pallas_call(functools.partial(unpack_kernel, width=width), out_shape=j...]
    transpose x2 -> x0, local copies, waits for them, and re-layouts: 11.4 us -> none  [the longest x1 5.75 us: unpack_first(): return tie(in_back).reshape(n_dp, d_rows, 2, own_experts, ff_here).transp...]
    unnamed x148 -> x145, local copies, waits for them, and re-layouts: 48.1 us -> 37.1 us
    all_to_all x1, waiting for transfers between devices: 62.7 us -> 72.5 us  [per_device(): lax.all_to_all(after(in_out, group_tokens, attn_in), 'dp', split_axis=0,...]
    all_to_all x1, starting transfers between devices: 3.48 us -> 12.5 us  [per_device(): lax.all_to_all(added(own_g, from_core[0], from_x), 'dp', split_axis=0, co...]
  transfers between devices with their start and end apart: 103 -> 103, of which waited for: 39 -> 38; matrix products, arithmetic and copies ran while one was open for 35% -> 31% of each run, Pallas kernels for 7% -> 8%
where the time goes in v2:
time: 845 us; the launch traced here: 834 us
  waiting for transfers between devices  269 us (32%)
  starting transfers between devices  161 us (19%)
  matrix products  130 us (15%)
  other arithmetic  111 us (13%)
  local copies, waits for them, and re-layouts  90.3 us (11%)
  Pallas kernels  69.4 us (8%)
    ppermute x72, waiting for transfers between devices, over_dp(): return lax.ppermute(piece, 'dp', moves)  147 us
    ppermute x72, starting transfers between devices, over_dp(): return lax.ppermute(piece, 'dp', moves)  111 us
    all_to_all x1, waiting for transfers between devices, per_device(): lax.all_to_all(after(in_out, group_tokens, attn_in), 'dp', split_axis=0,...  72.5 us
    ppermute x27, waiting for transfers between devices, over_expert(): return lax.ppermute(piece, 'expert', moves)  45.4 us
    unnamed x145, local copies, waits for them, and re-layouts  37.1 us
    convert_element_type x34, other arithmetic, added(): return total.astype(jnp.bfloat16)  33.8 us
    dot_general x2, matrix products, up(): return jnp.dot(sent, in_w, preferred_element_type=jnp.float32)  27.9 us
    pallas_call x1, Pallas kernels, rear(): pl.pallas_call(functools.partial(rear_kernel, heads=heads, rows=min(256,...  24.3 us
  transfers between devices with their start and end apart: 103, of which 38 were waited for; matrix products, arithmetic and copies ran while one was open for 31% of the time, Pallas kernels for 8%

profile of v2, /device:TPU:0, one launch (start us, length us, event | category | flops | bytes accessed | tf_op | source)
XLA Modules:
  0.0 833.7 jit_solution(1391000972174687927)
XLA Ops:
  0.7 3.1 collective-permute-start
  14.9 5.0 all-to-all-start
  27.9 6.1 pack_weights.1
  36.4 2.8 collective-permute-done.4
  47.6 4.3 collective-permute-done.7
  51.9 3.6 collective-permute-done.6
  65.7 5.3 collective-permute-done.8
  77.0 3.3 collective-permute-done.13
  91.0 2.9 fusion.15
  93.9 20.2 %front.1 = (bf16[1024,1536]{1,0:T(8,128)(2,1)}, bf16[1024,192]{1,0:T(8,128)(2,1)}, bf16[1024,64]{1,0:T(8,128)(2,1)}, bf16[1024,64]{1,0:T(8,128)(2,1)}, bf16[1024...) custom-call(bf16[1024,1536]{1,0:T(8,128)(2,1)} %copy-done.3, ...), custom_call_target="tpu_custom_call" | custom-call | tf_op jit(solution)/shard_map/front/pallas_call | solution.py:773
  125.3 8.2 collective-permute-done.18
  138.5 5.5 collective-permute-start.22
  153.0 3.5 collective-permute-done.20
  167.5 7.4 collective-permute-done.24
  174.9 3.0 collective-permute-done.25
  184.8 4.5 collective-permute-done.30
  189.4 4.7 collective-permute-done.29
  195.4 4.5 all-to-all-start.1
  209.6 6.3 constant_dynamic-update-slice_fusion.20.refs_0_.refs_1_.refs_2_.refs_3_.refs_4_.refs_5_.refs_6_.refs_7_.refs_8_.refs_9_.refs_10_.refs_11_.refs_12_.refs_13_.refs_14_.refs_15_
  215.9 72.5 %all-to-all-done.1 = bf16[8,192,1280]{2,1,0:T(8,128)(2,1)} async-done(((bf16[8,192,1280]{2,1,0:T(8,128)(2,1)}), bf16[8,192,1280]{2,1,0:T(8,128)(2,1)}, u32[]{:S(2)}, u32[]{:S(2)}) %all-to-all-start.1) | async-done | bytes 3932192 | tf_op jit(solution)/shard_map/all_to_all | solution.py:1012
  289.1 12.7 %take_blocks.1 = (bf16[4096,1536]{1,0:T(8,128)(2,1)}, bf16[4096,128]{1,0:T(8,128)(2,1)}) custom-call(s32[2,64]{1,0:T(2,128)} %pad_add_fusion.2.index_ref, bf16[4096,1664]{1,0:T(8,128)(2,1)} %constant_dynamic-update-slice_fusion.20.refs_0_.refs_1_.refs_2_.refs_3_.refs_4_.refs_5_.refs_6_.refs_7_.refs_8_.refs_9_.refs_10_.refs_11_.refs_12_.refs_13_.refs_14_.refs_15_, ...), custom_call_target="tpu_custom_call" | custom-call | tf_op jit(solution)/shard_map/take_blocks/pallas_call | solution.py:682
  308.4 15.3 %fusion.79 = f32[4096,640]{1,0:T(8,128)} fusion(bf16[4096,1536]{1,0:T(8,128)(2,1)} %get-tuple-element.219, bf16[640,1536]{1,0:T(8,128)(2,1)S(1)} %bitcast.161), kind=kOutput, calls=%fused_computation.406 | convolution fusion | flops 8053063680 | bytes 25034752 | tf_op jit(solution)/shard_map/dot_general | solution.py:1086
  328.8 11.1 %collective-permute-done.40 = bf16[128,1536]{1,0:T(8,128)(2,1)S(1)} collective-permute-done((bf16[128,1536]{1,0:T(8,128)(2,1)S(1)}, bf16[128,1536]{1,0:T(8,128)(2,1)S(1)}, u32[]{:S(2)}, u32[]{:S(2)}) %collective-permute-start.40) | collective-permute-done | bytes 393248 | tf_op jit(solution)/shard_map/ppermute | solution.py:405
  351.0 9.4 %collective-permute-done.44 = bf16[128,1536]{1,0:T(8,128)(2,1)S(1)} collective-permute-done((bf16[128,1536]{1,0:T(8,128)(2,1)S(1)}, bf16[128,1536]{1,0:T(8,128)(2,1)S(1)}, u32[]{:S(2)}, u32[]{:S(2)}) %collective-permute-start.44) | collective-permute-done | bytes 393248 | tf_op jit(solution)/shard_map/ppermute | solution.py:409
  365.8 14.0 %fusion.80 = f32[2048,1280]{1,0:T(8,128)} fusion(bf16[2048,1536]{1,0:T(8,128)(2,1)} %constant_dynamic-update-slice_fusion.41, bf16[1536,1280]{1,0:T(8,128)(2,1)} %bitcast.40), kind=kOutput, calls=%fused_computation.407 | convolution fusion | flops 8053063680 | bytes 20709376 | tf_op jit(solution)/shard_map/dot_general | solution.py:1097
  386.0 8.3 multiply_convert_fusion.5
  396.9 12.2 %convolution_convert_fusion.3 = bf16[2048,1536]{1,0:T(8,128)(2,1)} fusion(bf16[1536,1280]{1,0:T(8,128)(2,1)} %bitcast.40, bf16[2048,640]{1,0:T(8,128)(2,1)S(1)} %get-tuple-element.350, bf16[2048,640]{1,0:T(8,128)(2,1)S(1)} %get-tuple-element.349), kind=kOutput, calls=%fused_computation.3 | convolution fusion | flops 8066695168 | bytes 15466496 | tf_op jit(solution)/shard_map/dot_general | solution.py:1113
  411.0 13.8 %fusion.81 = f32[2048,1280]{1,0:T(8,128)} fusion(bf16[2048,1536]{1,0:T(8,128)(2,1)} %constant_dynamic-update-slice_fusion.58, bf16[1536,1280]{1,0:T(8,128)(2,1)} %bitcast.40), kind=kOutput, calls=%fused_computation.408 | convolution fusion | flops 8053063680 | bytes 20709376 | tf_op jit(solution)/shard_map/dot_general | solution.py:1097
  424.8 8.9 %multiply_convert_fusion.3 = (bf16[2048,640]{1,0:T(8,128)(2,1)S(1)}, bf16[2048,640]{1,0:T(8,128)(2,1)S(1)}, bf16[2048,640]{1,0:T(8,128)(2,1)}) fusion(f32[2048,1280]{1,0:T(8,128)} %fusion.81, f32[4096,640]{1,0:T(8,128)} %fusion.79, f32[4096,640]{1,0:T(8,128)S(1)} %fusion.17), kind=kLoop, calls=%fused_computation.17 | loop fusion | flops 26214400 | bytes 28835840 | tf_op jit(solution)/shard_map/convert.14
  433.7 11.9 %convolution_convert_fusion.2 = bf16[2048,1536]{1,0:T(8,128)(2,1)S(1)} fusion(bf16[1536,1280]{1,0:T(8,128)(2,1)} %bitcast.40, bf16[2048,640]{1,0:T(8,128)(2,1)S(1)} %get-tuple-element.348, bf16[2048,640]{1,0:T(8,128)(2,1)S(1)} %get-tuple-element.347), kind=kOutput, calls=%fused_computation.2 | convolution fusion | flops 8066695168 | bytes 15466496 | tf_op jit(solution)/shard_map/dot_general | solution.py:1113
  446.8 12.5 %fusion.82 = f32[1536,1280]{1,0:T(8,128)S(1)} fusion(bf16[2048,1536]{1,0:T(8,128)(2,1)} %constant_dynamic-update-slice_fusion.41, bf16[2048,1280]{1,0:T(8,128)(2,1)} %pad_maximum_fusion), kind=kOutput, calls=%fused_computation.409 | convolution fusion | flops 8053063680 | bytes 19398656 | tf_op jit(solution)/shard_map/dot_general | solution.py:1146
  459.3 5.4 convolution_convert_fusion.1
  464.8 5.0 add_convert_fusion.3
  472.0 7.0 convolution_convert_fusion
  479.1 10.9 %collective-permute-done.50 = bf16[256,1536]{1,0:T(8,128)(2,1)S(1)} collective-permute-done((bf16[256,1536]{1,0:T(8,128)(2,1)S(1)}, bf16[256,1536]{1,0:T(8,128)(2,1)S(1)}, u32[]{:S(2)}, u32[]{:S(2)}) %collective-permute-start.50) | collective-permute-done | bytes 786464 | tf_op jit(solution)/shard_map/ppermute | solution.py:409
  491.3 2.9 add_convert_fusion.2
  501.0 14.0 %fusion.6 = f32[1536,1280]{1,0:T(8,128)} fusion(bf16[2048,1536]{1,0:T(8,128)(2,1)} %constant_dynamic-update-slice_fusion.58, bf16[2048,640]{1,0:T(8,128)(2,1)} %copy-done.15, bf16[2048,640]{1,0:T(8,128)(2,1)} %copy-done.14), kind=kOutput, calls=%fused_computation.28 | convolution fusion | flops 8063549440 | bytes 19398656 | tf_op jit(solution)/shard_map/dot_general | solution.py:1154
  516.9 7.0 collective-permute-done.53
  527.7 8.7 %collective-permute-start.59 = (bf16[128,1536]{1,0:T(8,128)(2,1)}, bf16[128,1536]{1,0:T(8,128)(2,1)}, u32[]{:S(2)}, u32[]{:S(2)}) collective-permute-start(bf16[128,1536]{1,0:T(8,128)(2,1)} %pad_maximum_fusion.21), channel_id=1, source_target_pairs={{0,8},{4,12},{24,16},{28,20},{1,9},{5,13},{25,17},{29,21},{2,10},{... | collective-permute-start | bytes 1179656 | tf_op jit(solution)/shard_map/ppermute | solution.py:405
  539.6 9.1 %fusion.2 = f32[640,1536]{1,0:T(8,128)} fusion(bf16[2048,640]{1,0:T(8,128)(2,1)S(1)} %copy-done.13, bf16[4096,1536]{1,0:T(8,128)(2,1)} %get-tuple-element.219), kind=kOutput, calls=%fused_computation.8 | convolution fusion | flops 4026531840 | bytes 12845056 | tf_op jit(solution)/shard_map/dot_general | solution.py:1161
  550.5 6.0 add.878
  558.2 4.0 add_convert_fusion.1
  569.4 13.0 %collective-permute-done.63 = bf16[256,1536]{1,0:T(8,128)(2,1)S(1)} collective-permute-done((bf16[256,1536]{1,0:T(8,128)(2,1)S(1)}, bf16[256,1536]{1,0:T(8,128)(2,1)S(1)}, u32[]{:S(2)}, u32[]{:S(2)}) %collective-permute-start.63) | collective-permute-done | bytes 786464 | tf_op jit(solution)/shard_map/ppermute | solution.py:409
  583.6 2.7 add_convert_fusion
  592.4 21.6 %collective-permute-done.68 = bf16[128,1536]{1,0:T(8,128)(2,1)S(1)} collective-permute-done((bf16[128,1536]{1,0:T(8,128)(2,1)S(1)}, bf16[128,1536]{1,0:T(8,128)(2,1)S(1)}, u32[]{:S(2)}, u32[]{:S(2)}) %collective-permute-start.68) | collective-permute-done | bytes 393248 | tf_op jit(solution)/shard_map/ppermute | solution.py:405
  614.0 6.7 fusion
  634.4 8.8 %collective-permute-done.77 = bf16[128,1536]{1,0:T(8,128)(2,1)S(1)} collective-permute-done((bf16[128,1536]{1,0:T(8,128)(2,1)S(1)}, bf16[128,1536]{1,0:T(8,128)(2,1)S(1)}, u32[]{:S(2)}, u32[]{:S(2)}) %collective-permute-start.77) | collective-permute-done | bytes 393248 | tf_op jit(solution)/shard_map/ppermute | solution.py:405
  644.7 7.1 collective-permute-done.74
  655.2 6.2 collective-permute-start.82
  669.2 8.3 collective-permute-start.85
  679.4 8.1 collective-permute-done.85
  687.5 4.4 collective-permute-done.83
  694.2 7.1 collective-permute-done.87
  702.1 4.7 all-to-all-start.3
  708.3 24.3 %rear.1 = (bf16[1024,320]{1,0:T(8,128)(2,1)}, bf16[1024,1536]{1,0:T(8,128)(2,1)}, f32[1,1536]{1,0:T(1,128)}) custom-call(bf16[1024,1536]{1,0:T(8,128)(2,1)} %constant_dynamic-update-slice_fusion.67.g_ref, bf16[1536,192]{1,0:T(8,128)(2,1)} %slice.456.ow_ref, bf16[1024,192]{1,0:T(8,128)(2,1)} %get-tuple-element.292.q_ref, ...), custom_call_target="tpu_custom_call" | custom-call | tf_op jit(solution)/shard_map/rear/pallas_call | solution.py:861
  737.1 3.3 convolution_convert_fusion.4
  747.1 4.4 concatenate.177
  759.2 11.2 %collective-permute-done.90 = bf16[128,1536]{1,0:T(8,128)(2,1)S(1)} collective-permute-done((bf16[128,1536]{1,0:T(8,128)(2,1)S(1)}, bf16[128,1536]{1,0:T(8,128)(2,1)S(1)}, u32[]{:S(2)}, u32[]{:S(2)}) %collective-permute-start.90) | collective-permute-done | bytes 393248 | tf_op jit(solution)/shard_map/ppermute | solution.py:405
  770.5 3.5 collective-permute-done.89
  776.7 4.4 collective-permute-start.93
  789.5 4.3 all-to-all-done.3.x_ref
  793.8 12.5 %all-to-all-start.2 = ((bf16[8,48,640]{2,1,0:T(8,128)(2,1)}), bf16[8,48,640]{2,1,0:T(8,128)(2,1)S(1)}, u32[]{:S(2)}, u32[]{:S(2)}) async-start(bf16[8,48,640]{2,1,0:T(8,128)(2,1)} %fusion.8), calls=%async_computation.2 | async-start | bytes 983040 | tf_op jit(solution)/shard_map/all_to_all | solution.py:1260
  812.7 6.1 unpack_grads.1
  818.8 6.0 collective-permute-done.96
  (500 shorter events, 264.5 us)
Async XLA Ops:
  0.7 20.4 %collective-permute-start = (bf16[128,1536]{1,0:T(8,128)(2,1)}, bf16[128,1536]{1,0:T(8,128)(2,1)}, u32[]{:S(2)}, u32[]{:S(2)}) collective-permute-start(bf16[128,1536]{1,0:T(8,128)(2,1)} %bitcast.155), channel_id=1, source_target_pairs={{0,8},{4,12},{8,0},{12,4},{16,24},{20,28},{24,16},{28,20},{1,9},{5... | collective-permute-start | bytes 1179656 | tf_op jit(solution)/shard_map/ppermute | solution.py:405
  3.8 17.3 %collective-permute-start.1 = (bf16[128,1536]{1,0:T(8,128)(2,1)}, bf16[128,1536]{1,0:T(8,128)(2,1)}, u32[]{:S(2)}, u32[]{:S(2)}) collective-permute-start(bf16[128,1536]{1,0:T(8,128)(2,1)} %bitcast.156), channel_id=1, source_target_pairs={{8,16},{12,20},{16,8},{20,12},{9,17},{13,21},{17,9},{21,13},{10,18... | collective-permute-start | bytes 1179656 | tf_op jit(solution)/shard_map/ppermute | solution.py:405
  5.2 15.9 %collective-permute-start.2 = (bf16[128,1536]{1,0:T(8,128)(2,1)}, bf16[128,1536]{1,0:T(8,128)(2,1)}, u32[]{:S(2)}, u32[]{:S(2)}) collective-permute-start(bf16[128,1536]{1,0:T(8,128)(2,1)} %bitcast.157), channel_id=1, source_target_pairs={{0,4},{4,0},{8,12},{12,8},{16,20},{20,16},{24,28},{28,24},{1,5},{5... | collective-permute-start | bytes 1179656 | tf_op jit(solution)/shard_map/ppermute | solution.py:405
  14.9 30.2 %all-to-all-start = ((bf16[8,48,640]{2,1,0:T(8,128)(2,1)}), bf16[8,48,640]{2,1,0:T(8,128)(2,1)}, u32[]{:S(2)}, u32[]{:S(2)}) async-start(bf16[8,48,640]{2,1,0:T(8,128)(2,1)} %bitcast.23), calls=%async_computation | async-start | bytes 983040 | tf_op jit(solution)/shard_map/all_to_all | solution.py:1005
  24.5 14.6 %collective-permute-start.4 = (bf16[128,1536]{1,0:T(8,128)(2,1)}, bf16[128,1536]{1,0:T(8,128)(2,1)}, u32[]{:S(2)}, u32[]{:S(2)}) collective-permute-start(bf16[128,1536]{1,0:T(8,128)(2,1)} %collective-permute-done.1), channel_id=1, source_target_pairs={{8,0},{12,4},{16,24},{20,28},{9,1},{13,5},{17,25},{21,29},{10,2},{... | collective-permute-start | bytes 1179656 | tf_op jit(solution)/shard_map/ppermute | solution.py:405
  58.7 21.6 %collective-permute-start.13 = (bf16[2,8,48,640]{3,2,0,1:T(8,128)(2,1)}, bf16[2,8,48,640]{3,2,0,1:T(8,128)(2,1)}, u32[]{:S(2)}, u32[]{:S(2)}) collective-permute-start(bf16[2,8,48,640]{3,2,0,1:T(8,128)(2,1)} %pad_maximum_fusion.6), channel_id=1, source_target_pairs={{0,2},{1,3},{2,0},{3,1},{4,6},{5,7},{6,4},{7,5},{8,10},{9,11},{10,... | collective-permute-start | bytes 2949128 | tf_op jit(solution)/shard_map/ppermute | solution.py:409
  71.9 42.1 %collective-permute-start.10 = (bf16[128,1664]{1,0:T(8,128)(2,1)}, bf16[128,1664]{1,0:T(8,128)(2,1)}, u32[]{:S(2)}, u32[]{:S(2)}) collective-permute-start(bf16[128,1664]{1,0:T(8,128)(2,1)} %concatenate.138), channel_id=1, source_target_pairs={{8,16},{12,20},{16,8},{20,12},{9,17},{13,21},{17,9},{21,13},{10,18... | collective-permute-start | bytes 1277960 | tf_op jit(solution)/shard_map/ppermute | solution.py:405
  73.7 40.4 %collective-permute-start.11 = (bf16[128,1664]{1,0:T(8,128)(2,1)}, bf16[128,1664]{1,0:T(8,128)(2,1)}, u32[]{:S(2)}, u32[]{:S(2)}) collective-permute-start(bf16[128,1664]{1,0:T(8,128)(2,1)} %concatenate.138), channel_id=1, source_target_pairs={{0,4},{4,0},{8,12},{12,8},{16,20},{20,16},{24,28},{28,24},{1,5},{5... | collective-permute-start | bytes 1277960 | tf_op jit(solution)/shard_map/ppermute | solution.py:405
  74.5 39.6 %collective-permute-start.9 = (bf16[128,1664]{1,0:T(8,128)(2,1)}, bf16[128,1664]{1,0:T(8,128)(2,1)}, u32[]{:S(2)}, u32[]{:S(2)}) collective-permute-start(bf16[128,1664]{1,0:T(8,128)(2,1)} %concatenate.138), channel_id=1, source_target_pairs={{0,8},{4,12},{8,0},{12,4},{16,24},{20,28},{24,16},{28,20},{1,9},{5... | collective-permute-start | bytes 1277960 | tf_op jit(solution)/shard_map/ppermute | solution.py:405
  114.1 20.1 %collective-permute-start.14 = (bf16[128,1664]{1,0:T(8,128)(2,1)}, bf16[128,1664]{1,0:T(8,128)(2,1)S(1)}, u32[]{:S(2)}, u32[]{:S(2)}) collective-permute-start(bf16[128,1664]{1,0:T(8,128)(2,1)} %collective-permute-done.9), channel_id=1, source_target_pairs={{8,16},{12,20},{16,8},{20,12},{9,17},{13,21},{17,9},{21,13},{10,18... | collective-permute-start | bytes 1277960 | tf_op jit(solution)/shard_map/ppermute | solution.py:405
  114.8 19.4 %collective-permute-start.16 = (bf16[128,1664]{1,0:T(8,128)(2,1)}, bf16[128,1664]{1,0:T(8,128)(2,1)S(1)}, u32[]{:S(2)}, u32[]{:S(2)}) collective-permute-start(bf16[128,1664]{1,0:T(8,128)(2,1)} %collective-permute-done.9), channel_id=1, source_target_pairs={{0,4},{4,0},{8,12},{12,8},{16,20},{20,16},{24,28},{28,24},{1,5},{5... | collective-permute-start | bytes 1277960 | tf_op jit(solution)/shard_map/ppermute | solution.py:405
  116.7 18.0 %collective-permute-start.17 = (bf16[256,1664]{1,0:T(8,128)(2,1)S(1)}, bf16[256,1664]{1,0:T(8,128)(2,1)S(1)}, u32[]{:S(2)}, u32[]{:S(2)}) collective-permute-start(bf16[256,1664]{1,0:T(8,128)(2,1)S(1)} %pad_maximum_fusion.8), channel_id=1, source_target_pairs={{0,2},{1,3},{2,0},{3,1},{4,6},{5,7},{6,4},{7,5},{8,10},{9,11},{10,... | collective-permute-start | bytes 2555912 | tf_op jit(solution)/shard_map/ppermute | solution.py:409
  133.5 18.6 %collective-permute-start.23 = (bf16[128,1536]{1,0:T(8,128)(2,1)S(1)}, bf16[128,1536]{1,0:T(8,128)(2,1)S(1)}, u32[]{:S(2)}, u32[]{:S(2)}) collective-permute-start(bf16[128,1536]{1,0:T(8,128)(2,1)S(1)} %get-tuple-element.375), channel_id=1, source_target_pairs={{0,4},{4,0},{8,12},{12,8},{16,20},{20,16},{24,28},{28,24},{1,5},{5... | collective-permute-start | bytes 1179656 | tf_op jit(solution)/shard_map/ppermute | solution.py:405
  135.8 20.7 %collective-permute-start.21 = (bf16[256,1664]{1,0:T(8,128)(2,1)S(1)}, bf16[256,1664]{1,0:T(8,128)(2,1)S(1)}, u32[]{:S(2)}, u32[]{:S(2)}) collective-permute-start(bf16[256,1664]{1,0:T(8,128)(2,1)S(1)} %pad_maximum_fusion.9), channel_id=1, source_target_pairs={{0,2},{1,3},{2,0},{3,1},{4,6},{5,7},{6,4},{7,5},{8,10},{9,11},{10,... | collective-permute-start | bytes 2555912 | tf_op jit(solution)/shard_map/ppermute | solution.py:409
  138.5 14.5 %collective-permute-start.22 = (bf16[128,1536]{1,0:T(8,128)(2,1)S(1)}, bf16[128,1536]{1,0:T(8,128)(2,1)S(1)}, u32[]{:S(2)}, u32[]{:S(2)}) collective-permute-start(bf16[128,1536]{1,0:T(8,128)(2,1)S(1)} %add_convert_fusion.35), channel_id=1, source_target_pairs={{0,8},{4,12},{24,16},{28,20},{1,9},{5,13},{25,17},{29,21},{2,10},{... | collective-permute-start | bytes 1179656 | tf_op jit(solution)/shard_map/ppermute | solution.py:405
  152.1 14.6 %collective-permute-start.28 = (bf16[128,1536]{1,0:T(8,128)(2,1)S(1)}, bf16[128,1536]{1,0:T(8,128)(2,1)S(1)}, u32[]{:S(2)}, u32[]{:S(2)}) collective-permute-start(bf16[128,1536]{1,0:T(8,128)(2,1)S(1)} %get-tuple-element.374), channel_id=1, source_target_pairs={{0,4},{4,0},{8,12},{12,8},{16,20},{20,16},{24,28},{28,24},{1,5},{5... | collective-permute-start | bytes 1179656 | tf_op jit(solution)/shard_map/ppermute | solution.py:405
  159.7 18.2 %collective-permute-start.25 = (bf16[256,1664]{1,0:T(8,128)(2,1)S(1)}, bf16[256,1664]{1,0:T(8,128)(2,1)S(1)}, u32[]{:S(2)}, u32[]{:S(2)}) collective-permute-start(bf16[256,1664]{1,0:T(8,128)(2,1)S(1)} %pad_maximum_fusion.10), channel_id=1, source_target_pairs={{0,2},{1,3},{2,0},{3,1},{4,6},{5,7},{6,4},{7,5},{8,10},{9,11},{10,... | collective-permute-start | bytes 2555912 | tf_op jit(solution)/shard_map/ppermute | solution.py:409
  166.6 18.2 %collective-permute-start.32 = (bf16[128,1536]{1,0:T(8,128)(2,1)S(1)}, bf16[128,1536]{1,0:T(8,128)(2,1)S(1)}, u32[]{:S(2)}, u32[]{:S(2)}) collective-permute-start(bf16[128,1536]{1,0:T(8,128)(2,1)S(1)} %get-tuple-element.373), channel_id=1, source_target_pairs={{0,4},{4,0},{8,12},{12,8},{16,20},{20,16},{24,28},{28,24},{1,5},{5... | collective-permute-start | bytes 1179656 | tf_op jit(solution)/shard_map/ppermute | solution.py:405
  178.8 15.2 %collective-permute-start.29 = (bf16[256,1664]{1,0:T(8,128)(2,1)S(1)}, bf16[256,1664]{1,0:T(8,128)(2,1)S(1)}, u32[]{:S(2)}, u32[]{:S(2)}) collective-permute-start(bf16[256,1664]{1,0:T(8,128)(2,1)S(1)} %pad_maximum_fusion.11), channel_id=1, source_target_pairs={{0,2},{1,3},{2,0},{3,1},{4,6},{5,7},{6,4},{7,5},{8,10},{9,11},{10,... | collective-permute-start | bytes 2555912 | tf_op jit(solution)/shard_map/ppermute | solution.py:409
  195.4 93.1 %all-to-all-start.1 = ((bf16[8,192,1280]{2,1,0:T(8,128)(2,1)}), bf16[8,192,1280]{2,1,0:T(8,128)(2,1)}, u32[]{:S(2)}, u32[]{:S(2)}) async-start(bf16[8,192,1280]{2,1,0:T(8,128)(2,1)} %pack_weights.1), calls=%async_computation.1 | async-start | bytes 7864320 | tf_op jit(solution)/shard_map/all_to_all | solution.py:1012
  302.6 21.2 %collective-permute-start.36 = (bf16[128,1536]{1,0:T(8,128)(2,1)S(1)}, bf16[128,1536]{1,0:T(8,128)(2,1)S(1)}, u32[]{:S(2)}, u32[]{:S(2)}) collective-permute-start(bf16[128,1536]{1,0:T(8,128)(2,1)S(1)} %collective-permute-done.34), channel_id=1, source_target_pairs={{8,16},{12,20},{16,8},{20,12},{9,17},{13,21},{17,9},{21,13},{10,18... | collective-permute-start | bytes 1179656 | tf_op jit(solution)/shard_map/ppermute | solution.py:405
  304.0 19.8 %collective-permute-start.39 = (bf16[128,1536]{1,0:T(8,128)(2,1)S(1)}, bf16[128,1536]{1,0:T(8,128)(2,1)S(1)}, u32[]{:S(2)}, u32[]{:S(2)}) collective-permute-start(bf16[128,1536]{1,0:T(8,128)(2,1)S(1)} %pad_maximum_fusion.18), channel_id=1, source_target_pairs={{0,2},{1,3},{2,0},{3,1},{4,6},{5,7},{6,4},{7,5},{8,10},{9,11},{10,... | collective-permute-start | bytes 1179656 | tf_op jit(solution)/shard_map/ppermute | solution.py:409
  305.6 18.2 %collective-permute-start.38 = (bf16[128,1536]{1,0:T(8,128)(2,1)S(1)}, bf16[128,1536]{1,0:T(8,128)(2,1)S(1)}, u32[]{:S(2)}, u32[]{:S(2)}) collective-permute-start(bf16[128,1536]{1,0:T(8,128)(2,1)S(1)} %pad_maximum_fusion.17), channel_id=1, source_target_pairs={{0,4},{4,0},{8,12},{12,8},{16,20},{20,16},{24,28},{28,24},{1,5},{5... | collective-permute-start | bytes 1179656 | tf_op jit(solution)/shard_map/ppermute | solution.py:405
  307.1 16.7 %collective-permute-start.37 = (bf16[128,1536]{1,0:T(8,128)(2,1)S(1)}, bf16[128,1536]{1,0:T(8,128)(2,1)S(1)}, u32[]{:S(2)}, u32[]{:S(2)}) collective-permute-start(bf16[128,1536]{1,0:T(8,128)(2,1)S(1)} %collective-permute-done.35), channel_id=1, source_target_pairs={{8,0},{12,4},{16,24},{20,28},{9,1},{13,5},{17,25},{21,29},{10,2},{... | collective-permute-start | bytes 1179656 | tf_op jit(solution)/shard_map/ppermute | solution.py:405
  323.9 18.6 %collective-permute-start.42 = (bf16[256,1536]{1,0:T(8,128)(2,1)S(1)}, bf16[256,1536]{1,0:T(8,128)(2,1)S(1)}, u32[]{:S(2)}, u32[]{:S(2)}) collective-permute-start(bf16[256,1536]{1,0:T(8,128)(2,1)S(1)} %pad_maximum_fusion.13), channel_id=1, source_target_pairs={{0,4},{4,0},{8,12},{12,8},{16,20},{20,16},{24,28},{28,24},{1,5},{5... | collective-permute-start | bytes 2359304 | tf_op jit(solution)/shard_map/ppermute | solution.py:405
  324.5 18.3 %collective-permute-start.41 = (bf16[256,1536]{1,0:T(8,128)(2,1)S(1)}, bf16[256,1536]{1,0:T(8,128)(2,1)S(1)}, u32[]{:S(2)}, u32[]{:S(2)}) collective-permute-start(bf16[256,1536]{1,0:T(8,128)(2,1)S(1)} %pad_maximum_fusion.12), channel_id=1, source_target_pairs={{0,2},{1,3},{2,0},{3,1},{4,6},{5,7},{6,4},{7,5},{8,10},{9,11},{10,... | collective-permute-start | bytes 2359304 | tf_op jit(solution)/shard_map/ppermute | solution.py:409
  325.1 14.8 %collective-permute-start.40 = (bf16[128,1536]{1,0:T(8,128)(2,1)S(1)}, bf16[128,1536]{1,0:T(8,128)(2,1)S(1)}, u32[]{:S(2)}, u32[]{:S(2)}) collective-permute-start(bf16[128,1536]{1,0:T(8,128)(2,1)S(1)} %collective-permute-done.36), channel_id=1, source_target_pairs={{8,0},{12,4},{16,24},{20,28},{9,1},{13,5},{17,25},{21,29},{10,2},{... | collective-permute-start | bytes 1179656 | tf_op jit(solution)/shard_map/ppermute | solution.py:405
  360.9 19.9 %collective-permute-start.47 = (bf16[256,1536]{1,0:T(8,128)(2,1)S(1)}, bf16[256,1536]{1,0:T(8,128)(2,1)S(1)}, u32[]{:S(2)}, u32[]{:S(2)}) collective-permute-start(bf16[256,1536]{1,0:T(8,128)(2,1)S(1)} %pad_maximum_fusion.15), channel_id=1, source_target_pairs={{0,4},{4,0},{8,12},{12,8},{16,20},{20,16},{24,28},{28,24},{1,5},{5... | collective-permute-start | bytes 2359304 | tf_op jit(solution)/shard_map/ppermute | solution.py:405
  362.5 18.5 %collective-permute-start.46 = (bf16[256,1536]{1,0:T(8,128)(2,1)S(1)}, bf16[256,1536]{1,0:T(8,128)(2,1)S(1)}, u32[]{:S(2)}, u32[]{:S(2)}) collective-permute-start(bf16[256,1536]{1,0:T(8,128)(2,1)S(1)} %pad_maximum_fusion.14), channel_id=1, source_target_pairs={{0,2},{1,3},{2,0},{3,1},{4,6},{5,7},{6,4},{7,5},{8,10},{9,11},{10,... | collective-permute-start | bytes 2359304 | tf_op jit(solution)/shard_map/ppermute | solution.py:409
  386.0 23.2 %collective-permute-start.48 = (bf16[1024,1536]{1,0:T(8,128)(2,1)}, bf16[1024,1536]{1,0:T(8,128)(2,1)S(1)}, u32[]{:S(2)}, u32[]{:S(2)}) collective-permute-start(bf16[1024,1536]{1,0:T(8,128)(2,1)} %get-tuple-element.398), channel_id=1, source_target_pairs={{0,1},{1,0},{2,3},{3,2},{4,5},{5,4},{6,7},{7,6},{8,9},{9,8},{10,11... | collective-permute-start | bytes 9437192 | tf_op jit(solution)/shard_map/ppermute | solution.py:409
  445.9 18.9 %collective-permute-start.49 = (bf16[1024,1536]{1,0:T(8,128)(2,1)S(1)}, bf16[1024,1536]{1,0:T(8,128)(2,1)}, u32[]{:S(2)}, u32[]{:S(2)}) collective-permute-start(bf16[1024,1536]{1,0:T(8,128)(2,1)S(1)} %slice.465), channel_id=1, source_target_pairs={{0,1},{1,0},{2,3},{3,2},{4,5},{5,4},{6,7},{7,6},{8,9},{9,8},{10,11... | collective-permute-start | bytes 9437192 | tf_op jit(solution)/shard_map/ppermute | solution.py:409
  446.7 32.4 %collective-permute-start.52 = (bf16[1024,1536]{1,0:T(8,128)(2,1)S(1)}, bf16[1024,1536]{1,0:T(8,128)(2,1)S(1)}, u32[]{:S(2)}, u32[]{:S(2)}) collective-permute-start(bf16[1024,1536]{1,0:T(8,128)(2,1)S(1)} %slice.389), channel_id=1, source_target_pairs={{0,1},{1,0},{2,3},{3,2},{4,5},{5,4},{6,7},{7,6},{8,9},{9,8},{10,11... | collective-permute-start | bytes 9437192 | tf_op jit(solution)/shard_map/ppermute | solution.py:409
  469.9 20.1 %collective-permute-start.50 = (bf16[256,1536]{1,0:T(8,128)(2,1)S(1)}, bf16[256,1536]{1,0:T(8,128)(2,1)S(1)}, u32[]{:S(2)}, u32[]{:S(2)}) collective-permute-start(bf16[256,1536]{1,0:T(8,128)(2,1)S(1)} %get-tuple-element.372), channel_id=1, source_target_pairs={{0,2},{1,3},{2,0},{3,1},{4,6},{5,7},{6,4},{7,5},{8,10},{9,11},{10,... | collective-permute-start | bytes 2359304 | tf_op jit(solution)/shard_map/ppermute | solution.py:409
  471.5 19.9 %collective-permute-start.51 = (bf16[256,1536]{1,0:T(8,128)(2,1)S(1)}, bf16[256,1536]{1,0:T(8,128)(2,1)}, u32[]{:S(2)}, u32[]{:S(2)}) collective-permute-start(bf16[256,1536]{1,0:T(8,128)(2,1)S(1)} %get-tuple-element.371), channel_id=1, source_target_pairs={{0,4},{4,0},{8,12},{12,8},{16,20},{20,16},{24,28},{28,24},{1,5},{5... | collective-permute-start | bytes 2359304 | tf_op jit(solution)/shard_map/ppermute | solution.py:405
  495.2 28.6 %collective-permute-start.55 = (bf16[256,1536]{1,0:T(8,128)(2,1)}, bf16[256,1536]{1,0:T(8,128)(2,1)S(1)}, u32[]{:S(2)}, u32[]{:S(2)}) collective-permute-start(bf16[256,1536]{1,0:T(8,128)(2,1)} %get-tuple-element.368), channel_id=1, source_target_pairs={{0,2},{1,3},{2,0},{3,1},{4,6},{5,7},{6,4},{7,5},{8,10},{9,11},{10,... | collective-permute-start | bytes 2359304 | tf_op jit(solution)/shard_map/ppermute | solution.py:409
  496.3 27.6 %collective-permute-start.56 = (bf16[256,1536]{1,0:T(8,128)(2,1)S(1)}, bf16[256,1536]{1,0:T(8,128)(2,1)S(1)}, u32[]{:S(2)}, u32[]{:S(2)}) collective-permute-start(bf16[256,1536]{1,0:T(8,128)(2,1)S(1)} %get-tuple-element.367), channel_id=1, source_target_pairs={{0,4},{4,0},{8,12},{12,8},{16,20},{20,16},{24,28},{28,24},{1,5},{5... | collective-permute-start | bytes 2359304 | tf_op jit(solution)/shard_map/ppermute | solution.py:405
  498.4 25.4 %collective-permute-start.53 = (bf16[128,1536]{1,0:T(8,128)(2,1)S(1)}, bf16[128,1536]{1,0:T(8,128)(2,1)}, u32[]{:S(2)}, u32[]{:S(2)}) collective-permute-start(bf16[128,1536]{1,0:T(8,128)(2,1)S(1)} %slice.471), channel_id=1, source_target_pairs={{0,4},{4,0},{8,12},{12,8},{16,20},{20,16},{24,28},{28,24},{1,5},{5... | collective-permute-start | bytes 1179656 | tf_op jit(solution)/shard_map/ppermute | solution.py:405
  500.0 23.9 %collective-permute-start.54 = (bf16[128,1536]{1,0:T(8,128)(2,1)S(1)}, bf16[128,1536]{1,0:T(8,128)(2,1)S(1)}, u32[]{:S(2)}, u32[]{:S(2)}) collective-permute-start(bf16[128,1536]{1,0:T(8,128)(2,1)S(1)} %slice.473), channel_id=1, source_target_pairs={{0,2},{1,3},{2,0},{3,1},{4,6},{5,7},{6,4},{7,5},{8,10},{9,11},{10,... | collective-permute-start | bytes 1179656 | tf_op jit(solution)/shard_map/ppermute | solution.py:409
  516.9 41.3 %collective-permute-start.60 = (bf16[1024,1536]{1,0:T(8,128)(2,1)}, bf16[1024,1536]{1,0:T(8,128)(2,1)}, u32[]{:S(2)}, u32[]{:S(2)}) collective-permute-start(bf16[1024,1536]{1,0:T(8,128)(2,1)} %slice.404), channel_id=1, source_target_pairs={{0,1},{1,0},{2,3},{3,2},{4,5},{5,4},{6,7},{7,6},{8,9},{9,8},{10,11... | collective-permute-start | bytes 9437192 | tf_op jit(solution)/shard_map/ppermute | solution.py:409
  527.7 28.9 %collective-permute-start.59 = (bf16[128,1536]{1,0:T(8,128)(2,1)}, bf16[128,1536]{1,0:T(8,128)(2,1)}, u32[]{:S(2)}, u32[]{:S(2)}) collective-permute-start(bf16[128,1536]{1,0:T(8,128)(2,1)} %pad_maximum_fusion.21), channel_id=1, source_target_pairs={{0,8},{4,12},{24,16},{28,20},{1,9},{5,13},{25,17},{29,21},{2,10},{... | collective-permute-start | bytes 1179656 | tf_op jit(solution)/shard_map/ppermute | solution.py:405
  537.6 20.6 %collective-permute-start.57 = (bf16[128,1536]{1,0:T(8,128)(2,1)}, bf16[128,1536]{1,0:T(8,128)(2,1)}, u32[]{:S(2)}, u32[]{:S(2)}) collective-permute-start(bf16[128,1536]{1,0:T(8,128)(2,1)} %slice.480), channel_id=1, source_target_pairs={{0,4},{4,0},{8,12},{12,8},{16,20},{20,16},{24,28},{28,24},{1,5},{5... | collective-permute-start | bytes 1179656 | tf_op jit(solution)/shard_map/ppermute | solution.py:405
  539.0 19.2 %collective-permute-start.58 = (bf16[128,1536]{1,0:T(8,128)(2,1)}, bf16[128,1536]{1,0:T(8,128)(2,1)}, u32[]{:S(2)}, u32[]{:S(2)}) collective-permute-start(bf16[128,1536]{1,0:T(8,128)(2,1)} %slice.482), channel_id=1, source_target_pairs={{0,2},{1,3},{2,0},{3,1},{4,6},{5,7},{6,4},{7,5},{8,10},{9,11},{10,... | collective-permute-start | bytes 1179656 | tf_op jit(solution)/shard_map/ppermute | solution.py:409
  550.5 18.9 %collective-permute-start.65 = (bf16[1024,1536]{1,0:T(8,128)(2,1)}, bf16[1024,1536]{1,0:T(8,128)(2,1)}, u32[]{:S(2)}, u32[]{:S(2)}) collective-permute-start(bf16[1024,1536]{1,0:T(8,128)(2,1)} %slice.411), channel_id=1, source_target_pairs={{0,1},{1,0},{2,3},{3,2},{4,5},{5,4},{6,7},{7,6},{8,9},{9,8},{10,11... | collective-permute-start | bytes 9437192 | tf_op jit(solution)/shard_map/ppermute | solution.py:409
  562.4 20.0 %collective-permute-start.63 = (bf16[256,1536]{1,0:T(8,128)(2,1)S(1)}, bf16[256,1536]{1,0:T(8,128)(2,1)S(1)}, u32[]{:S(2)}, u32[]{:S(2)}) collective-permute-start(bf16[256,1536]{1,0:T(8,128)(2,1)S(1)} %get-tuple-element.364), channel_id=1, source_target_pairs={{0,2},{1,3},{2,0},{3,1},{4,6},{5,7},{6,4},{7,5},{8,10},{9,11},{10,... | collective-permute-start | bytes 2359304 | tf_op jit(solution)/shard_map/ppermute | solution.py:409
  563.9 19.7 %collective-permute-start.64 = (bf16[256,1536]{1,0:T(8,128)(2,1)S(1)}, bf16[256,1536]{1,0:T(8,128)(2,1)S(1)}, u32[]{:S(2)}, u32[]{:S(2)}) collective-permute-start(bf16[256,1536]{1,0:T(8,128)(2,1)S(1)} %get-tuple-element.363), channel_id=1, source_target_pairs={{0,4},{4,0},{8,12},{12,8},{16,20},{20,16},{24,28},{28,24},{1,5},{5... | collective-permute-start | bytes 2359304 | tf_op jit(solution)/shard_map/ppermute | solution.py:405
  586.4 37.1 %collective-permute-start.70 = (bf16[256,1536]{1,0:T(8,128)(2,1)S(1)}, bf16[256,1536]{1,0:T(8,128)(2,1)S(1)}, u32[]{:S(2)}, u32[]{:S(2)}) collective-permute-start(bf16[256,1536]{1,0:T(8,128)(2,1)S(1)} %get-tuple-element.360), channel_id=1, source_target_pairs={{0,2},{1,3},{2,0},{3,1},{4,6},{5,7},{6,4},{7,5},{8,10},{9,11},{10,... | collective-permute-start | bytes 2359304 | tf_op jit(solution)/shard_map/ppermute | solution.py:409
  587.1 36.4 %collective-permute-start.71 = (bf16[256,1536]{1,0:T(8,128)(2,1)S(1)}, bf16[256,1536]{1,0:T(8,128)(2,1)S(1)}, u32[]{:S(2)}, u32[]{:S(2)}) collective-permute-start(bf16[256,1536]{1,0:T(8,128)(2,1)S(1)} %get-tuple-element.359), channel_id=1, source_target_pairs={{0,4},{4,0},{8,12},{12,8},{16,20},{20,16},{24,28},{28,24},{1,5},{5... | collective-permute-start | bytes 2359304 | tf_op jit(solution)/shard_map/ppermute | solution.py:405
  588.9 25.1 %collective-permute-start.68 = (bf16[128,1536]{1,0:T(8,128)(2,1)S(1)}, bf16[128,1536]{1,0:T(8,128)(2,1)S(1)}, u32[]{:S(2)}, u32[]{:S(2)}) collective-permute-start(bf16[128,1536]{1,0:T(8,128)(2,1)S(1)} %slice.493), channel_id=1, source_target_pairs={{0,4},{4,0},{8,12},{12,8},{16,20},{20,16},{24,28},{28,24},{1,5},{5... | collective-permute-start | bytes 1179656 | tf_op jit(solution)/shard_map/ppermute | solution.py:405
  589.6 33.9 %collective-permute-start.69 = (bf16[128,1536]{1,0:T(8,128)(2,1)S(1)}, bf16[128,1536]{1,0:T(8,128)(2,1)S(1)}, u32[]{:S(2)}, u32[]{:S(2)}) collective-permute-start(bf16[128,1536]{1,0:T(8,128)(2,1)S(1)} %slice.495), channel_id=1, source_target_pairs={{0,2},{1,3},{2,0},{3,1},{4,6},{5,7},{6,4},{7,5},{8,10},{9,11},{10,... | collective-permute-start | bytes 1179656 | tf_op jit(solution)/shard_map/ppermute | solution.py:409
  591.2 32.3 %collective-permute-start.67 = (bf16[128,1536]{1,0:T(8,128)(2,1)S(1)}, bf16[128,1536]{1,0:T(8,128)(2,1)S(1)}, u32[]{:S(2)}, u32[]{:S(2)}) collective-permute-start(bf16[128,1536]{1,0:T(8,128)(2,1)S(1)} %add_convert_fusion.24), channel_id=1, source_target_pairs={{8,16},{12,20},{16,8},{20,12},{9,17},{13,21},{17,9},{21,13},{10,18... | collective-permute-start | bytes 1179656 | tf_op jit(solution)/shard_map/ppermute | solution.py:405
  626.3 18.4 %collective-permute-start.72 = (bf16[128,1536]{1,0:T(8,128)(2,1)S(1)}, bf16[128,1536]{1,0:T(8,128)(2,1)S(1)}, u32[]{:S(2)}, u32[]{:S(2)}) collective-permute-start(bf16[128,1536]{1,0:T(8,128)(2,1)S(1)} %get-tuple-element.339), channel_id=1, source_target_pairs={{0,8},{4,12},{8,0},{12,4},{16,24},{20,28},{24,16},{28,20},{1,9},{5... | collective-permute-start | bytes 1179656 | tf_op jit(solution)/shard_map/ppermute | solution.py:405
  628.4 14.9 %collective-permute-start.77 = (bf16[128,1536]{1,0:T(8,128)(2,1)S(1)}, bf16[128,1536]{1,0:T(8,128)(2,1)S(1)}, u32[]{:S(2)}, u32[]{:S(2)}) collective-permute-start(bf16[128,1536]{1,0:T(8,128)(2,1)S(1)} %pad_maximum_fusion.23), channel_id=1, source_target_pairs={{0,8},{4,12},{24,16},{28,20},{1,9},{5,13},{25,17},{29,21},{2,10},{... | collective-permute-start | bytes 1179656 | tf_op jit(solution)/shard_map/ppermute | solution.py:405
  651.8 14.9 %collective-permute-start.78 = (bf16[128,1536]{1,0:T(8,128)(2,1)S(1)}, bf16[128,1536]{1,0:T(8,128)(2,1)S(1)}, u32[]{:S(2)}, u32[]{:S(2)}) collective-permute-start(bf16[128,1536]{1,0:T(8,128)(2,1)S(1)} %collective-permute-done.72), channel_id=1, source_target_pairs={{8,16},{12,20},{16,8},{20,12},{9,17},{13,21},{17,9},{21,13},{10,18... | collective-permute-start | bytes 1179656 | tf_op jit(solution)/shard_map/ppermute | solution.py:405
  669.2 18.3 %collective-permute-start.85 = (bf16[128,1536]{1,0:T(8,128)(2,1)S(1)}, bf16[128,1536]{1,0:T(8,128)(2,1)S(1)}, u32[]{:S(2)}, u32[]{:S(2)}) collective-permute-start(bf16[128,1536]{1,0:T(8,128)(2,1)S(1)} %add_convert_fusion.18), channel_id=1, source_target_pairs={{0,8},{4,12},{8,0},{12,4},{16,24},{20,28},{24,16},{28,20},{1,9},{5... | collective-permute-start | bytes 1179656 | tf_op jit(solution)/shard_map/ppermute | solution.py:405
  702.1 91.7 %all-to-all-start.3 = ((bf16[8,192,1280]{2,1,0:T(8,128)(2,1)}), bf16[8,192,1280]{2,1,0:T(8,128)(2,1)}, u32[]{:S(2)}, u32[]{:S(2)}) async-start(bf16[8,192,1280]{2,1,0:T(8,128)(2,1)} %bitcast.145), calls=%async_computation.3 | async-start | bytes 7864320 | tf_op jit(solution)/shard_map/all_to_all | solution.py:1204
  735.1 19.2 %collective-permute-start.88 = (bf16[128,1536]{1,0:T(8,128)(2,1)}, bf16[128,1536]{1,0:T(8,128)(2,1)}, u32[]{:S(2)}, u32[]{:S(2)}) collective-permute-start(bf16[128,1536]{1,0:T(8,128)(2,1)} %get-tuple-element.356), channel_id=1, source_target_pairs={{0,4},{4,0},{8,12},{12,8},{16,20},{20,16},{24,28},{28,24},{1,5},{5... | collective-permute-start | bytes 1179656 | tf_op jit(solution)/shard_map/ppermute | solution.py:405
  754.4 19.6 %collective-permute-start.91 = (bf16[2,8,48,640]{3,2,1,0:T(8,128)(2,1)S(1)}, bf16[2,8,48,640]{3,2,1,0:T(8,128)(2,1)S(1)}, u32[]{:S(2)}, u32[]{:S(2)}) collective-permute-start(bf16[2,8,48,640]{3,2,1,0:T(8,128)(2,1)S(1)} %pad_maximum_fusion.7), channel_id=1, source_target_pairs={{0,1},{1,0},{2,3},{3,2},{4,5},{5,4},{6,7},{7,6},{8,9},{9,8},{10,11... | collective-permute-start | bytes 2949128 | tf_op jit(solution)/shard_map/ppermute | solution.py:409
  754.5 15.9 %collective-permute-start.90 = (bf16[128,1536]{1,0:T(8,128)(2,1)S(1)}, bf16[128,1536]{1,0:T(8,128)(2,1)S(1)}, u32[]{:S(2)}, u32[]{:S(2)}) collective-permute-start(bf16[128,1536]{1,0:T(8,128)(2,1)S(1)} %copy-done.30), channel_id=1, source_target_pairs={{0,4},{4,0},{8,12},{12,8},{16,20},{20,16},{24,28},{28,24},{1,5},{5... | collective-permute-start | bytes 1179656 | tf_op jit(solution)/shard_map/ppermute | solution.py:405
  755.8 18.2 %collective-permute-start.89 = (bf16[128,1536]{1,0:T(8,128)(2,1)S(1)}, bf16[128,1536]{1,0:T(8,128)(2,1)S(1)}, u32[]{:S(2)}, u32[]{:S(2)}) collective-permute-start(bf16[128,1536]{1,0:T(8,128)(2,1)S(1)} %add_convert_fusion.16), channel_id=1, source_target_pairs={{0,8},{4,12},{24,16},{28,20},{1,9},{5,13},{25,17},{29,21},{2,10},{... | collective-permute-start | bytes 1179656 | tf_op jit(solution)/shard_map/ppermute | solution.py:405
  757.7 28.5 %collective-permute-start.94 = (bf16[128,1536]{1,0:T(8,128)(2,1)S(1)}, bf16[128,1536]{1,0:T(8,128)(2,1)S(1)}, u32[]{:S(2)}, u32[]{:S(2)}) collective-permute-start(bf16[128,1536]{1,0:T(8,128)(2,1)S(1)} %copy-done.29), channel_id=1, source_target_pairs={{0,4},{4,0},{8,12},{12,8},{16,20},{20,16},{24,28},{28,24},{1,5},{5... | collective-permute-start | bytes 1179656 | tf_op jit(solution)/shard_map/ppermute | solution.py:405
  784.4 34.3 %collective-permute-start.98 = (bf16[128,1536]{1,0:T(8,128)(2,1)S(1)}, bf16[128,1536]{1,0:T(8,128)(2,1)S(1)}, u32[]{:S(2)}, u32[]{:S(2)}) collective-permute-start(bf16[128,1536]{1,0:T(8,128)(2,1)S(1)} %copy-done.28), channel_id=1, source_target_pairs={{0,4},{4,0},{8,12},{12,8},{16,20},{20,16},{24,28},{28,24},{1,5},{5... | collective-permute-start | bytes 1179656 | tf_op jit(solution)/shard_map/ppermute | solution.py:405
  787.8 31.0 %collective-permute-start.97 = (bf16[128,1536]{1,0:T(8,128)(2,1)}, bf16[128,1536]{1,0:T(8,128)(2,1)S(1)}, u32[]{:S(2)}, u32[]{:S(2)}) collective-permute-start(bf16[128,1536]{1,0:T(8,128)(2,1)} %add_convert_fusion.12), channel_id=1, source_target_pairs={{8,16},{12,20},{16,8},{20,12},{9,17},{13,21},{17,9},{21,13},{10,18... | collective-permute-start | bytes 1179656 | tf_op jit(solution)/shard_map/ppermute | solution.py:405
  793.8 31.0 %all-to-all-start.2 = ((bf16[8,48,640]{2,1,0:T(8,128)(2,1)}), bf16[8,48,640]{2,1,0:T(8,128)(2,1)S(1)}, u32[]{:S(2)}, u32[]{:S(2)}) async-start(bf16[8,48,640]{2,1,0:T(8,128)(2,1)} %fusion.8), calls=%async_computation.2 | async-start | bytes 983040 | tf_op jit(solution)/shard_map/all_to_all | solution.py:1260
  808.5 16.4 %collective-permute-start.96 = (bf16[128,1536]{1,0:T(8,128)(2,1)}, bf16[128,1536]{1,0:T(8,128)(2,1)S(1)}, u32[]{:S(2)}, u32[]{:S(2)}) collective-permute-start(bf16[128,1536]{1,0:T(8,128)(2,1)} %add_convert_fusion.13), channel_id=1, source_target_pairs={{0,8},{4,12},{8,0},{12,4},{16,24},{20,28},{24,16},{28,20},{1,9},{5... | collective-permute-start | bytes 1179656 | tf_op jit(solution)/shard_map/ppermute | solution.py:405
  (94 other events, 1339.5 us)

commit v3 on v2

--- a/solution.py
+++ b/solution.py
@@ -505,41 +505,6 @@
         return total
 
 
-def gather_beside_sum(piece, attention):
-    (near, middle, y0), attended = one_round(
-        (over_dp(piece, Z_NEAR), over_dp(piece, Z_MIDDLE), swap_y(piece)), (piece,), attention
-    )
-    part = attended[-1]
-    pair0 = joined(piece, y0)
-    total = DpScatter(part)
-    (far, out1, y1, x0, sums), _ = one_round(
-        (
-            over_dp(near, Z_MIDDLE),
-            over_dp(middle, Z_OUT),
-            swap_y(near),
-            swap_x(pair0),
-            total.step(),
-        ),
-        (near, middle, pair0),
-    )
-    total.keep(sums)
-    third = middle + out1
-    pair1 = joined(near, y1)
-    (out2, y2, x1, sums), _ = one_round(
-        (over_dp(far, Z_OUT), swap_y(third), swap_x(pair1), total.step()), (far, third, pair1)
-    )
-    total.keep(sums)
-    fourth = far + out2
-    pair2 = joined(third, y2)
-    (y3, x2, sums), _ = one_round((swap_y(fourth), swap_x(pair2), total.step()), (fourth, pair2))
-    total.keep(sums)
-    pair3 = joined(fourth, y3)
-    (x3, sums), _ = one_round((swap_x(pair3), total.step()), (pair3,))
-    total.keep(sums)
-    here = joined(pair0, x0, pair1, x1, pair2, x2, pair3, x3)
-    return joined(here, swap_core(here)), total.total(), attended
-
-
 def gather_pairs(piece, covers):
     works = []
 
@@ -1004,13 +969,43 @@
     ).transpose(1, 0, 2)
     attn_in = lax.all_to_all(attn_out, "dp", split_axis=0, concat_axis=0, tiled=True)
 
-    group_tokens, (_, in_out, _, _) = dp_gather(
-        tokens[0], (None, lambda tie, works: pack_in(tie), None, None)
-    )
+    every = jnp.arange(E, dtype=jnp.int32)[None, :]
+    dense = sum(
+        jnp.where(routes[0][:, k : k + 1] == every, gates[0][:, k : k + 1], 0.0)
+        for k in range(TOPK)
+    )
+    dense_top = rounded(dense)
+    dense_mid = rounded(dense - dense_top)
+    meta = jnp.concatenate(
+        [
+            dense_top,
+            dense_mid,
+            dense - dense_top - dense_mid,
+            jnp.zeros((tok_rows, 128 - 3 * E), jnp.float32),
+        ],
+        axis=1,
+    ).astype(jnp.bfloat16)
+
+    piece = tokens[0]
+    (near, middle, y0), _ = one_round(
+        (over_dp(piece, Z_NEAR), over_dp(piece, Z_MIDDLE), swap_y(piece)), (piece,)
+    )
+    (far, out1, y1), in_out = one_round(
+        (over_dp(near, Z_MIDDLE), over_dp(middle, Z_OUT), swap_y(near)), (near, middle), pack_in
+    )
+    third = middle + out1
+    (out2, y2), _ = one_round((over_dp(far, Z_OUT), swap_y(third)), (far, third))
+    fourth = far + out2
+    cot_piece = after(jnp.concatenate([cotangent[0], meta], axis=1), third)
+    (y3, cot_near, cot_middle), _ = one_round(
+        (swap_y(fourth), over_dp(cot_piece, Z_NEAR), over_dp(cot_piece, Z_MIDDLE)),
+        (fourth, cot_piece),
+    )
+    group_tokens = joined(piece, y0, near, y1, third, y2, fourth, y3)
     attn_two = jnp.stack([attn_in, swap_core(attn_in)])
     attn_four = joined(attn_two, swap_x(attn_two))
     in_w = lax.all_to_all(
-        after(in_out, group_tokens, attn_in), "dp", split_axis=0, concat_axis=0, tiled=True
+        after(in_out, cot_near, attn_in), "dp", split_axis=0, concat_axis=0, tiled=True
     ).reshape(model, 2 * ff_cols)
     z_own, y_own = lax.axis_index("dp") // 2, lax.axis_index("dp") % 2
     slot_dp = 2 * jnp.asarray(SLOT_Z, jnp.int32)[:, z_own]
@@ -1036,23 +1031,6 @@
 
     down_w = down_weight.astype(jnp.bfloat16).transpose(1, 0, 2).reshape(ff_cols, model)
 
-    every = jnp.arange(E, dtype=jnp.int32)[None, :]
-    dense = sum(
-        jnp.where(routes[0][:, k : k + 1] == every, gates[0][:, k : k + 1], 0.0)
-        for k in range(TOPK)
-    )
-    dense_top = rounded(dense)
-    dense_mid = rounded(dense - dense_top)
-    meta = jnp.concatenate(
-        [
-            dense_top,
-            dense_mid,
-            dense - dense_top - dense_mid,
-            jnp.zeros((tok_rows, 128 - 3 * E), jnp.float32),
-        ],
-        axis=1,
-    ).astype(jnp.bfloat16)
-
     seq_ids, cosine, sine_table = rope_parts(seq_lengths, places)
     cosine, sine_table = cosine[:, 0], sine_table[:, 0]
     row_ids = jnp.stack([seq_ids, places], axis=1)
@@ -1063,8 +1041,29 @@
             tie(group_tokens), gain_one[None], qkv_w, o_w, cosine, sine_table, row_ids, col_ids
         )
 
-    cot_out = after(jnp.concatenate([cotangent[0], meta], axis=1), group_tokens)
-    cot_all, branch, attended = gather_beside_sum(cot_out, attention)
+    (cot_far, out1, y0), _ = one_round(
+        (over_dp(cot_near, Z_MIDDLE), over_dp(cot_middle, Z_OUT), swap_y(cot_piece)),
+        (cot_near, cot_middle),
+    )
+    third = cot_middle + out1
+    pair0 = joined(cot_piece, y0)
+    outs = over_dp(cot_far, Z_OUT), swap_y(cot_near), swap_x(pair0)
+    (out2, y1, x0), attended = one_round(outs, (cot_far, pair0), attention)
+    fourth = cot_far + out2
+    pair1 = joined(cot_near, y1)
+    total = DpScatter(attended[-1])
+    (y2, x1, sums), _ = one_round((swap_y(third), swap_x(pair1), total.step()), (third, pair1))
+    total.keep(sums)
+    pair2 = joined(third, y2)
+    (y3, x2, sums), _ = one_round((swap_y(fourth), swap_x(pair2), total.step()), (fourth, pair2))
+    total.keep(sums)
+    pair3 = joined(fourth, y3)
+    (x3, sums), _ = one_round((swap_x(pair3), total.step()), (pair3,))
+    total.keep(sums)
+    cot_here = joined(pair0, x0, pair1, x1, pair2, x2, pair3, x3)
+    (sums, cot_there), _ = one_round((total.step(), swap_core(cot_here)), (cot_here,))
+    total.keep(sums)
+    cot_all, branch = joined(cot_here, cot_there), total.total()
     normed, queries, keys, vals, mixed_low, run_top, run_total, _ = attended
     rows_from, meta_from = far_order(ex_index, dealt_of)
     inputs = tokens[0].astype(jnp.float32)

time: 845 us -> 849 us (level)
  starting transfers between devices: 161 us -> 182 us
  waiting for transfers between devices: 269 us -> 251 us
    all_to_all x1, waiting for transfers between devices: 72.5 us -> 7.34 us  [per_device(): lax.all_to_all(after(in_out, cot_near, attn_in), 'dp', split_axis=0, conc...]
    ppermute x72, waiting for transfers between devices: 147 us -> 182 us  [over_dp(): return lax.ppermute(piece, 'dp', moves)]
    ppermute x72, starting transfers between devices: 111 us -> 138 us  [over_dp(): return lax.ppermute(piece, 'dp', moves)]
    ppermute x27, waiting for transfers between devices: 45.4 us -> 56.4 us  [over_expert(): return lax.ppermute(piece, 'expert', moves)]
    unnamed x145 -> x176, local copies, waits for them, and re-layouts: 37.1 us -> 43 us
where the time goes in v3:
time: 849 us; the launch traced here: 842 us
  waiting for transfers between devices  251 us (30%)
  starting transfers between devices  182 us (21%)
  matrix products  130 us (15%)
  other arithmetic  111 us (13%)
  local copies, waits for them, and re-layouts  95.6 us (11%)
  Pallas kernels  69.5 us (8%)
    ppermute x72, waiting for transfers between devices, over_dp(): return lax.ppermute(piece, 'dp', moves)  182 us
    ppermute x72, starting transfers between devices, over_dp(): return lax.ppermute(piece, 'dp', moves)  138 us
    ppermute x27, waiting for transfers between devices, over_expert(): return lax.ppermute(piece, 'expert', moves)  56.4 us
    unnamed x176, local copies, waits for them, and re-layouts  43 us
    convert_element_type x34, other arithmetic, added(): return total.astype(jnp.bfloat16)  33 us
    dot_general x2, matrix products, up(): return jnp.dot(sent, in_w, preferred_element_type=jnp.float32)  28 us
    pallas_call x1, Pallas kernels, rear(): pl.pallas_call(functools.partial(rear_kernel, heads=heads, rows=min(256,...  24.4 us
    dot_general x2, matrix products, back(): lax.dot_general(grads_here, in_w, COLS_DIMS, preferred_element_type=jnp.f...  24.2 us
  transfers between devices with their start and end apart: 103, of which 38 were waited for; matrix products, arithmetic and copies ran while one was open for 31% of the time, Pallas kernels for 8%

profile of v3, /device:TPU:0, one launch (start us, length us, event | category | flops | bytes accessed | tf_op | source)
XLA Modules:
  0.0 842.0 jit_solution(12165263249516489550)
XLA Ops:
  0.7 3.1 collective-permute-start
  14.9 5.0 all-to-all-start
  25.8 6.1 pack_weights.1
  51.0 5.1 collective-permute-start.9
  65.2 6.2 collective-permute-done.8
  80.4 5.4 collective-permute-done.12
  103.7 2.9 fusion.15
  106.6 20.2 %front.1 = (bf16[1024,1536]{1,0:T(8,128)(2,1)}, bf16[1024,192]{1,0:T(8,128)(2,1)}, bf16[1024,64]{1,0:T(8,128)(2,1)}, bf16[1024,64]{1,0:T(8,128)(2,1)}, bf16[1024...) custom-call(bf16[1024,1536]{1,0:T(8,128)(2,1)} %copy-done.3, ...), custom_call_target="tpu_custom_call" | custom-call | tf_op jit(solution)/shard_map/front/pallas_call | solution.py:738
  142.8 4.0 collective-permute-done.21
  148.7 5.0 collective-permute-start.24
  160.4 5.5 collective-permute-done.23
  166.0 4.8 collective-permute-start.28
  176.1 11.3 %collective-permute-done.26 = bf16[256,1664]{1,0:T(8,128)(2,1)S(1)} collective-permute-done((bf16[256,1664]{1,0:T(8,128)(2,1)S(1)}, bf16[256,1664]{1,0:T(8,128)(2,1)S(1)}, u32[]{:S(2)}, u32[]{:S(2)}) %collective-permute-start.26) | collective-permute-done | bytes 852000 | tf_op jit(solution)/shard_map/ppermute | solution.py:409
  188.8 4.6 all-to-all-start.1
  193.3 3.7 convert_element_type.565
  203.3 4.2 collective-permute-start.30
  210.6 25.0 %collective-permute-done.32 = bf16[128,1536]{1,0:T(8,128)(2,1)S(1)} collective-permute-done((bf16[128,1536]{1,0:T(8,128)(2,1)}, bf16[128,1536]{1,0:T(8,128)(2,1)S(1)}, u32[]{:S(2)}, u32[]{:S(2)}) %collective-permute-start.32) | collective-permute-done | bytes 393248 | tf_op jit(solution)/shard_map/ppermute | solution.py:405
  235.6 31.6 %collective-permute-done.30 = bf16[128,1536]{1,0:T(8,128)(2,1)S(1)} collective-permute-done((bf16[128,1536]{1,0:T(8,128)(2,1)S(1)}, bf16[128,1536]{1,0:T(8,128)(2,1)S(1)}, u32[]{:S(2)}, u32[]{:S(2)}) %collective-permute-start.30) | collective-permute-done | bytes 393248 | tf_op jit(solution)/shard_map/ppermute | solution.py:405
  268.7 6.3 constant_dynamic-update-slice_fusion.22.refs_0_.refs_1_.refs_2_.refs_3_.refs_4_.refs_5_.refs_6_.refs_7_.refs_8_.refs_9_.refs_10_.refs_11_.refs_12_.refs_13_.refs_14_.refs_15_
  275.0 7.3 all-to-all-done.1
  282.4 16.2 %collective-permute-start.34 = (bf16[128,1536]{1,0:T(8,128)(2,1)S(1)}, bf16[128,1536]{1,0:T(8,128)(2,1)S(1)}, u32[]{:S(2)}, u32[]{:S(2)}) collective-permute-start(bf16[128,1536]{1,0:T(8,128)(2,1)S(1)} %multiply_convert_fusion.9), channel_id=1, source_target_pairs={{0,8},{4,12},{8,0},{12,4},{16,24},{20,28},{24,16},{28,20},{1,9},{5... | collective-permute-start | bytes 1179656 | tf_op jit(solution)/shard_map/ppermute | solution.py:405
  299.4 12.7 %take_blocks.1 = (bf16[4096,1536]{1,0:T(8,128)(2,1)}, bf16[4096,128]{1,0:T(8,128)(2,1)}) custom-call(s32[2,64]{1,0:T(2,128)} %pad_add_fusion.2.index_ref, bf16[4096,1664]{1,0:T(8,128)(2,1)} %constant_dynamic-update-slice_fusion.22.refs_0_.refs_1_.refs_2_.refs_3_.refs_4_.refs_5_.refs_6_.refs_7_.refs_8_.refs_9_.refs_10_.refs_11_.refs_12_.refs_13_.refs_14_.refs_15_, ...), custom_call_target="tpu_custom_call" | custom-call | tf_op jit(solution)/shard_map/take_blocks/pallas_call | solution.py:647
  317.7 15.3 %fusion.79 = f32[4096,640]{1,0:T(8,128)} fusion(bf16[4096,1536]{1,0:T(8,128)(2,1)} %get-tuple-element.223, bf16[640,1536]{1,0:T(8,128)(2,1)S(1)} %bitcast.161), kind=kOutput, calls=%fused_computation.407 | convolution fusion | flops 8053063680 | bytes 25034752 | tf_op jit(solution)/shard_map/dot_general | solution.py:1085
  339.0 9.3 %collective-permute-done.40 = bf16[128,1536]{1,0:T(8,128)(2,1)S(1)} collective-permute-done((bf16[128,1536]{1,0:T(8,128)(2,1)S(1)}, bf16[128,1536]{1,0:T(8,128)(2,1)S(1)}, u32[]{:S(2)}, u32[]{:S(2)}) %collective-permute-start.40) | collective-permute-done | bytes 393248 | tf_op jit(solution)/shard_map/ppermute | solution.py:405
  348.4 3.1 collective-permute-done.42
  361.0 8.5 %collective-permute-done.44 = bf16[128,1536]{1,0:T(8,128)(2,1)S(1)} collective-permute-done((bf16[128,1536]{1,0:T(8,128)(2,1)S(1)}, bf16[128,1536]{1,0:T(8,128)(2,1)S(1)}, u32[]{:S(2)}, u32[]{:S(2)}) %collective-permute-start.44) | collective-permute-done | bytes 393248 | tf_op jit(solution)/shard_map/ppermute | solution.py:409
  374.8 14.2 %fusion.80 = f32[2048,1280]{1,0:T(8,128)} fusion(bf16[2048,1536]{1,0:T(8,128)(2,1)} %constant_dynamic-update-slice_fusion.43, bf16[1536,1280]{1,0:T(8,128)(2,1)} %bitcast.40), kind=kOutput, calls=%fused_computation.408 | convolution fusion | flops 8053063680 | bytes 20709376 | tf_op jit(solution)/shard_map/dot_general | solution.py:1096
  395.9 8.4 multiply_convert_fusion.5
  407.0 12.2 %convolution_convert_fusion.3 = bf16[2048,1536]{1,0:T(8,128)(2,1)} fusion(bf16[1536,1280]{1,0:T(8,128)(2,1)} %bitcast.40, bf16[2048,640]{1,0:T(8,128)(2,1)S(1)} %get-tuple-element.354, bf16[2048,640]{1,0:T(8,128)(2,1)S(1)} %get-tuple-element.353), kind=kOutput, calls=%fused_computation.3 | convolution fusion | flops 8066695168 | bytes 15466496 | tf_op jit(solution)/shard_map/dot_general | solution.py:1112
  421.1 13.8 %fusion.81 = f32[2048,1280]{1,0:T(8,128)} fusion(bf16[2048,1536]{1,0:T(8,128)(2,1)} %constant_dynamic-update-slice_fusion.60, bf16[1536,1280]{1,0:T(8,128)(2,1)} %bitcast.40), kind=kOutput, calls=%fused_computation.409 | convolution fusion | flops 8053063680 | bytes 20709376 | tf_op jit(solution)/shard_map/dot_general | solution.py:1096
  434.9 8.5 %multiply_convert_fusion.3 = (bf16[2048,640]{1,0:T(8,128)(2,1)S(1)}, bf16[2048,640]{1,0:T(8,128)(2,1)S(1)}, bf16[2048,640]{1,0:T(8,128)(2,1)}) fusion(f32[2048,1280]{1,0:T(8,128)} %fusion.81, f32[4096,640]{1,0:T(8,128)} %fusion.79, f32[4096,640]{1,0:T(8,128)S(1)} %fusion.17), kind=kLoop, calls=%fused_computation.17 | loop fusion | flops 26214400 | bytes 28835840 | tf_op jit(solution)/shard_map/convert.14
  443.5 11.9 %convolution_convert_fusion.2 = bf16[2048,1536]{1,0:T(8,128)(2,1)S(1)} fusion(bf16[1536,1280]{1,0:T(8,128)(2,1)} %bitcast.40, bf16[2048,640]{1,0:T(8,128)(2,1)S(1)} %get-tuple-element.352, bf16[2048,640]{1,0:T(8,128)(2,1)S(1)} %get-tuple-element.351), kind=kOutput, calls=%fused_computation.2 | convolution fusion | flops 8066695168 | bytes 15466496 | tf_op jit(solution)/shard_map/dot_general | solution.py:1112
  456.5 12.5 %fusion.82 = f32[1536,1280]{1,0:T(8,128)S(1)} fusion(bf16[2048,1536]{1,0:T(8,128)(2,1)} %constant_dynamic-update-slice_fusion.43, bf16[2048,1280]{1,0:T(8,128)(2,1)} %pad_maximum_fusion), kind=kOutput, calls=%fused_computation.410 | convolution fusion | flops 8053063680 | bytes 19398656 | tf_op jit(solution)/shard_map/dot_general | solution.py:1145
  469.1 5.4 convolution_convert_fusion.1
  474.5 5.0 add_convert_fusion.3
  480.8 7.0 convolution_convert_fusion
  487.9 11.9 %collective-permute-done.50 = bf16[256,1536]{1,0:T(8,128)(2,1)S(1)} collective-permute-done((bf16[256,1536]{1,0:T(8,128)(2,1)S(1)}, bf16[256,1536]{1,0:T(8,128)(2,1)S(1)}, u32[]{:S(2)}, u32[]{:S(2)}) %collective-permute-start.50) | collective-permute-done | bytes 786464 | tf_op jit(solution)/shard_map/ppermute | solution.py:409
  510.3 14.0 %fusion.6 = f32[1536,1280]{1,0:T(8,128)} fusion(bf16[2048,1536]{1,0:T(8,128)(2,1)} %constant_dynamic-update-slice_fusion.60, bf16[2048,640]{1,0:T(8,128)(2,1)} %copy-done.15, bf16[2048,640]{1,0:T(8,128)(2,1)} %copy-done.14), kind=kOutput, calls=%fused_computation.28 | convolution fusion | flops 8063549440 | bytes 19398656 | tf_op jit(solution)/shard_map/dot_general | solution.py:1153
  526.2 6.4 collective-permute-done.53
  536.6 7.4 collective-permute-start.59
  548.0 9.1 %fusion.2 = f32[640,1536]{1,0:T(8,128)} fusion(bf16[2048,640]{1,0:T(8,128)(2,1)S(1)} %copy-done.13, bf16[4096,1536]{1,0:T(8,128)(2,1)} %get-tuple-element.223), kind=kOutput, calls=%fused_computation.8 | convolution fusion | flops 4026531840 | bytes 12845056 | tf_op jit(solution)/shard_map/dot_general | solution.py:1160
  558.9 6.0 add.878
  566.6 4.0 add_convert_fusion.1
  576.9 13.8 %collective-permute-done.63 = bf16[256,1536]{1,0:T(8,128)(2,1)S(1)} collective-permute-done((bf16[256,1536]{1,0:T(8,128)(2,1)S(1)}, bf16[256,1536]{1,0:T(8,128)(2,1)S(1)}, u32[]{:S(2)}, u32[]{:S(2)}) %collective-permute-start.63) | collective-permute-done | bytes 786464 | tf_op jit(solution)/shard_map/ppermute | solution.py:409
  599.7 22.7 %collective-permute-done.68 = bf16[128,1536]{1,0:T(8,128)(2,1)S(1)} collective-permute-done((bf16[128,1536]{1,0:T(8,128)(2,1)S(1)}, bf16[128,1536]{1,0:T(8,128)(2,1)S(1)}, u32[]{:S(2)}, u32[]{:S(2)}) %collective-permute-start.68) | collective-permute-done | bytes 393248 | tf_op jit(solution)/shard_map/ppermute | solution.py:405
  622.4 6.5 fusion
  641.8 9.7 %collective-permute-done.77 = bf16[128,1536]{1,0:T(8,128)(2,1)S(1)} collective-permute-done((bf16[128,1536]{1,0:T(8,128)(2,1)S(1)}, bf16[128,1536]{1,0:T(8,128)(2,1)S(1)}, u32[]{:S(2)}, u32[]{:S(2)}) %collective-permute-start.77) | collective-permute-done | bytes 393248 | tf_op jit(solution)/shard_map/ppermute | solution.py:405
  653.0 7.0 collective-permute-done.74
  663.5 6.2 collective-permute-start.82
  677.4 8.3 collective-permute-start.85
  687.6 8.0 collective-permute-done.85
  695.7 4.5 collective-permute-done.83
  702.4 7.2 collective-permute-done.87
  710.3 4.7 all-to-all-start.3
  716.5 24.4 %rear.1 = (bf16[1024,320]{1,0:T(8,128)(2,1)}, bf16[1024,1536]{1,0:T(8,128)(2,1)}, f32[1,1536]{1,0:T(1,128)}) custom-call(bf16[1024,1536]{1,0:T(8,128)(2,1)} %constant_dynamic-update-slice_fusion.69.g_ref, bf16[1536,192]{1,0:T(8,128)(2,1)} %slice.456.ow_ref, bf16[1024,192]{1,0:T(8,128)(2,1)} %get-tuple-element.296.q_ref, ...), custom_call_target="tpu_custom_call" | custom-call | tf_op jit(solution)/shard_map/rear/pallas_call | solution.py:826
  745.4 3.3 convolution_convert_fusion.4
  755.4 4.4 concatenate.177
  767.5 11.2 %collective-permute-done.90 = bf16[128,1536]{1,0:T(8,128)(2,1)S(1)} collective-permute-done((bf16[128,1536]{1,0:T(8,128)(2,1)S(1)}, bf16[128,1536]{1,0:T(8,128)(2,1)S(1)}, u32[]{:S(2)}, u32[]{:S(2)}) %collective-permute-start.90) | collective-permute-done | bytes 393248 | tf_op jit(solution)/shard_map/ppermute | solution.py:405
  778.7 3.5 collective-permute-done.89
  784.1 4.4 collective-permute-start.93
  796.8 5.6 all-to-all-done.3.x_ref
  802.4 12.2 %all-to-all-start.2 = ((bf16[8,48,640]{2,1,0:T(8,128)(2,1)}), bf16[8,48,640]{2,1,0:T(8,128)(2,1)S(1)}, u32[]{:S(2)}, u32[]{:S(2)}) async-start(bf16[8,48,640]{2,1,0:T(8,128)(2,1)} %fusion.8), calls=%async_computation.2 | async-start | bytes 983040 | tf_op jit(solution)/shard_map/all_to_all | solution.py:1259
  821.0 6.1 unpack_grads.1
  827.1 6.0 collective-permute-done.96
  (529 shorter events, 268.5 us)
Async XLA Ops:
  0.7 20.4 %collective-permute-start = (bf16[128,1536]{1,0:T(8,128)(2,1)}, bf16[128,1536]{1,0:T(8,128)(2,1)}, u32[]{:S(2)}, u32[]{:S(2)}) collective-permute-start(bf16[128,1536]{1,0:T(8,128)(2,1)} %bitcast.155), channel_id=1, source_target_pairs={{0,8},{4,12},{8,0},{12,4},{16,24},{20,28},{24,16},{28,20},{1,9},{5... | collective-permute-start | bytes 1179656 | tf_op jit(solution)/shard_map/ppermute | solution.py:405
  3.8 17.3 %collective-permute-start.1 = (bf16[128,1536]{1,0:T(8,128)(2,1)}, bf16[128,1536]{1,0:T(8,128)(2,1)}, u32[]{:S(2)}, u32[]{:S(2)}) collective-permute-start(bf16[128,1536]{1,0:T(8,128)(2,1)} %bitcast.156), channel_id=1, source_target_pairs={{8,16},{12,20},{16,8},{20,12},{9,17},{13,21},{17,9},{21,13},{10,18... | collective-permute-start | bytes 1179656 | tf_op jit(solution)/shard_map/ppermute | solution.py:405
  5.2 15.9 %collective-permute-start.2 = (bf16[128,1536]{1,0:T(8,128)(2,1)}, bf16[128,1536]{1,0:T(8,128)(2,1)}, u32[]{:S(2)}, u32[]{:S(2)}) collective-permute-start(bf16[128,1536]{1,0:T(8,128)(2,1)} %bitcast.157), channel_id=1, source_target_pairs={{0,4},{4,0},{8,12},{12,8},{16,20},{20,16},{24,28},{28,24},{1,5},{5... | collective-permute-start | bytes 1179656 | tf_op jit(solution)/shard_map/ppermute | solution.py:405
  14.9 41.2 %all-to-all-start = ((bf16[8,48,640]{2,1,0:T(8,128)(2,1)}), bf16[8,48,640]{2,1,0:T(8,128)(2,1)}, u32[]{:S(2)}, u32[]{:S(2)}) async-start(bf16[8,48,640]{2,1,0:T(8,128)(2,1)} %bitcast.23), calls=%async_computation | async-start | bytes 983040 | tf_op jit(solution)/shard_map/all_to_all | solution.py:970
  49.5 15.2 %collective-permute-start.10 = (bf16[128,1664]{1,0:T(8,128)(2,1)}, bf16[128,1664]{1,0:T(8,128)(2,1)}, u32[]{:S(2)}, u32[]{:S(2)}) collective-permute-start(bf16[128,1664]{1,0:T(8,128)(2,1)} %concatenate.138), channel_id=1, source_target_pairs={{8,16},{12,20},{16,8},{20,12},{9,17},{13,21},{17,9},{21,13},{10,18... | collective-permute-start | bytes 1277960 | tf_op jit(solution)/shard_map/ppermute | solution.py:405
  62.7 30.7 %collective-permute-start.18 = (bf16[2,8,48,640]{3,2,0,1:T(8,128)(2,1)S(1)}, bf16[2,8,48,640]{3,2,0,1:T(8,128)(2,1)S(1)}, u32[]{:S(2)}, u32[]{:S(2)}) collective-permute-start(bf16[2,8,48,640]{3,2,0,1:T(8,128)(2,1)S(1)} %pad_maximum_fusion.6), channel_id=1, source_target_pairs={{0,2},{1,3},{2,0},{3,1},{4,6},{5,7},{6,4},{7,5},{8,10},{9,11},{10,... | collective-permute-start | bytes 2949128 | tf_op jit(solution)/shard_map/ppermute | solution.py:409
  64.3 16.1 %collective-permute-start.13 = (bf16[128,1664]{1,0:T(8,128)(2,1)}, bf16[128,1664]{1,0:T(8,128)(2,1)S(1)}, u32[]{:S(2)}, u32[]{:S(2)}) collective-permute-start(bf16[128,1664]{1,0:T(8,128)(2,1)} %concatenate.138), channel_id=1, source_target_pairs={{0,4},{4,0},{8,12},{12,8},{16,20},{20,16},{24,28},{28,24},{1,5},{5... | collective-permute-start | bytes 1277960 | tf_op jit(solution)/shard_map/ppermute | solution.py:405
  76.3 50.5 %collective-permute-start.15 = (bf16[128,1664]{1,0:T(8,128)(2,1)}, bf16[128,1664]{1,0:T(8,128)(2,1)}, u32[]{:S(2)}, u32[]{:S(2)}) collective-permute-start(bf16[128,1664]{1,0:T(8,128)(2,1)} %collective-permute-done.9), channel_id=1, source_target_pairs={{0,4},{4,0},{8,12},{12,8},{16,20},{20,16},{24,28},{28,24},{1,5},{5... | collective-permute-start | bytes 1277960 | tf_op jit(solution)/shard_map/ppermute | solution.py:405
  87.0 39.9 %collective-permute-start.16 = (bf16[256,1664]{1,0:T(8,128)(2,1)}, bf16[256,1664]{1,0:T(8,128)(2,1)}, u32[]{:S(2)}, u32[]{:S(2)}) collective-permute-start(bf16[256,1664]{1,0:T(8,128)(2,1)} %get-tuple-element.426), channel_id=1, source_target_pairs={{0,2},{1,3},{2,0},{3,1},{4,6},{5,7},{6,4},{7,5},{8,10},{9,11},{10,... | collective-permute-start | bytes 2555912 | tf_op jit(solution)/shard_map/ppermute | solution.py:409
  88.5 38.4 %collective-permute-start.14 = (bf16[128,1664]{1,0:T(8,128)(2,1)}, bf16[128,1664]{1,0:T(8,128)(2,1)}, u32[]{:S(2)}, u32[]{:S(2)}) collective-permute-start(bf16[128,1664]{1,0:T(8,128)(2,1)} %collective-permute-done.11), channel_id=1, source_target_pairs={{8,0},{12,4},{16,24},{20,28},{9,1},{13,5},{17,25},{21,29},{10,2},{... | collective-permute-start | bytes 1277960 | tf_op jit(solution)/shard_map/ppermute | solution.py:405
  91.8 49.4 %collective-permute-start.20 = (bf16[128,1664]{1,0:T(8,128)(2,1)}, bf16[128,1664]{1,0:T(8,128)(2,1)}, u32[]{:S(2)}, u32[]{:S(2)}) collective-permute-start(bf16[128,1664]{1,0:T(8,128)(2,1)} %add.825), channel_id=1, source_target_pairs={{0,4},{4,0},{8,12},{12,8},{16,20},{20,16},{24,28},{28,24},{1,5},{5... | collective-permute-start | bytes 1277960 | tf_op jit(solution)/shard_map/ppermute | solution.py:405
  128.0 18.8 %collective-permute-start.21 = (bf16[256,1664]{1,0:T(8,128)(2,1)S(1)}, bf16[256,1664]{1,0:T(8,128)(2,1)S(1)}, u32[]{:S(2)}, u32[]{:S(2)}) collective-permute-start(bf16[256,1664]{1,0:T(8,128)(2,1)S(1)} %pad_maximum_fusion.8), channel_id=1, source_target_pairs={{0,2},{1,3},{2,0},{3,1},{4,6},{5,7},{6,4},{7,5},{8,10},{9,11},{10,... | collective-permute-start | bytes 2555912 | tf_op jit(solution)/shard_map/ppermute | solution.py:409
  131.3 27.7 %collective-permute-start.25 = (bf16[128,1536]{1,0:T(8,128)(2,1)S(1)}, bf16[128,1536]{1,0:T(8,128)(2,1)S(1)}, u32[]{:S(2)}, u32[]{:S(2)}) collective-permute-start(bf16[128,1536]{1,0:T(8,128)(2,1)S(1)} %get-tuple-element.379), channel_id=1, source_target_pairs={{0,4},{4,0},{8,12},{12,8},{16,20},{20,16},{24,28},{28,24},{1,5},{5... | collective-permute-start | bytes 1179656 | tf_op jit(solution)/shard_map/ppermute | solution.py:405
  134.1 26.3 %collective-permute-start.19 = (bf16[128,1664]{1,0:T(8,128)(2,1)S(1)}, bf16[128,1664]{1,0:T(8,128)(2,1)S(1)}, u32[]{:S(2)}, u32[]{:S(2)}) collective-permute-start(bf16[128,1664]{1,0:T(8,128)(2,1)S(1)} %add.824), channel_id=1, source_target_pairs={{0,4},{4,0},{8,12},{12,8},{16,20},{20,16},{24,28},{28,24},{1,5},{5... | collective-permute-start | bytes 1277960 | tf_op jit(solution)/shard_map/ppermute | solution.py:405
  141.2 34.2 %collective-permute-start.29 = (bf16[128,1536]{1,0:T(8,128)(2,1)S(1)}, bf16[128,1536]{1,0:T(8,128)(2,1)S(1)}, u32[]{:S(2)}, u32[]{:S(2)}) collective-permute-start(bf16[128,1536]{1,0:T(8,128)(2,1)S(1)} %get-tuple-element.378), channel_id=1, source_target_pairs={{0,4},{4,0},{8,12},{12,8},{16,20},{20,16},{24,28},{28,24},{1,5},{5... | collective-permute-start | bytes 1179656 | tf_op jit(solution)/shard_map/ppermute | solution.py:405
  148.0 17.9 %collective-permute-start.23 = (bf16[256,1664]{1,0:T(8,128)(2,1)S(1)}, bf16[256,1664]{1,0:T(8,128)(2,1)S(1)}, u32[]{:S(2)}, u32[]{:S(2)}) collective-permute-start(bf16[256,1664]{1,0:T(8,128)(2,1)S(1)} %pad_maximum_fusion.9), channel_id=1, source_target_pairs={{0,2},{1,3},{2,0},{3,1},{4,6},{5,7},{6,4},{7,5},{8,10},{9,11},{10,... | collective-permute-start | bytes 2555912 | tf_op jit(solution)/shard_map/ppermute | solution.py:409
  170.9 16.5 %collective-permute-start.26 = (bf16[256,1664]{1,0:T(8,128)(2,1)S(1)}, bf16[256,1664]{1,0:T(8,128)(2,1)S(1)}, u32[]{:S(2)}, u32[]{:S(2)}) collective-permute-start(bf16[256,1664]{1,0:T(8,128)(2,1)S(1)} %pad_maximum_fusion.10), channel_id=1, source_target_pairs={{0,2},{1,3},{2,0},{3,1},{4,6},{5,7},{6,4},{7,5},{8,10},{9,11},{10,... | collective-permute-start | bytes 2555912 | tf_op jit(solution)/shard_map/ppermute | solution.py:409
  188.7 78.6 %collective-permute-start.33 = (bf16[2048,1664]{1,0:T(8,128)(2,1)}, bf16[2048,1664]{1,0:T(8,128)(2,1)}, u32[]{:S(2)}, u32[]{:S(2)}) collective-permute-start(bf16[2048,1664]{1,0:T(8,128)(2,1)} %get-tuple-element.395), channel_id=1, source_target_pairs={{0,1},{1,0},{2,3},{3,2},{4,5},{5,4},{6,7},{7,6},{8,9},{9,8},{10,11... | collective-permute-start | bytes 20447240 | tf_op jit(solution)/shard_map/ppermute | solution.py:409
  188.8 93.6 %all-to-all-start.1 = ((bf16[8,192,1280]{2,1,0:T(8,128)(2,1)}), bf16[8,192,1280]{2,1,0:T(8,128)(2,1)}, u32[]{:S(2)}, u32[]{:S(2)}) async-start(bf16[8,192,1280]{2,1,0:T(8,128)(2,1)} %pack_weights.1), calls=%async_computation.1 | async-start | bytes 7864320 | tf_op jit(solution)/shard_map/all_to_all | solution.py:1007
  198.3 37.3 %collective-permute-start.32 = (bf16[128,1536]{1,0:T(8,128)(2,1)}, bf16[128,1536]{1,0:T(8,128)(2,1)S(1)}, u32[]{:S(2)}, u32[]{:S(2)}) collective-permute-start(bf16[128,1536]{1,0:T(8,128)(2,1)} %get-tuple-element.377), channel_id=1, source_target_pairs={{0,4},{4,0},{8,12},{12,8},{16,20},{20,16},{24,28},{28,24},{1,5},{5... | collective-permute-start | bytes 1179656 | tf_op jit(solution)/shard_map/ppermute | solution.py:405
  201.4 34.2 %collective-permute-start.31 = (bf16[128,1536]{1,0:T(8,128)(2,1)S(1)}, bf16[128,1536]{1,0:T(8,128)(2,1)S(1)}, u32[]{:S(2)}, u32[]{:S(2)}) collective-permute-start(bf16[128,1536]{1,0:T(8,128)(2,1)S(1)} %add_convert_fusion.31), channel_id=1, source_target_pairs={{8,16},{12,20},{16,8},{20,12},{9,17},{13,21},{17,9},{21,13},{10,18... | collective-permute-start | bytes 1179656 | tf_op jit(solution)/shard_map/ppermute | solution.py:405
  203.3 63.9 %collective-permute-start.30 = (bf16[128,1536]{1,0:T(8,128)(2,1)S(1)}, bf16[128,1536]{1,0:T(8,128)(2,1)S(1)}, u32[]{:S(2)}, u32[]{:S(2)}) collective-permute-start(bf16[128,1536]{1,0:T(8,128)(2,1)S(1)} %add_convert_fusion.32), channel_id=1, source_target_pairs={{0,8},{4,12},{8,0},{12,4},{16,24},{20,28},{24,16},{28,20},{1,9},{5... | collective-permute-start | bytes 1179656 | tf_op jit(solution)/shard_map/ppermute | solution.py:405
  282.4 30.5 %collective-permute-start.34 = (bf16[128,1536]{1,0:T(8,128)(2,1)S(1)}, bf16[128,1536]{1,0:T(8,128)(2,1)S(1)}, u32[]{:S(2)}, u32[]{:S(2)}) collective-permute-start(bf16[128,1536]{1,0:T(8,128)(2,1)S(1)} %multiply_convert_fusion.9), channel_id=1, source_target_pairs={{0,8},{4,12},{8,0},{12,4},{16,24},{20,28},{24,16},{28,20},{1,9},{5... | collective-permute-start | bytes 1179656 | tf_op jit(solution)/shard_map/ppermute | solution.py:405
  312.8 20.2 %collective-permute-start.36 = (bf16[128,1536]{1,0:T(8,128)(2,1)S(1)}, bf16[128,1536]{1,0:T(8,128)(2,1)S(1)}, u32[]{:S(2)}, u32[]{:S(2)}) collective-permute-start(bf16[128,1536]{1,0:T(8,128)(2,1)S(1)} %collective-permute-done.34), channel_id=1, source_target_pairs={{8,16},{12,20},{16,8},{20,12},{9,17},{13,21},{17,9},{21,13},{10,18... | collective-permute-start | bytes 1179656 | tf_op jit(solution)/shard_map/ppermute | solution.py:405
  314.3 18.7 %collective-permute-start.39 = (bf16[128,1536]{1,0:T(8,128)(2,1)S(1)}, bf16[128,1536]{1,0:T(8,128)(2,1)S(1)}, u32[]{:S(2)}, u32[]{:S(2)}) collective-permute-start(bf16[128,1536]{1,0:T(8,128)(2,1)S(1)} %pad_maximum_fusion.17), channel_id=1, source_target_pairs={{0,2},{1,3},{2,0},{3,1},{4,6},{5,7},{6,4},{7,5},{8,10},{9,11},{10,... | collective-permute-start | bytes 1179656 | tf_op jit(solution)/shard_map/ppermute | solution.py:409
  314.9 18.1 %collective-permute-start.38 = (bf16[128,1536]{1,0:T(8,128)(2,1)S(1)}, bf16[128,1536]{1,0:T(8,128)(2,1)S(1)}, u32[]{:S(2)}, u32[]{:S(2)}) collective-permute-start(bf16[128,1536]{1,0:T(8,128)(2,1)S(1)} %pad_maximum_fusion.16), channel_id=1, source_target_pairs={{0,4},{4,0},{8,12},{12,8},{16,20},{20,16},{24,28},{28,24},{1,5},{5... | collective-permute-start | bytes 1179656 | tf_op jit(solution)/shard_map/ppermute | solution.py:405
  316.4 16.6 %collective-permute-start.37 = (bf16[128,1536]{1,0:T(8,128)(2,1)S(1)}, bf16[128,1536]{1,0:T(8,128)(2,1)S(1)}, u32[]{:S(2)}, u32[]{:S(2)}) collective-permute-start(bf16[128,1536]{1,0:T(8,128)(2,1)S(1)} %collective-permute-done.35), channel_id=1, source_target_pairs={{8,0},{12,4},{16,24},{20,28},{9,1},{13,5},{17,25},{21,29},{10,2},{... | collective-permute-start | bytes 1179656 | tf_op jit(solution)/shard_map/ppermute | solution.py:405
  333.2 18.3 %collective-permute-start.42 = (bf16[256,1536]{1,0:T(8,128)(2,1)S(1)}, bf16[256,1536]{1,0:T(8,128)(2,1)S(1)}, u32[]{:S(2)}, u32[]{:S(2)}) collective-permute-start(bf16[256,1536]{1,0:T(8,128)(2,1)S(1)} %pad_maximum_fusion.12), channel_id=1, source_target_pairs={{0,4},{4,0},{8,12},{12,8},{16,20},{20,16},{24,28},{28,24},{1,5},{5... | collective-permute-start | bytes 2359304 | tf_op jit(solution)/shard_map/ppermute | solution.py:405
  333.8 18.0 %collective-permute-start.41 = (bf16[256,1536]{1,0:T(8,128)(2,1)S(1)}, bf16[256,1536]{1,0:T(8,128)(2,1)S(1)}, u32[]{:S(2)}, u32[]{:S(2)}) collective-permute-start(bf16[256,1536]{1,0:T(8,128)(2,1)S(1)} %pad_maximum_fusion.11), channel_id=1, source_target_pairs={{0,2},{1,3},{2,0},{3,1},{4,6},{5,7},{6,4},{7,5},{8,10},{9,11},{10,... | collective-permute-start | bytes 2359304 | tf_op jit(solution)/shard_map/ppermute | solution.py:409
  370.9 19.1 %collective-permute-start.47 = (bf16[256,1536]{1,0:T(8,128)(2,1)S(1)}, bf16[256,1536]{1,0:T(8,128)(2,1)S(1)}, u32[]{:S(2)}, u32[]{:S(2)}) collective-permute-start(bf16[256,1536]{1,0:T(8,128)(2,1)S(1)} %pad_maximum_fusion.14), channel_id=1, source_target_pairs={{0,4},{4,0},{8,12},{12,8},{16,20},{20,16},{24,28},{28,24},{1,5},{5... | collective-permute-start | bytes 2359304 | tf_op jit(solution)/shard_map/ppermute | solution.py:405
  372.4 18.5 %collective-permute-start.46 = (bf16[256,1536]{1,0:T(8,128)(2,1)S(1)}, bf16[256,1536]{1,0:T(8,128)(2,1)S(1)}, u32[]{:S(2)}, u32[]{:S(2)}) collective-permute-start(bf16[256,1536]{1,0:T(8,128)(2,1)S(1)} %pad_maximum_fusion.13), channel_id=1, source_target_pairs={{0,2},{1,3},{2,0},{3,1},{4,6},{5,7},{6,4},{7,5},{8,10},{9,11},{10,... | collective-permute-start | bytes 2359304 | tf_op jit(solution)/shard_map/ppermute | solution.py:409
  395.9 23.3 %collective-permute-start.48 = (bf16[1024,1536]{1,0:T(8,128)(2,1)}, bf16[1024,1536]{1,0:T(8,128)(2,1)S(1)}, u32[]{:S(2)}, u32[]{:S(2)}) collective-permute-start(bf16[1024,1536]{1,0:T(8,128)(2,1)} %get-tuple-element.402), channel_id=1, source_target_pairs={{0,1},{1,0},{2,3},{3,2},{4,5},{5,4},{6,7},{7,6},{8,9},{9,8},{10,11... | collective-permute-start | bytes 9437192 | tf_op jit(solution)/shard_map/ppermute | solution.py:409
  455.6 18.9 %collective-permute-start.49 = (bf16[1024,1536]{1,0:T(8,128)(2,1)S(1)}, bf16[1024,1536]{1,0:T(8,128)(2,1)}, u32[]{:S(2)}, u32[]{:S(2)}) collective-permute-start(bf16[1024,1536]{1,0:T(8,128)(2,1)S(1)} %slice.465), channel_id=1, source_target_pairs={{0,1},{1,0},{2,3},{3,2},{4,5},{5,4},{6,7},{7,6},{8,9},{9,8},{10,11... | collective-permute-start | bytes 9437192 | tf_op jit(solution)/shard_map/ppermute | solution.py:409
  456.4 31.5 %collective-permute-start.52 = (bf16[1024,1536]{1,0:T(8,128)(2,1)S(1)}, bf16[1024,1536]{1,0:T(8,128)(2,1)S(1)}, u32[]{:S(2)}, u32[]{:S(2)}) collective-permute-start(bf16[1024,1536]{1,0:T(8,128)(2,1)S(1)} %slice.389), channel_id=1, source_target_pairs={{0,1},{1,0},{2,3},{3,2},{4,5},{5,4},{6,7},{7,6},{8,9},{9,8},{10,11... | collective-permute-start | bytes 9437192 | tf_op jit(solution)/shard_map/ppermute | solution.py:409
  479.7 20.1 %collective-permute-start.50 = (bf16[256,1536]{1,0:T(8,128)(2,1)S(1)}, bf16[256,1536]{1,0:T(8,128)(2,1)S(1)}, u32[]{:S(2)}, u32[]{:S(2)}) collective-permute-start(bf16[256,1536]{1,0:T(8,128)(2,1)S(1)} %get-tuple-element.376), channel_id=1, source_target_pairs={{0,2},{1,3},{2,0},{3,1},{4,6},{5,7},{6,4},{7,5},{8,10},{9,11},{10,... | collective-permute-start | bytes 2359304 | tf_op jit(solution)/shard_map/ppermute | solution.py:409
  480.3 20.4 %collective-permute-start.51 = (bf16[256,1536]{1,0:T(8,128)(2,1)S(1)}, bf16[256,1536]{1,0:T(8,128)(2,1)}, u32[]{:S(2)}, u32[]{:S(2)}) collective-permute-start(bf16[256,1536]{1,0:T(8,128)(2,1)S(1)} %get-tuple-element.375), channel_id=1, source_target_pairs={{0,4},{4,0},{8,12},{12,8},{16,20},{20,16},{24,28},{28,24},{1,5},{5... | collective-permute-start | bytes 2359304 | tf_op jit(solution)/shard_map/ppermute | solution.py:405
  504.5 28.1 %collective-permute-start.55 = (bf16[256,1536]{1,0:T(8,128)(2,1)}, bf16[256,1536]{1,0:T(8,128)(2,1)S(1)}, u32[]{:S(2)}, u32[]{:S(2)}) collective-permute-start(bf16[256,1536]{1,0:T(8,128)(2,1)} %get-tuple-element.372), channel_id=1, source_target_pairs={{0,2},{1,3},{2,0},{3,1},{4,6},{5,7},{6,4},{7,5},{8,10},{9,11},{10,... | collective-permute-start | bytes 2359304 | tf_op jit(solution)/shard_map/ppermute | solution.py:409
  505.5 27.2 %collective-permute-start.56 = (bf16[256,1536]{1,0:T(8,128)(2,1)S(1)}, bf16[256,1536]{1,0:T(8,128)(2,1)S(1)}, u32[]{:S(2)}, u32[]{:S(2)}) collective-permute-start(bf16[256,1536]{1,0:T(8,128)(2,1)S(1)} %get-tuple-element.371), channel_id=1, source_target_pairs={{0,4},{4,0},{8,12},{12,8},{16,20},{20,16},{24,28},{28,24},{1,5},{5... | collective-permute-start | bytes 2359304 | tf_op jit(solution)/shard_map/ppermute | solution.py:405
  507.6 25.0 %collective-permute-start.53 = (bf16[128,1536]{1,0:T(8,128)(2,1)S(1)}, bf16[128,1536]{1,0:T(8,128)(2,1)}, u32[]{:S(2)}, u32[]{:S(2)}) collective-permute-start(bf16[128,1536]{1,0:T(8,128)(2,1)S(1)} %slice.471), channel_id=1, source_target_pairs={{0,4},{4,0},{8,12},{12,8},{16,20},{20,16},{24,28},{28,24},{1,5},{5... | collective-permute-start | bytes 1179656 | tf_op jit(solution)/shard_map/ppermute | solution.py:405
  509.2 23.5 %collective-permute-start.54 = (bf16[128,1536]{1,0:T(8,128)(2,1)S(1)}, bf16[128,1536]{1,0:T(8,128)(2,1)S(1)}, u32[]{:S(2)}, u32[]{:S(2)}) collective-permute-start(bf16[128,1536]{1,0:T(8,128)(2,1)S(1)} %slice.473), channel_id=1, source_target_pairs={{0,2},{1,3},{2,0},{3,1},{4,6},{5,7},{6,4},{7,5},{8,10},{9,11},{10,... | collective-permute-start | bytes 1179656 | tf_op jit(solution)/shard_map/ppermute | solution.py:409
  526.2 40.3 %collective-permute-start.60 = (bf16[1024,1536]{1,0:T(8,128)(2,1)}, bf16[1024,1536]{1,0:T(8,128)(2,1)}, u32[]{:S(2)}, u32[]{:S(2)}) collective-permute-start(bf16[1024,1536]{1,0:T(8,128)(2,1)} %slice.404), channel_id=1, source_target_pairs={{0,1},{1,0},{2,3},{3,2},{4,5},{5,4},{6,7},{7,6},{8,9},{9,8},{10,11... | collective-permute-start | bytes 9437192 | tf_op jit(solution)/shard_map/ppermute | solution.py:409
  536.6 28.4 %collective-permute-start.59 = (bf16[128,1536]{1,0:T(8,128)(2,1)}, bf16[128,1536]{1,0:T(8,128)(2,1)}, u32[]{:S(2)}, u32[]{:S(2)}) collective-permute-start(bf16[128,1536]{1,0:T(8,128)(2,1)} %pad_maximum_fusion.20), channel_id=1, source_target_pairs={{0,8},{4,12},{24,16},{28,20},{1,9},{5,13},{25,17},{29,21},{2,10},{... | collective-permute-start | bytes 1179656 | tf_op jit(solution)/shard_map/ppermute | solution.py:405
  545.1 21.4 %collective-permute-start.57 = (bf16[128,1536]{1,0:T(8,128)(2,1)}, bf16[128,1536]{1,0:T(8,128)(2,1)}, u32[]{:S(2)}, u32[]{:S(2)}) collective-permute-start(bf16[128,1536]{1,0:T(8,128)(2,1)} %slice.480), channel_id=1, source_target_pairs={{0,4},{4,0},{8,12},{12,8},{16,20},{20,16},{24,28},{28,24},{1,5},{5... | collective-permute-start | bytes 1179656 | tf_op jit(solution)/shard_map/ppermute | solution.py:405
  546.5 20.1 %collective-permute-start.58 = (bf16[128,1536]{1,0:T(8,128)(2,1)}, bf16[128,1536]{1,0:T(8,128)(2,1)}, u32[]{:S(2)}, u32[]{:S(2)}) collective-permute-start(bf16[128,1536]{1,0:T(8,128)(2,1)} %slice.482), channel_id=1, source_target_pairs={{0,2},{1,3},{2,0},{3,1},{4,6},{5,7},{6,4},{7,5},{8,10},{9,11},{10,... | collective-permute-start | bytes 1179656 | tf_op jit(solution)/shard_map/ppermute | solution.py:409
  558.9 18.0 %collective-permute-start.65 = (bf16[1024,1536]{1,0:T(8,128)(2,1)}, bf16[1024,1536]{1,0:T(8,128)(2,1)}, u32[]{:S(2)}, u32[]{:S(2)}) collective-permute-start(bf16[1024,1536]{1,0:T(8,128)(2,1)} %slice.411), channel_id=1, source_target_pairs={{0,1},{1,0},{2,3},{3,2},{4,5},{5,4},{6,7},{7,6},{8,9},{9,8},{10,11... | collective-permute-start | bytes 9437192 | tf_op jit(solution)/shard_map/ppermute | solution.py:409
  570.7 20.0 %collective-permute-start.63 = (bf16[256,1536]{1,0:T(8,128)(2,1)S(1)}, bf16[256,1536]{1,0:T(8,128)(2,1)S(1)}, u32[]{:S(2)}, u32[]{:S(2)}) collective-permute-start(bf16[256,1536]{1,0:T(8,128)(2,1)S(1)} %get-tuple-element.368), channel_id=1, source_target_pairs={{0,2},{1,3},{2,0},{3,1},{4,6},{5,7},{6,4},{7,5},{8,10},{9,11},{10,... | collective-permute-start | bytes 2359304 | tf_op jit(solution)/shard_map/ppermute | solution.py:409
  571.4 19.7 %collective-permute-start.64 = (bf16[256,1536]{1,0:T(8,128)(2,1)S(1)}, bf16[256,1536]{1,0:T(8,128)(2,1)S(1)}, u32[]{:S(2)}, u32[]{:S(2)}) collective-permute-start(bf16[256,1536]{1,0:T(8,128)(2,1)S(1)} %get-tuple-element.367), channel_id=1, source_target_pairs={{0,4},{4,0},{8,12},{12,8},{16,20},{20,16},{24,28},{28,24},{1,5},{5... | collective-permute-start | bytes 2359304 | tf_op jit(solution)/shard_map/ppermute | solution.py:405
  593.9 37.8 %collective-permute-start.70 = (bf16[256,1536]{1,0:T(8,128)(2,1)S(1)}, bf16[256,1536]{1,0:T(8,128)(2,1)S(1)}, u32[]{:S(2)}, u32[]{:S(2)}) collective-permute-start(bf16[256,1536]{1,0:T(8,128)(2,1)S(1)} %get-tuple-element.364), channel_id=1, source_target_pairs={{0,2},{1,3},{2,0},{3,1},{4,6},{5,7},{6,4},{7,5},{8,10},{9,11},{10,... | collective-permute-start | bytes 2359304 | tf_op jit(solution)/shard_map/ppermute | solution.py:409
  595.4 36.3 %collective-permute-start.71 = (bf16[256,1536]{1,0:T(8,128)(2,1)S(1)}, bf16[256,1536]{1,0:T(8,128)(2,1)S(1)}, u32[]{:S(2)}, u32[]{:S(2)}) collective-permute-start(bf16[256,1536]{1,0:T(8,128)(2,1)S(1)} %get-tuple-element.363), channel_id=1, source_target_pairs={{0,4},{4,0},{8,12},{12,8},{16,20},{20,16},{24,28},{28,24},{1,5},{5... | collective-permute-start | bytes 2359304 | tf_op jit(solution)/shard_map/ppermute | solution.py:405
  597.3 25.1 %collective-permute-start.68 = (bf16[128,1536]{1,0:T(8,128)(2,1)S(1)}, bf16[128,1536]{1,0:T(8,128)(2,1)S(1)}, u32[]{:S(2)}, u32[]{:S(2)}) collective-permute-start(bf16[128,1536]{1,0:T(8,128)(2,1)S(1)} %slice.493), channel_id=1, source_target_pairs={{0,4},{4,0},{8,12},{12,8},{16,20},{20,16},{24,28},{28,24},{1,5},{5... | collective-permute-start | bytes 1179656 | tf_op jit(solution)/shard_map/ppermute | solution.py:405
  598.0 33.7 %collective-permute-start.69 = (bf16[128,1536]{1,0:T(8,128)(2,1)S(1)}, bf16[128,1536]{1,0:T(8,128)(2,1)S(1)}, u32[]{:S(2)}, u32[]{:S(2)}) collective-permute-start(bf16[128,1536]{1,0:T(8,128)(2,1)S(1)} %slice.495), channel_id=1, source_target_pairs={{0,2},{1,3},{2,0},{3,1},{4,6},{5,7},{6,4},{7,5},{8,10},{9,11},{10,... | collective-permute-start | bytes 1179656 | tf_op jit(solution)/shard_map/ppermute | solution.py:409
  598.7 33.0 %collective-permute-start.67 = (bf16[128,1536]{1,0:T(8,128)(2,1)S(1)}, bf16[128,1536]{1,0:T(8,128)(2,1)S(1)}, u32[]{:S(2)}, u32[]{:S(2)}) collective-permute-start(bf16[128,1536]{1,0:T(8,128)(2,1)S(1)} %add_convert_fusion.24), channel_id=1, source_target_pairs={{8,16},{12,20},{16,8},{20,12},{9,17},{13,21},{17,9},{21,13},{10,18... | collective-permute-start | bytes 1179656 | tf_op jit(solution)/shard_map/ppermute | solution.py:405
  634.5 18.4 %collective-permute-start.72 = (bf16[128,1536]{1,0:T(8,128)(2,1)S(1)}, bf16[128,1536]{1,0:T(8,128)(2,1)S(1)}, u32[]{:S(2)}, u32[]{:S(2)}) collective-permute-start(bf16[128,1536]{1,0:T(8,128)(2,1)S(1)} %get-tuple-element.343), channel_id=1, source_target_pairs={{0,8},{4,12},{8,0},{12,4},{16,24},{20,28},{24,16},{28,20},{1,9},{5... | collective-permute-start | bytes 1179656 | tf_op jit(solution)/shard_map/ppermute | solution.py:405
  677.4 18.2 %collective-permute-start.85 = (bf16[128,1536]{1,0:T(8,128)(2,1)S(1)}, bf16[128,1536]{1,0:T(8,128)(2,1)S(1)}, u32[]{:S(2)}, u32[]{:S(2)}) collective-permute-start(bf16[128,1536]{1,0:T(8,128)(2,1)S(1)} %add_convert_fusion.18), channel_id=1, source_target_pairs={{0,8},{4,12},{8,0},{12,4},{16,24},{20,28},{24,16},{28,20},{1,9},{5... | collective-permute-start | bytes 1179656 | tf_op jit(solution)/shard_map/ppermute | solution.py:405
  710.3 92.1 %all-to-all-start.3 = ((bf16[8,192,1280]{2,1,0:T(8,128)(2,1)}), bf16[8,192,1280]{2,1,0:T(8,128)(2,1)}, u32[]{:S(2)}, u32[]{:S(2)}) async-start(bf16[8,192,1280]{2,1,0:T(8,128)(2,1)} %bitcast.145), calls=%async_computation.3 | async-start | bytes 7864320 | tf_op jit(solution)/shard_map/all_to_all | solution.py:1203
  743.4 19.2 %collective-permute-start.88 = (bf16[128,1536]{1,0:T(8,128)(2,1)}, bf16[128,1536]{1,0:T(8,128)(2,1)}, u32[]{:S(2)}, u32[]{:S(2)}) collective-permute-start(bf16[128,1536]{1,0:T(8,128)(2,1)} %get-tuple-element.360), channel_id=1, source_target_pairs={{0,4},{4,0},{8,12},{12,8},{16,20},{20,16},{24,28},{28,24},{1,5},{5... | collective-permute-start | bytes 1179656 | tf_op jit(solution)/shard_map/ppermute | solution.py:405
  762.7 19.5 %collective-permute-start.91 = (bf16[2,8,48,640]{3,2,1,0:T(8,128)(2,1)S(1)}, bf16[2,8,48,640]{3,2,1,0:T(8,128)(2,1)S(1)}, u32[]{:S(2)}, u32[]{:S(2)}) collective-permute-start(bf16[2,8,48,640]{3,2,1,0:T(8,128)(2,1)S(1)} %pad_maximum_fusion.7), channel_id=1, source_target_pairs={{0,1},{1,0},{2,3},{3,2},{4,5},{5,4},{6,7},{7,6},{8,9},{9,8},{10,11... | collective-permute-start | bytes 2949128 | tf_op jit(solution)/shard_map/ppermute | solution.py:409
  762.8 15.9 %collective-permute-start.90 = (bf16[128,1536]{1,0:T(8,128)(2,1)S(1)}, bf16[128,1536]{1,0:T(8,128)(2,1)S(1)}, u32[]{:S(2)}, u32[]{:S(2)}) collective-permute-start(bf16[128,1536]{1,0:T(8,128)(2,1)S(1)} %copy-done.31), channel_id=1, source_target_pairs={{0,4},{4,0},{8,12},{12,8},{16,20},{20,16},{24,28},{28,24},{1,5},{5... | collective-permute-start | bytes 1179656 | tf_op jit(solution)/shard_map/ppermute | solution.py:405
  764.1 18.1 %collective-permute-start.89 = (bf16[128,1536]{1,0:T(8,128)(2,1)S(1)}, bf16[128,1536]{1,0:T(8,128)(2,1)S(1)}, u32[]{:S(2)}, u32[]{:S(2)}) collective-permute-start(bf16[128,1536]{1,0:T(8,128)(2,1)S(1)} %add_convert_fusion.16), channel_id=1, source_target_pairs={{0,8},{4,12},{24,16},{28,20},{1,9},{5,13},{25,17},{29,21},{2,10},{... | collective-permute-start | bytes 1179656 | tf_op jit(solution)/shard_map/ppermute | solution.py:405
  766.0 27.6 %collective-permute-start.94 = (bf16[128,1536]{1,0:T(8,128)(2,1)S(1)}, bf16[128,1536]{1,0:T(8,128)(2,1)S(1)}, u32[]{:S(2)}, u32[]{:S(2)}) collective-permute-start(bf16[128,1536]{1,0:T(8,128)(2,1)S(1)} %copy-done.30), channel_id=1, source_target_pairs={{0,4},{4,0},{8,12},{12,8},{16,20},{20,16},{24,28},{28,24},{1,5},{5... | collective-permute-start | bytes 1179656 | tf_op jit(solution)/shard_map/ppermute | solution.py:405
  791.8 35.3 %collective-permute-start.98 = (bf16[128,1536]{1,0:T(8,128)(2,1)S(1)}, bf16[128,1536]{1,0:T(8,128)(2,1)S(1)}, u32[]{:S(2)}, u32[]{:S(2)}) collective-permute-start(bf16[128,1536]{1,0:T(8,128)(2,1)S(1)} %copy-done.29), channel_id=1, source_target_pairs={{0,4},{4,0},{8,12},{12,8},{16,20},{20,16},{24,28},{28,24},{1,5},{5... | collective-permute-start | bytes 1179656 | tf_op jit(solution)/shard_map/ppermute | solution.py:405
  795.2 31.9 %collective-permute-start.97 = (bf16[128,1536]{1,0:T(8,128)(2,1)}, bf16[128,1536]{1,0:T(8,128)(2,1)S(1)}, u32[]{:S(2)}, u32[]{:S(2)}) collective-permute-start(bf16[128,1536]{1,0:T(8,128)(2,1)} %add_convert_fusion.12), channel_id=1, source_target_pairs={{8,16},{12,20},{16,8},{20,12},{9,17},{13,21},{17,9},{21,13},{10,18... | collective-permute-start | bytes 1179656 | tf_op jit(solution)/shard_map/ppermute | solution.py:405
  802.4 30.7 %all-to-all-start.2 = ((bf16[8,48,640]{2,1,0:T(8,128)(2,1)}), bf16[8,48,640]{2,1,0:T(8,128)(2,1)S(1)}, u32[]{:S(2)}, u32[]{:S(2)}) async-start(bf16[8,48,640]{2,1,0:T(8,128)(2,1)} %fusion.8), calls=%async_computation.2 | async-start | bytes 983040 | tf_op jit(solution)/shard_map/all_to_all | solution.py:1259
  816.8 16.4 %collective-permute-start.96 = (bf16[128,1536]{1,0:T(8,128)(2,1)}, bf16[128,1536]{1,0:T(8,128)(2,1)S(1)}, u32[]{:S(2)}, u32[]{:S(2)}) collective-permute-start(bf16[128,1536]{1,0:T(8,128)(2,1)} %add_convert_fusion.13), channel_id=1, source_target_pairs={{0,8},{4,12},{8,0},{12,4},{16,24},{20,28},{24,16},{28,20},{1,9},{5... | collective-permute-start | bytes 1179656 | tf_op jit(solution)/shard_map/ppermute | solution.py:405
  (109 other events, 1478.8 us)
